TPU v7x, 512 devices: a whole 4x8x8 slice. The times are simulated.
512 devices in a mesh: ep: 64 (over y, x, core), tp: 8 (over z).
Axes of the slice: x: 4, y: 8, z: 8, core: 2. Of those that a mesh axis runs over, the one named last changes fastest.
Arguments:
- tokens: bfloat16 [8192, 2048], P('ep', 'tp'), may hold values from -6 to 6
- cotangent: bfloat16 [8192, 2048], P('ep', 'tp'), may hold values from -6 to 6
- expert_ids: int32 [8192, 6], P('ep'), may hold values from 0 to 63, all different within a row; in each aligned block of 128 rows (0 to 127, 128 to 255, ...) at most 16 rows name the same one
- gate_values: float32 [8192, 6], P('ep'), may hold values from 0.1 to 1
- w_gate: bfloat16 [64, 1408, 2048], P('ep', 'tp'), may hold values from -0.125 to 0.125
- w_up: bfloat16 [64, 1408, 2048], P('ep', 'tp'), may hold values from -0.125 to 0.125
- w_down: bfloat16 [64, 1408, 2048], P('ep', 'tp'), may hold values from -0.15625 to 0.15625
Outputs:
- input_grad: bfloat16 [8192, 2048], P('ep', 'tp')
- grad_gate: bfloat16 [64, 1408, 2048], P('ep', 'tp')
- grad_up: bfloat16 [64, 1408, 2048], P('ep', 'tp')
- grad_down: bfloat16 [64, 1408, 2048], P('ep', 'tp')
Inputs may be any that keep to these rules, and one draw needn't show every extreme that they name: `expert_ids`: each token names 6 different experts. Among the 128 tokens of one group, no expert is named more than 16 times.
All inputs are finite; a program needn't handle non-finite values.
Results may differ from a plain program's by a relative error of at most 0.017.
Values may be sent and summed in bfloat16 or wider, within the bound.
No kernel may reach another device: no remote copies, remote signals or barrier semaphores. Data moves between devices by JAX's collectives and lax.ppermute only.
A program may use at most 64 MiB of HBM per device.

v0:
```python
import jax
import jax.numpy as jnp
from jax import lax
from jax.sharding import PartitionSpec as P


def sent_together(arrays, axis, split_dim, concat_dim, along):
    ends, at = ([], 0)
    for a in arrays[:-1]:
        at += a.shape[along]
        ends.append(at)
    both = jnp.concatenate(arrays, axis=along)
    return tuple(
        jnp.split(
            lax.all_to_all(both, axis, split_axis=split_dim, concat_axis=concat_dim, tiled=True),
            ends,
            axis=along,
        )
    )


def in_one_piece(arrays, axis, dim, along):
    widths = [a.shape[along] for a in arrays]
    both = jnp.concatenate(arrays, axis=along)
    filled = lax.all_gather(both, axis, axis=dim, tiled=True)
    return tuple(jnp.split(filled, [sum(widths[:k]) for k in range(1, len(widths))], axis=along))


def slot_numbers(flat_ids, experts):
    onehot = (flat_ids[:, None] == jnp.arange(experts, dtype=jnp.int32)[None, :]).astype(jnp.int32)
    before = jnp.cumsum(onehot, axis=0) - onehot
    return jnp.sum(before * onehot, axis=1)


def pair_table(expert_ids, experts, capacity):
    flat_ids = expert_ids.reshape(-1)
    position = flat_ids * capacity + slot_numbers(flat_ids, experts)
    matches = position[None, :] == jnp.arange(experts * capacity, dtype=jnp.int32)[:, None]
    usable = jnp.any(matches, axis=1)
    numbers = jnp.arange(flat_ids.shape[0], dtype=jnp.int32)[None, :]
    pair_index = jnp.sum(jnp.where(matches, numbers, 0), axis=1)
    return (pair_index, usable, position)


def dispatch_rows(features, cotangent, gate_values, pair_index, usable, top_count):
    token_index = pair_index // top_count
    feature_rows = jnp.where(usable[:, None], features[token_index], jnp.zeros((), features.dtype))
    scaled = gate_values.reshape(-1)[pair_index][:, None] * cotangent[token_index].astype(
        jnp.float32
    )
    cotangent_rows = jnp.where(usable[:, None], scaled, jnp.zeros((), jnp.float32)).astype(
        jnp.bfloat16
    )
    return (feature_rows, cotangent_rows)


def contract_rows(left, right):
    return lax.dot_general(
        left, right, (((0,), (0,)), ((), ())), preferred_element_type=jnp.float32
    )


def contract_width(left, right):
    return lax.dot_general(
        left, right, (((1,), (1,)), ((), ())), preferred_element_type=jnp.float32
    )


def local(tokens, cotangent, expert_ids, gate_values, w_gate, w_up, w_down):
    group_count = lax.axis_size("ep")
    tok_count, top_count = expert_ids.shape
    capacity = max(2, tok_count * top_count * 4 // (group_count * 3))
    pair_index, usable, position = pair_table(expert_ids, group_count, capacity)
    feature_rows, cotangent_rows = dispatch_rows(
        tokens, cotangent, gate_values, pair_index, usable, top_count
    )
    slice_width = feature_rows.shape[1]
    feature_rows, cotangent_rows = sent_together(
        (
            feature_rows.reshape(group_count, capacity, slice_width),
            cotangent_rows.reshape(group_count, capacity, slice_width),
        ),
        "ep",
        0,
        0,
        1,
    )
    feature_rows, cotangent_rows = in_one_piece((feature_rows, cotangent_rows), "tp", 2, 0)
    model_width = feature_rows.shape[2]
    row_count = group_count * capacity
    expert_inputs = feature_rows.reshape(row_count, model_width)
    expert_cotangent = cotangent_rows.reshape(row_count, model_width)
    gate_weight = w_gate[0]
    up_weight = w_up[0]
    down_weight = w_down[0]
    gate_pre = contract_width(expert_inputs, gate_weight)
    up_proj = contract_width(expert_inputs, up_weight)
    sigmoid_gate = jax.nn.sigmoid(gate_pre)
    swish_value = gate_pre * sigmoid_gate
    hidden = (swish_value * up_proj).astype(jnp.bfloat16)
    hidden_grad = contract_width(expert_cotangent, down_weight)
    gate_grad = (
        hidden_grad * up_proj * sigmoid_gate * (1.0 + gate_pre * (1.0 - sigmoid_gate))
    ).astype(jnp.bfloat16)
    up_grad = (hidden_grad * swish_value).astype(jnp.bfloat16)
    grad_gate = contract_rows(gate_grad, expert_inputs).astype(jnp.bfloat16)
    grad_up = contract_rows(up_grad, expert_inputs).astype(jnp.bfloat16)
    grad_down = contract_rows(hidden, expert_cotangent).astype(jnp.bfloat16)
    input_terms = jnp.dot(gate_grad, gate_weight, preferred_element_type=jnp.float32)
    input_terms = input_terms + jnp.dot(up_grad, up_weight, preferred_element_type=jnp.float32)
    summed = lax.psum_scatter(
        input_terms.astype(jnp.bfloat16), "tp", scatter_dimension=1, tiled=True
    )
    returned = summed.reshape(group_count, capacity, -1)
    returned = lax.all_to_all(returned, "ep", split_axis=0, concat_axis=0, tiled=True)
    returned = returned.reshape(row_count, -1)
    picked = jnp.take(returned, position, axis=0).astype(jnp.float32)
    input_grad = jnp.sum(picked.reshape(tok_count, top_count, -1), axis=1).astype(jnp.bfloat16)
    return (input_grad, grad_gate[None], grad_up[None], grad_down[None])


def solution(mesh):
    in_specs = (
        P("ep", "tp"),
        P("ep", "tp"),
        P("ep", None),
        P("ep", None),
        P("ep", "tp", None),
        P("ep", "tp", None),
        P("ep", "tp", None),
    )
    out_specs = (P("ep", "tp"), P("ep", "tp", None), P("ep", "tp", None), P("ep", "tp", None))
    return jax.shard_map(local, mesh=mesh, in_specs=in_specs, out_specs=out_specs, check_vma=False)
```

profile of v0, /device:TPU:1, one launch (start us, length us, event | category | flops | bytes accessed | tf_op | source)
XLA Modules:
  0.0 280.5 jit_solution(12960853965099221193)
XLA Ops:
  7.2 0.0 copy-start
  7.2 0.0 all-gather.2.cloned.1.call-start
  7.2 0.9 copy.22
  8.1 0.1 eq.39
  8.2 0.1 reshape.165
  8.4 1.8 reduce-window.6
  10.2 0.3 slice_reduce_fusion
  10.5 0.1 fusion.18
  10.7 0.4 select_reduce_fusion
  11.0 0.4 fusion
  11.5 0.8 copy.27
  12.3 0.1 reshape.167
  12.5 4.5 %gather_fusion.1 = f32[1024]{0:T(1024)S(1)} fusion(f32[768]{0:T(1024)S(1)} %reshape.167, s32[1024]{0:T(1024)S(1)} %broadcast_clamp_fusion), kind=kCustom, calls=%fused_computation.1 | custom fusion | bytes 12288 | tf_op jit(solution)/shard_map/gather | solution.py:48
  17.0 0.1 mul.67
  17.1 0.1 broadcast_in_dim.66
  17.2 3.9 %gather_fusion.2 = bf16[1024,256]{1,0:T(8,128)(2,1)S(1)} fusion(bf16[128,256]{1,0:T(8,128)(2,1)S(1)} %copy-done.1, s32[1024]{0:T(1024)S(1)} %broadcast_clamp_fusion.1), kind=kCustom, calls=%fused_computation.2 | custom fusion | bytes 1052672 | tf_op jit(solution)/shard_map/gather | solution.py:48
  21.1 3.9 %gather_fusion = bf16[1024,256]{1,0:T(8,128)(2,1)S(1)} fusion(bf16[128,256]{1,0:T(8,128)(2,1)S(1)} %copy-done.2, s32[1024]{0:T(1024)S(1)} %broadcast_clamp_fusion.1), kind=kCustom, calls=%fused_computation | custom fusion | bytes 1052672 | tf_op jit(solution)/shard_map/gather | solution.py:47
  25.1 0.2 broadcast_select_fusion
  25.3 0.3 fusion.5
  25.7 0.1 pad_maximum_fusion
  25.8 39.4 %all_to_all.10 = bf16[64,32,256]{2,1,0:T(8,128)(2,1)S(1)} all-to-all(bf16[64,32,256]{2,1,0:T(8,128)(2,1)S(1)} %pad_maximum_fusion), channel_id=1, replica_groups=mesh['ep'=64,'tp'=8] {'ep'}, dimensions={0} | all-to-all | bytes 2097152 | tf_op jit(solution)/shard_map/all_to_all | solution.py:15
  65.2 0.1 fusion.24
  65.3 1.2 pad_maximum_fusion.1
  66.4 0.0 all-gather.2.cloned.1.call-update
  66.5 0.0 reduce-scatter.2.cloned.1.call-start
  66.5 101.6 %all-gather.2.cloned.1.call-done = bf16[128,16,2048]{2,1,0:T(8,128)(2,1)} async-done(((bf16[128,16,256]{2,1,0:T(8,128)(2,1)}), bf16[128,16,2048]{2,1,0:T(8,128)(2,1)}) %all-gather.2.cloned.1.call-update) | async-done | bytes 8388624 | tf_op jit(solution)/shard_map/all_gather | solution.py:25
  168.2 4.0 %fusion.23 = (bf16[64,16,2048]{2,1,0:T(8,128)(2,1)S(1)}, bf16[64,16,2048]{2,1,0:T(8,128)(2,1)S(1)}) fusion(bf16[128,16,2048]{2,1,0:T(8,128)(2,1)} %all-gather.2.cloned.1.call-done), kind=kLoop, calls=%fused_computation.57 | loop fusion | bytes 16777216 | tf_op jit(solution)/shard_map/split | solution.py:26
  172.2 1.6 fusion.11
  173.8 1.6 fusion.8
  175.4 1.7 multiply_convert_fusion.1
  177.1 1.3 fusion.6
  178.4 3.3 %add_convert_fusion = bf16[1024,2048]{1,0:T(8,128)(2,1)} fusion(f32[1024,2048]{1,0:T(8,128)S(1)} %fusion.6, bf16[1024,176]{0,1:T(8,128)(2,1)S(1)} %get-tuple-element.6, bf16[1,176,2048]{2,1,0:T(8,128)(2,1)S(1)} %copy-done.7), kind=kOutput, calls=%fused_computation.4 | convolution fusion | flops 742391808 | bytes 13664256 | tf_op jit(solution)/shard_map/dot_general | solution.py:110
  181.7 0.0 reduce-scatter.2.cloned.1.call-update
  181.8 0.1 reduce_sum.37
  181.9 0.5 copy-done.8
  182.4 0.1 copy.28
  182.5 0.1 mul.76
  182.7 0.1 copy.25
  182.8 0.1 copy.26
  183.0 58.8 %reduce-scatter.2.cloned.1.call-done = bf16[1024,256]{1,0:T(8,128)(2,1)} async-done(((bf16[1024,2048]{1,0:T(8,128)(2,1)}), bf16[1024,256]{1,0:T(8,128)(2,1)}) %reduce-scatter.2.cloned.1.call-update) | async-done | bytes 524304 | tf_op jit(solution)/shard_map/reduce_scatter | solution.py:111
  241.7 10.3 %all-to-all-start.1 = ((bf16[64,16,256]{2,1,0:T(8,128)(2,1)}), bf16[64,16,256]{2,1,0:T(8,128)(2,1)S(1)}, u32[]{:S(2)}, u32[]{:S(2)}) async-start(bf16[64,16,256]{2,1,0:T(8,128)(2,1)} %bitcast.70), calls=%async_computation.2 | async-start | bytes 1048576 | tf_op jit(solution)/shard_map/all_to_all | solution.py:115
  252.1 4.1 %fusion.2 = bf16[1,176,2048]{2,1,0:T(8,128)(2,1)} fusion(bf16[1024,176]{0,1:T(8,128)(2,1)S(1)} %get-tuple-element.6, bf16[1024,2048]{1,0:T(8,128)(2,1)} %bitcast.63), kind=kOutput, calls=%fused_computation.12 | convolution fusion | flops 738557952 | bytes 5275648 | tf_op jit(solution)/shard_map/dot_general | solution.py:58
  256.2 1.8 fusion.1
  258.1 1.9 fusion.3
  259.9 9.9 %all-to-all-done.1 = bf16[64,16,256]{2,1,0:T(8,128)(2,1)S(1)} async-done(((bf16[64,16,256]{2,1,0:T(8,128)(2,1)}), bf16[64,16,256]{2,1,0:T(8,128)(2,1)S(1)}, u32[]{:S(2)}, u32[]{:S(2)}) %all-to-all-start.1) | async-done | bytes 524320 | tf_op jit(solution)/shard_map/all_to_all | solution.py:115
  269.8 2.6 gather_fusion.3
  272.5 0.1 gather.22
  272.6 1.0 select_reduce_fusion.1
  (32 shorter events, 0.2 us)
Async XLA Ops:
  7.2 166.6 %copy-start = (bf16[1,176,2048]{2,1,0:T(8,128)(2,1)S(1)}, bf16[1,176,2048]{2,1,0:T(8,128)(2,1)}, u32[]{:S(2)}) copy-start(bf16[1,176,2048]{2,1,0:T(8,128)(2,1)} %param.11) | copy-start | bytes 2162692
  7.2 10.0 %copy-start.1 = (bf16[128,256]{1,0:T(8,128)(2,1)S(1)}, bf16[128,256]{1,0:T(8,128)(2,1)}, u32[]{:S(2)}) copy-start(bf16[128,256]{1,0:T(8,128)(2,1)} %param.8) | copy-start | bytes 196612
  7.2 161.0 %all-gather.2.cloned.1.call-start = ((), (), s32[]{:S(2)}) async-start(), calls=%async_computation.3 | async-start | bytes 9437184 | tf_op jit(solution)/shard_map/all_gather | solution.py:25
  12.5 8.7 %copy-start.2 = (bf16[128,256]{1,0:T(8,128)(2,1)S(1)}, bf16[128,256]{1,0:T(8,128)(2,1)}, u32[]{:S(2)}) copy-start(bf16[128,256]{1,0:T(8,128)(2,1)} %param.7) | copy-start | bytes 196612
  66.5 105.7 %copy-start.7 = (bf16[1,176,2048]{2,1,0:T(8,128)(2,1)S(1)}, bf16[1,176,2048]{2,1,0:T(8,128)(2,1)}, u32[]{:S(2)}) copy-start(bf16[1,176,2048]{2,1,0:T(8,128)(2,1)} %param.12) | copy-start | bytes 2162692
  66.5 175.3 %reduce-scatter.2.cloned.1.call-start = ((), (), s32[]{:S(2)}) async-start(), calls=%async_computation.4 | async-start | bytes 4718592 | tf_op jit(solution)/shard_map/reduce_scatter | solution.py:111
  172.2 3.2 %copy-start.3 = (bf16[64,16,2048]{2,1,0:T(8,128)(2,1)}, bf16[64,16,2048]{2,1,0:T(8,128)(2,1)S(1)}, u32[]{:S(2)}) copy-start(bf16[64,16,2048]{2,1,0:T(8,128)(2,1)S(1)} %get-tuple-element.5) | copy-start | bytes 12582916
  172.2 3.2 %copy-start.5 = (bf16[64,16,2048]{2,1,0:T(8,128)(2,1)}, bf16[64,16,2048]{2,1,0:T(8,128)(2,1)S(1)}, u32[]{:S(2)}) copy-start(bf16[64,16,2048]{2,1,0:T(8,128)(2,1)S(1)} %get-tuple-element.4) | copy-start | bytes 12582916
  173.8 1.6 copy-start.9
  175.4 1.7 copy-start.10
  181.7 0.7 copy-start.8
  241.7 28.1 %all-to-all-start.1 = ((bf16[64,16,256]{2,1,0:T(8,128)(2,1)}), bf16[64,16,256]{2,1,0:T(8,128)(2,1)S(1)}, u32[]{:S(2)}, u32[]{:S(2)}) async-start(bf16[64,16,256]{2,1,0:T(8,128)(2,1)} %bitcast.70), calls=%async_computation.2 | async-start | bytes 1048576 | tf_op jit(solution)/shard_map/all_to_all | solution.py:115
  252.1 4.2 %copy-start.4 = (bf16[64,16,2048]{2,1,0:T(8,128)(2,1)S(1)}, bf16[64,16,2048]{2,1,0:T(8,128)(2,1)}, u32[]{:S(2)}) copy-start(bf16[64,16,2048]{2,1,0:T(8,128)(2,1)} %copy-done.3) | copy-start | bytes 12582916
  252.1 6.0 %copy-start.6 = (bf16[64,16,2048]{2,1,0:T(8,128)(2,1)S(1)}, bf16[64,16,2048]{2,1,0:T(8,128)(2,1)}, u32[]{:S(2)}) copy-start(bf16[64,16,2048]{2,1,0:T(8,128)(2,1)} %copy-done.5) | copy-start | bytes 12582916
  252.1 6.0 %copy-start.11 = (f32[1024,176]{0,1:T(8,128)S(1)}, f32[1024,176]{0,1:T(8,128)}, u32[]{:S(2)}) copy-start(f32[1024,176]{0,1:T(8,128)} %copy-done.10) | copy-start | bytes 2162692
Sparse Core Ops, SparseCore 0:
  66.6 101.5 all-gather.1
  181.9 59.8 reduce-scatter.1
where the time goes:
time: 281 us; the launch traced here: 280 us
  waiting for transfers between devices  170 us (60%)
  blocking collectives  39.4 us (14%)
  local copies, waits for them, and re-layouts  22.9 us (8%)
  matrix products  17.2 us (6%)
  between operations  14.4 us (5%)
  starting transfers between devices  10.4 us (4%)
  other arithmetic  5.74 us (2%)
    all_gather x1, waiting for transfers between devices, in_one_piece(): filled = lax.all_gather(both, axis, axis=dim, tiled=True)  102 us
    reduce_scatter x1, waiting for transfers between devices, local(): lax.psum_scatter(input_terms.astype(jnp.bfloat16), 'tp', scatter_dimensio...  58.8 us
    all_to_all x1, blocking collectives, sent_together(): lax.all_to_all(both, axis, split_axis=split_dim, concat_axis=concat_dim,...  39.4 us
    all_to_all x1, starting transfers between devices, local(): lax.all_to_all(returned, 'ep', split_axis=0, concat_axis=0, tiled=True)  10.3 us
    all_to_all x1, waiting for transfers between devices, local(): lax.all_to_all(returned, 'ep', split_axis=0, concat_axis=0, tiled=True)  9.89 us
    dot_general x3, matrix products, contract_rows(): lax.dot_general(left, right, (((0,), (0,)), ((), ())), preferred_element_...  7.79 us
  transfers between devices with their start and end apart: 3, of which 3 were waited for; matrix products, arithmetic and copies ran while one was open for 3% of the time, Pallas kernels for 0%

commit v1 on v0

v1 whole, which is shorter than its diff:
```python
import jax
import jax.numpy as jnp
import numpy as np
from jax import lax
from jax.experimental import pallas as pl
from jax.experimental.pallas import tpu as pltpu
from jax.sharding import PartitionSpec as P

VMEM = pl.BlockSpec(memory_space=pltpu.VMEM)
SMEM = pl.BlockSpec(memory_space=pltpu.SMEM)
PARAMS = pltpu.CompilerParams(vmem_limit_bytes=48 * 1024 * 1024)


def nt(left, right):
    return lax.dot_general(left, right, (((1,), (1,)), ((), ())), preferred_element_type=jnp.float32)


def tn(left, right):
    return lax.dot_general(left, right, (((0,), (0,)), ((), ())), preferred_element_type=jnp.float32)


def nn(left, right):
    return jnp.dot(left, right, preferred_element_type=jnp.float32)


def dispatch(ids, gates, both, experts, slots):
    top, tokens = ids.shape
    width = both.shape[1] // 2
    count = experts * slots

    def kernel(ids_ref, gates_ref, both_ref, rows_ref, place_ref):
        ids = ids_ref[...]
        gates = gates_ref[...]
        expert = lax.broadcasted_iota(jnp.int32, (experts, tokens), 0)
        named = jnp.zeros((experts, tokens), jnp.float32)
        gate = jnp.zeros((experts, tokens), jnp.float32)
        for k in range(top):
            hit = ids[k : k + 1, :] == expert
            named = jnp.where(hit, 1.0, named)
            gate = jnp.where(hit, gates[k : k + 1, :], gate)
        earlier = (
            lax.broadcasted_iota(jnp.int32, (tokens, tokens), 0)
            < lax.broadcasted_iota(jnp.int32, (tokens, tokens), 1)
        ).astype(jnp.float32)
        before = nn(named.astype(jnp.bfloat16), earlier.astype(jnp.bfloat16))
        slot = jnp.where(named > 0.0, before, -1.0)
        shape = (experts, slots, tokens)
        wanted = lax.broadcasted_iota(jnp.int32, shape, 1).astype(jnp.float32)
        match = jnp.broadcast_to(slot[:, None, :], shape) == wanted
        scale = jnp.where(match, jnp.broadcast_to(gate[:, None, :], shape), 0.0)
        scale = jnp.sum(scale.reshape(count, tokens), axis=1, keepdims=True)
        place = match.astype(jnp.float32).reshape(count, tokens).astype(jnp.bfloat16)
        place_ref[...] = place
        rows_ref[:, :width] = nn(place, both_ref[:, :width]).astype(jnp.bfloat16)
        rows_ref[:, width:] = (scale * nn(place, both_ref[:, width:])).astype(jnp.bfloat16)

    return pl.pallas_call(
        kernel,
        out_shape=(
            jax.ShapeDtypeStruct((count, 2 * width), jnp.bfloat16),
            jax.ShapeDtypeStruct((count, tokens), jnp.bfloat16),
        ),
        in_specs=[VMEM] * 3,
        out_specs=(VMEM, VMEM),
        compiler_params=PARAMS,
        name="dispatch",
    )(ids, gates, both)


def first_products(owners, features, cotangents, weights):
    count = len(features)
    rows, width = features[0].shape
    units = weights[0].shape[0]

    def kernel(owners_ref, *refs):
        x, g = refs[:count], refs[count : 2 * count]
        w_gate, w_up, w_down = refs[2 * count : 2 * count + 3]
        a_ref, b_ref, dh_ref = refs[2 * count + 3 :]
        for k in range(count):
            part = pl.ds(pl.multiple_of(owners_ref[k] * width, width), width)
            a, b = nt(w_gate[:, part], x[k][...]), nt(w_up[:, part], x[k][...])
            dh = nt(w_down[:, part], g[k][...])
            if k == 0:
                a_ref[...], b_ref[...], dh_ref[...] = a, b, dh
            else:
                a_ref[...] += a
                b_ref[...] += b
                dh_ref[...] += dh

    return pl.pallas_call(
        kernel,
        out_shape=[jax.ShapeDtypeStruct((units, rows), jnp.float32)] * 3,
        in_specs=[SMEM] + [VMEM] * (2 * count + 3),
        out_specs=[VMEM] * 3,
        compiler_params=PARAMS,
        name="first_products",
    )(owners, *features, *cotangents, *weights)


def activations(owners, features, cotangents, weights, sums):
    count = len(features)
    rows, width = features[0].shape
    units = weights[0].shape[0]

    def kernel(owners_ref, *refs):
        x, g = refs[:count], refs[count : 2 * count]
        w_gate, w_up, w_down = refs[2 * count : 2 * count + 3]
        a_ref, b_ref, dh_ref = refs[2 * count + 3 : 2 * count + 6]
        grads_ref, hidden_ref = refs[2 * count + 6 :]
        a, b, dh = a_ref[...], b_ref[...], dh_ref[...]
        for k in range(count):
            part = pl.ds(pl.multiple_of(owners_ref[k] * width, width), width)
            a += nt(w_gate[:, part], x[k][...])
            b += nt(w_up[:, part], x[k][...])
            dh += nt(w_down[:, part], g[k][...])
        s = jax.nn.sigmoid(a)
        swish = a * s
        hidden_ref[...] = (swish * b).astype(jnp.bfloat16)
        grads_ref[:units, :] = (dh * b * s * (1.0 + a * (1.0 - s))).astype(jnp.bfloat16)
        grads_ref[units:, :] = (dh * swish).astype(jnp.bfloat16)

    return pl.pallas_call(
        kernel,
        out_shape=(
            jax.ShapeDtypeStruct((2 * units, rows), jnp.bfloat16),
            jax.ShapeDtypeStruct((units, rows), jnp.bfloat16),
        ),
        in_specs=[SMEM] + [VMEM] * (2 * count + 6),
        out_specs=(VMEM, VMEM),
        compiler_params=PARAMS,
        name="activations",
    )(owners, *features, *cotangents, *weights, *sums)


def weight_grads(owners, features, cotangents, grads, hidden):
    count = len(features)
    rows, width = features[0].shape
    units = hidden.shape[0]

    def kernel(owners_ref, *refs):
        x, g = refs[:count], refs[count : 2 * count]
        grads_ref, hidden_ref, gate_ref, up_ref, down_ref = refs[2 * count :]
        for k in range(count):
            part = pl.ds(pl.multiple_of(owners_ref[k] * width, width), width)
            both = nn(grads_ref[...], x[k][...]).astype(jnp.bfloat16)
            gate_ref[:, part] = both[:units]
            up_ref[:, part] = both[units:]
            down_ref[:, part] = nn(hidden_ref[...], g[k][...]).astype(jnp.bfloat16)

    return pl.pallas_call(
        kernel,
        out_shape=[jax.ShapeDtypeStruct((units, count * width), jnp.bfloat16)] * 3,
        in_specs=[SMEM] + [VMEM] * (2 * count + 2),
        out_specs=[VMEM] * 3,
        compiler_params=PARAMS,
        name="weight_grads",
    )(owners, *features, *cotangents, grads, hidden)


def local(tokens, cotangent, expert_ids, gate_values, w_gate, w_up, w_down):
    groups = lax.axis_size("ep")
    ring = lax.axis_size("tp")
    half = ring // 2
    tok_count, top_count = expert_ids.shape
    slots = max(2, tok_count * top_count * 4 // (groups * 3))
    width = tokens.shape[1]
    rows = groups * slots
    me = lax.axis_index("tp")
    weights = (w_gate[0], w_up[0], w_down[0])

    def moved(value, by):
        return lax.ppermute(value, "tp", [(i, (i + by) % ring) for i in range(ring)])

    def over_ep(value):
        shape = (groups, slots, value.shape[1])
        value = lax.all_to_all(value.reshape(shape), "ep", split_axis=0, concat_axis=0, tiled=True)
        return value.reshape(rows, -1)

    ids, gates = expert_ids.T, gate_values.T
    both = jnp.concatenate([tokens, cotangent], axis=1)
    far_both = moved(both, half)
    sent, place = dispatch(ids, gates, both, groups, slots)
    mine = over_ep(sent)
    far_sent, _ = dispatch(ids, gates, far_both, groups, slots)
    mine, far_sent = lax.optimization_barrier((mine, far_sent))
    far = over_ep(far_sent)

    x, g = {0: mine[:, :width]}, {0: mine[:, width:]}
    x[half], g[half] = far[:, :width], far[:, width:]
    for step in range(1, half):
        for blocks in (x, g):
            blocks[-step] = moved(blocks[1 - step], 1)
            blocks[step] = moved(blocks[step - 1], -1)

    def owners(order):
        steps = np.array([d % ring for d in order], np.int32)
        return lax.rem(me.astype(jnp.int32) + steps, np.int32(ring))

    def picked(blocks, order):
        return [blocks[d] for d in order]

    early = [d for step in range(half - 1) for d in ([-step, step] if step else [0])]
    late = [1 - half, half - 1, half]
    sums = first_products(owners(early), picked(x, early), picked(g, early), weights)
    grads, hidden = activations(owners(late), picked(x, late), picked(g, late), weights, sums)

    paired = jnp.concatenate(weights[:2], axis=0)

    def partial(d):
        at = lax.rem(me + d % ring, ring) * width
        return tn(grads, lax.dynamic_slice_in_dim(paired, at, width, axis=1))

    far_back = over_ep(partial(half).astype(jnp.bfloat16))
    right = partial(half - 1).astype(jnp.bfloat16)
    left = partial(1 - half).astype(jnp.bfloat16)
    for d in range(half - 2, -1, -1):
        right, left = moved(right, 1), moved(left, -1)
        if d:
            right = (right.astype(jnp.float32) + partial(d)).astype(jnp.bfloat16)
            left = (left.astype(jnp.float32) + partial(-d)).astype(jnp.bfloat16)
    total = partial(0) + right.astype(jnp.float32) + left.astype(jnp.float32)

    order = early + late
    grad_gate, grad_up, grad_down = weight_grads(
        owners(order), picked(x, order), picked(g, order), grads, hidden
    )
    back = over_ep(total.astype(jnp.bfloat16))
    far_tokens = moved(tn(place, far_back).astype(jnp.bfloat16), half)
    input_grad = (tn(place, back) + far_tokens.astype(jnp.float32)).astype(jnp.bfloat16)
    return (input_grad, grad_gate[None], grad_up[None], grad_down[None])


def solution(mesh):
    in_specs = (
        P("ep", "tp"),
        P("ep", "tp"),
        P("ep", None),
        P("ep", None),
        P("ep", "tp", None),
        P("ep", "tp", None),
        P("ep", "tp", None),
    )
    out_specs = (P("ep", "tp"), P("ep", "tp", None), P("ep", "tp", None), P("ep", "tp", None))
    return jax.shard_map(local, mesh=mesh, in_specs=in_specs, out_specs=out_specs, check_vma=False)
```

time: 281 us -> 240 us (0.85)
  starting transfers between devices: 10.4 us -> 125 us
  waiting for transfers between devices: 170 us -> 65.6 us
  blocking collectives: 39.4 us -> 0 us
  Pallas kernels: 0 us -> 19.7 us
  local copies, waits for them, and re-layouts: 22.9 us -> 8.5 us
  between operations: 14.4 us -> 1.2 us
  other arithmetic: 5.74 us -> 0.03 us
    all_gather x1 -> x0, waiting for transfers between devices: 102 us -> none  [in_one_piece(): filled = lax.all_gather(both, axis, axis=dim, tiled=True)]
    ppermute x0 -> x20, starting transfers between devices: none -> 81.3 us  [moved(): lax.ppermute(value, 'tp', [(i, (i + by) % ring) for i in range(ring)])]
    reduce_scatter x1 -> x0, waiting for transfers between devices: 58.8 us -> none  [local(): lax.psum_scatter(input_terms.astype(jnp.bfloat16), 'tp', scatter_dimensio...]
    ppermute x0 -> x20, waiting for transfers between devices: none -> 50.7 us  [moved(): lax.ppermute(value, 'tp', [(i, (i + by) % ring) for i in range(ring)])]
    all_to_all x1 -> x0, blocking collectives: 39.4 us -> none  [sent_together(): lax.all_to_all(both, axis, split_axis=split_dim, concat_axis=concat_dim,...]
    all_to_all x1 -> x4, starting transfers between devices: 10.3 us -> 43.2 us  [over_ep(): lax.all_to_all(value.reshape(shape), 'ep', split_axis=0, concat_axis=0, t...]
    pallas_call x0 -> x5, Pallas kernels: none -> 19.7 us  [the longest x1 6.24 us: weight_grads(): pl.pallas_call(kernel, out_shape=[jax.ShapeDtypeStruct((units, count * wi...]
    gather x5 -> x0, local copies, waits for them, and re-layouts: 15.2 us -> none  [the longest x1 4.53 us: dispatch_rows(): gate_values.reshape(-1)[pair_index][:, None]]
  transfers between devices with their start and end apart: 3 -> 24, of which waited for: 3 -> 12; matrix products, arithmetic and copies ran while one was open for 3% -> 7% of each run, Pallas kernels for 0% -> 6%
where the time goes in v1:
time: 240 us; the launch traced here: 239 us
  starting transfers between devices  125 us (52%)
  waiting for transfers between devices  65.6 us (27%)
  Pallas kernels  19.7 us (8%)
  matrix products  19 us (8%)
  local copies, waits for them, and re-layouts  8.5 us (4%)
    ppermute x20, starting transfers between devices, moved(): lax.ppermute(value, 'tp', [(i, (i + by) % ring) for i in range(ring)])  81.3 us
    ppermute x20, waiting for transfers between devices, moved(): lax.ppermute(value, 'tp', [(i, (i + by) % ring) for i in range(ring)])  50.7 us
    all_to_all x4, starting transfers between devices, over_ep(): lax.all_to_all(value.reshape(shape), 'ep', split_axis=0, concat_axis=0, t...  43.2 us
    dot_general x10, matrix products, tn(): lax.dot_general(left, right, (((0,), (0,)), ((), ())), preferred_element_...  19 us
    all_to_all x4, waiting for transfers between devices, over_ep(): lax.all_to_all(value.reshape(shape), 'ep', split_axis=0, concat_axis=0, t...  14.9 us
    pallas_call x1, Pallas kernels, weight_grads(): pl.pallas_call(kernel, out_shape=[jax.ShapeDtypeStruct((units, count * wi...  6.24 us
    unnamed x49, local copies, waits for them, and re-layouts  6.21 us
    pallas_call x1, Pallas kernels, first_products(): pl.pallas_call(kernel, out_shape=[jax.ShapeDtypeStruct((units, rows), jnp...  5.86 us
  transfers between devices with their start and end apart: 24, of which 12 were waited for; matrix products, arithmetic and copies ran while one was open for 7% of the time, Pallas kernels for 6%

profile of v1, /device:TPU:1, one launch (start us, length us, event | category | flops | bytes accessed | tf_op | source)
XLA Modules:
  0.0 238.6 jit_solution(4879432733948059831)
XLA Ops:
  3.7 1.6 dispatch.2
  5.3 11.7 %all-to-all-start = ((bf16[64,16,512]{2,1,0:T(8,128)(2,1)}), bf16[64,16,512]{2,1,0:T(8,128)(2,1)S(1)}, u32[]{:S(2)}, u32[]{:S(2)}) async-start(bf16[64,16,512]{2,1,0:T(8,128)(2,1)} %bitcast.2), calls=%async_computation | async-start | bytes 2097152 | tf_op jit(solution)/shard_map/all_to_all | solution.py:176
  17.1 10.6 %collective-permute-start = (bf16[128,512]{1,0:T(8,128)(2,1)S(1)}, bf16[128,512]{1,0:T(8,128)(2,1)S(1)}, u32[]{:S(2)}, u32[]{:S(2)}) collective-permute-start(bf16[128,512]{1,0:T(8,128)(2,1)S(1)} %constant_dynamic-update-slice_fusion.both_ref), channel_id=1, source_target_pairs={{0,4},{1,5},{2,6},{3,7},{4,0},{5,1},{6,2},{7,3},{8,12},{9,13},{10,... | collective-permute-start | bytes 393224 | tf_op jit(solution)/shard_map/ppermute | solution.py:172
  27.7 3.5 %collective-permute-done.both_ref = bf16[128,512]{1,0:T(8,128)(2,1)S(1)} collective-permute-done((bf16[128,512]{1,0:T(8,128)(2,1)S(1)}, bf16[128,512]{1,0:T(8,128)(2,1)S(1)}, u32[]{:S(2)}, u32[]{:S(2)}) %collective-permute-start) | collective-permute-done | bytes 131104 | tf_op jit(solution)/shard_map/ppermute | solution.py:172
  31.2 1.7 dispatch.3
  32.9 12.2 %all-to-all-done = bf16[64,16,512]{2,1,0:T(8,128)(2,1)S(1)} async-done(((bf16[64,16,512]{2,1,0:T(8,128)(2,1)}), bf16[64,16,512]{2,1,0:T(8,128)(2,1)S(1)}, u32[]{:S(2)}, u32[]{:S(2)}) %all-to-all-start) | async-done | bytes 1048608 | tf_op jit(solution)/shard_map/all_to_all | solution.py:176
  45.1 6.7 %all-to-all-start.1 = ((bf16[64,16,512]{2,1,0:T(8,128)(2,1)}), bf16[64,16,512]{2,1,0:T(8,128)(2,1)}, u32[]{:S(2)}, u32[]{:S(2)}) async-start(bf16[64,16,512]{2,1,0:T(8,128)(2,1)} %bitcast.4), calls=%async_computation.1 | async-start | bytes 2097152 | tf_op jit(solution)/shard_map/all_to_all | solution.py:176
  51.8 4.0 %collective-permute-start.1 = (bf16[1024,256]{1,0:T(8,128)(2,1)S(1)}, bf16[1024,256]{1,0:T(8,128)(2,1)S(1)}, u32[]{:S(2)}, u32[]{:S(2)}) collective-permute-start(bf16[1024,256]{1,0:T(8,128)(2,1)S(1)} %get-tuple-element.33.refs_0_), channel_id=1, source_target_pairs={{0,1},{1,2},{2,3},{3,4},{4,5},{5,6},{6,7},{7,0},{8,9},{9,10},{10,1... | collective-permute-start | bytes 1572872 | tf_op jit(solution)/shard_map/ppermute | solution.py:172
  55.9 8.6 %collective-permute-start.4 = (bf16[1024,256]{1,0:T(8,128)(2,1)S(1)}, bf16[1024,256]{1,0:T(8,128)(2,1)S(1)}, u32[]{:S(2)}, u32[]{:S(2)}) collective-permute-start(bf16[1024,256]{1,0:T(8,128)(2,1)S(1)} %get-tuple-element.33.refs_0_), channel_id=1, source_target_pairs={{0,7},{1,0},{2,1},{3,2},{4,3},{5,4},{6,5},{7,6},{8,15},{9,8},{10,9... | collective-permute-start | bytes 1572872 | tf_op jit(solution)/shard_map/ppermute | solution.py:172
  64.5 1.9 collective-permute-start.7
  66.4 4.6 %collective-permute-start.10 = (bf16[1024,256]{1,0:T(8,128)(2,1)S(1)}, bf16[1024,256]{1,0:T(8,128)(2,1)S(1)}, u32[]{:S(2)}, u32[]{:S(2)}) collective-permute-start(bf16[1024,256]{1,0:T(8,128)(2,1)S(1)} %get-tuple-element.32.refs_5_.refs_8_), channel_id=1, source_target_pairs={{0,7},{1,0},{2,1},{3,2},{4,3},{5,4},{6,5},{7,6},{8,15},{9,8},{10,9... | collective-permute-start | bytes 1572872 | tf_op jit(solution)/shard_map/ppermute | solution.py:172
  71.0 3.5 %collective-permute-done.1.refs_1_ = bf16[1024,256]{1,0:T(8,128)(2,1)S(1)} collective-permute-done((bf16[1024,256]{1,0:T(8,128)(2,1)S(1)}, bf16[1024,256]{1,0:T(8,128)(2,1)S(1)}, u32[]{:S(2)}, u32[]{:S(2)}) %collective-permute-start.1) | collective-permute-done | bytes 524320 | tf_op jit(solution)/shard_map/ppermute | solution.py:172
  74.4 1.9 collective-permute-start.2
  76.4 4.6 %collective-permute-start.5 = (bf16[1024,256]{1,0:T(8,128)(2,1)S(1)}, bf16[1024,256]{1,0:T(8,128)(2,1)}, u32[]{:S(2)}, u32[]{:S(2)}) collective-permute-start(bf16[1024,256]{1,0:T(8,128)(2,1)S(1)} %collective-permute-done.4.refs_2_), channel_id=1, source_target_pairs={{0,7},{1,0},{2,1},{3,2},{4,3},{5,4},{6,5},{7,6},{8,15},{9,8},{10,9... | collective-permute-start | bytes 1572872 | tf_op jit(solution)/shard_map/ppermute | solution.py:172
  81.0 4.6 %collective-permute-done.7.refs_6_.refs_9_ = bf16[1024,256]{1,0:T(8,128)(2,1)S(1)} collective-permute-done((bf16[1024,256]{1,0:T(8,128)(2,1)S(1)}, bf16[1024,256]{1,0:T(8,128)(2,1)S(1)}, u32[]{:S(2)}, u32[]{:S(2)}) %collective-permute-start.7) | collective-permute-done | bytes 524320 | tf_op jit(solution)/shard_map/ppermute | solution.py:172
  85.6 1.9 collective-permute-start.8
  87.5 4.6 %collective-permute-start.11 = (bf16[1024,256]{1,0:T(8,128)(2,1)S(1)}, bf16[1024,256]{1,0:T(8,128)(2,1)}, u32[]{:S(2)}, u32[]{:S(2)}) collective-permute-start(bf16[1024,256]{1,0:T(8,128)(2,1)S(1)} %collective-permute-done.10.refs_7_.refs_10_), channel_id=1, source_target_pairs={{0,7},{1,0},{2,1},{3,2},{4,3},{5,4},{6,5},{7,6},{8,15},{9,8},{10,9... | collective-permute-start | bytes 1572872 | tf_op jit(solution)/shard_map/ppermute | solution.py:172
  92.1 4.8 %collective-permute-done.2.refs_3_ = bf16[1024,256]{1,0:T(8,128)(2,1)} collective-permute-done((bf16[1024,256]{1,0:T(8,128)(2,1)S(1)}, bf16[1024,256]{1,0:T(8,128)(2,1)}, u32[]{:S(2)}, u32[]{:S(2)}) %collective-permute-start.2) | collective-permute-done | bytes 524320 | tf_op jit(solution)/shard_map/ppermute | solution.py:172
  96.9 1.9 collective-permute-start.3
  98.8 4.6 %collective-permute-start.6 = (bf16[1024,256]{1,0:T(8,128)(2,1)}, bf16[1024,256]{1,0:T(8,128)(2,1)}, u32[]{:S(2)}, u32[]{:S(2)}) collective-permute-start(bf16[1024,256]{1,0:T(8,128)(2,1)} %collective-permute-done.5.refs_4_), channel_id=1, source_target_pairs={{0,7},{1,0},{2,1},{3,2},{4,3},{5,4},{6,5},{7,6},{8,15},{9,8},{10,9... | collective-permute-start | bytes 1572872 | tf_op jit(solution)/shard_map/ppermute | solution.py:172
  103.4 4.7 %collective-permute-done.8.refs_8_.refs_11_ = bf16[1024,256]{1,0:T(8,128)(2,1)} collective-permute-done((bf16[1024,256]{1,0:T(8,128)(2,1)S(1)}, bf16[1024,256]{1,0:T(8,128)(2,1)}, u32[]{:S(2)}, u32[]{:S(2)}) %collective-permute-start.8) | collective-permute-done | bytes 524320 | tf_op jit(solution)/shard_map/ppermute | solution.py:172
  108.1 1.9 collective-permute-start.9
  110.1 4.6 %collective-permute-start.12 = (bf16[1024,256]{1,0:T(8,128)(2,1)}, bf16[1024,256]{1,0:T(8,128)(2,1)}, u32[]{:S(2)}, u32[]{:S(2)}) collective-permute-start(bf16[1024,256]{1,0:T(8,128)(2,1)} %collective-permute-done.11.refs_9_.refs_12_), channel_id=1, source_target_pairs={{0,7},{1,0},{2,1},{3,2},{4,3},{5,4},{6,5},{7,6},{8,15},{9,8},{10,9... | collective-permute-start | bytes 1572872 | tf_op jit(solution)/shard_map/ppermute | solution.py:172
  114.7 5.9 %first_products.1 = (f32[176,1024]{1,0:T(8,128)S(1)}, f32[176,1024]{1,0:T(8,128)}, f32[176,1024]{1,0:T(8,128)}) custom-call(s32[5]{0:T(128)S(1)} %compare_select_fusion.2.owners_ref, bf16[1024,256]{1,0:T(8,128)(2,1)S(1)} %get-tuple-element.33.refs_0_, bf16[1024,256]{1,0:T(8,128)(2,1)S(1)} %collective-permute-done.1.refs_1_, ...), custom_call_target="tpu_custom_call" | custom-call | tf_op jit(solution)/shard_map/first_products/pallas_call | solution.py:90
  121.5 1.4 fusion.41
  122.9 7.7 %collective-permute-done.9.refs_3_.refs_13_ = bf16[1024,256]{1,0:T(8,128)(2,1)} collective-permute-done((bf16[1024,256]{1,0:T(8,128)(2,1)}, bf16[1024,256]{1,0:T(8,128)(2,1)}, u32[]{:S(2)}, u32[]{:S(2)}) %collective-permute-start.9) | collective-permute-done | bytes 524320 | tf_op jit(solution)/shard_map/ppermute | solution.py:172
  131.5 4.3 %activations.1 = (bf16[352,1024]{1,0:T(8,128)(2,1)S(1)}, bf16[176,1024]{1,0:T(8,128)(2,1)S(1)}) custom-call(s32[3]{0:T(128)S(1)} %compare_select_fusion.4.owners_ref, bf16[1024,256]{1,0:T(8,128)(2,1)} %collective-permute-done.3.refs_0_.refs_5_, bf16[1024,256]{1,0:T(8,128)(2,1)} %collective-permute-done.6.refs_1_.refs_6_, ...), custom_call_target="tpu_custom_call" | custom-call | tf_op jit(solution)/shard_map/activations/pallas_call | solution.py:122
  137.1 5.3 %collective-permute-start.16 = (bf16[1024,256]{1,0:T(8,128)(2,1)}, bf16[1024,256]{1,0:T(8,128)(2,1)}, u32[]{:S(2)}, u32[]{:S(2)}) collective-permute-start(bf16[1024,256]{1,0:T(8,128)(2,1)} %convolution_convert_fusion.1), channel_id=1, source_target_pairs={{0,7},{1,0},{2,1},{3,2},{4,3},{5,4},{6,5},{7,6},{8,15},{9,8},{10,9... | collective-permute-start | bytes 1572872 | tf_op jit(solution)/shard_map/ppermute | solution.py:172
  143.7 1.9 collective-permute-start.13
  145.7 6.9 %collective-permute-done.16 = bf16[1024,256]{1,0:T(8,128)(2,1)} collective-permute-done((bf16[1024,256]{1,0:T(8,128)(2,1)}, bf16[1024,256]{1,0:T(8,128)(2,1)}, u32[]{:S(2)}, u32[]{:S(2)}) %collective-permute-start.16) | collective-permute-done | bytes 524320 | tf_op jit(solution)/shard_map/ppermute | solution.py:172
  152.6 2.3 fusion.4
  154.9 5.3 %collective-permute-start.17 = (bf16[1024,256]{1,0:T(8,128)(2,1)}, bf16[1024,256]{1,0:T(8,128)(2,1)}, u32[]{:S(2)}, u32[]{:S(2)}) collective-permute-start(bf16[1024,256]{1,0:T(8,128)(2,1)} %fusion.4), channel_id=1, source_target_pairs={{0,7},{1,0},{2,1},{3,2},{4,3},{5,4},{6,5},{7,6},{8,15},{9,8},{10,9... | collective-permute-start | bytes 1572872 | tf_op jit(solution)/shard_map/ppermute | solution.py:172
  160.2 2.3 fusion.2
  162.6 1.9 collective-permute-start.14
  165.8 12.9 %all-to-all-start.3 = ((bf16[64,16,256]{2,1,0:T(8,128)(2,1)}), bf16[64,16,256]{2,1,0:T(8,128)(2,1)}, u32[]{:S(2)}, u32[]{:S(2)}) async-start(bf16[64,16,256]{2,1,0:T(8,128)(2,1)} %bitcast.55), calls=%async_computation.3 | async-start | bytes 1048576 | tf_op jit(solution)/shard_map/all_to_all | solution.py:176
  178.7 2.3 fusion.5
  181.0 5.0 %collective-permute-start.18 = (bf16[1024,256]{1,0:T(8,128)(2,1)}, bf16[1024,256]{1,0:T(8,128)(2,1)}, u32[]{:S(2)}, u32[]{:S(2)}) collective-permute-start(bf16[1024,256]{1,0:T(8,128)(2,1)} %fusion.5), channel_id=1, source_target_pairs={{0,7},{1,0},{2,1},{3,2},{4,3},{5,4},{6,5},{7,6},{8,15},{9,8},{10,9... | collective-permute-start | bytes 1572872 | tf_op jit(solution)/shard_map/ppermute | solution.py:172
  186.1 2.3 fusion.3
  188.4 1.9 collective-permute-start.15
  190.3 6.6 %collective-permute-done.18 = bf16[1024,256]{1,0:T(8,128)(2,1)} collective-permute-done((bf16[1024,256]{1,0:T(8,128)(2,1)}, bf16[1024,256]{1,0:T(8,128)(2,1)}, u32[]{:S(2)}, u32[]{:S(2)}) %collective-permute-start.18) | collective-permute-done | bytes 524320 | tf_op jit(solution)/shard_map/ppermute | solution.py:172
  196.9 7.5 %collective-permute-done.15 = bf16[1024,256]{1,0:T(8,128)(2,1)} collective-permute-done((bf16[1024,256]{1,0:T(8,128)(2,1)}, bf16[1024,256]{1,0:T(8,128)(2,1)}, u32[]{:S(2)}, u32[]{:S(2)}) %collective-permute-start.15) | collective-permute-done | bytes 524320 | tf_op jit(solution)/shard_map/ppermute | solution.py:172
  204.4 2.6 %fusion.1 = bf16[1024,256]{1,0:T(8,128)(2,1)} fusion(bf16[352,1024]{1,0:T(8,128)(2,1)S(1)} %get-tuple-element.25.refs_16_, bf16[1024,256]{1,0:T(8,128)(2,1)} %collective-permute-done.18, bf16[1024,256]{1,0:T(8,128)(2,1)} %collective-permute-done.15, s32[]{:T(128)S(6)} %select_n.24, bf16[176,2048]{1,0:T(8,128)(2,1)S(1)} %bitcast.37, ...), kind=kOutput, calls=%fused_computation.22 | convolution fusion | flops 186220544 | bytes 3735556 | tf_op jit(solution)/shard_map/dot_general | solution.py:19
  207.0 12.0 %all-to-all-start.2 = ((bf16[64,16,256]{2,1,0:T(8,128)(2,1)}), bf16[64,16,256]{2,1,0:T(8,128)(2,1)}, u32[]{:S(2)}, u32[]{:S(2)}) async-start(bf16[64,16,256]{2,1,0:T(8,128)(2,1)} %bitcast.56), calls=%async_computation.2 | async-start | bytes 1048576 | tf_op jit(solution)/shard_map/all_to_all | solution.py:176
  219.0 1.3 convolution_convert_fusion.3
  220.3 4.2 %collective-permute-start.19 = (bf16[128,256]{1,0:T(8,128)(2,1)S(1)}, bf16[128,256]{1,0:T(8,128)(2,1)S(1)}, u32[]{:S(2)}, u32[]{:S(2)}) collective-permute-start(bf16[128,256]{1,0:T(8,128)(2,1)S(1)} %convolution_convert_fusion.3), channel_id=1, source_target_pairs={{0,4},{1,5},{2,6},{3,7},{4,0},{5,1},{6,2},{7,3},{8,12},{9,13},{10,... | collective-permute-start | bytes 196616 | tf_op jit(solution)/shard_map/ppermute | solution.py:172
  227.7 6.2 %weight_grads.1 = (bf16[176,2048]{1,0:T(8,128)(2,1)}, bf16[176,2048]{1,0:T(8,128)(2,1)}, bf16[176,2048]{1,0:T(8,128)(2,1)}) custom-call(s32[8]{0:T(128)S(1)} %compare_select_fusion.owners_ref, bf16[1024,256]{1,0:T(8,128)(2,1)S(1)} %get-tuple-element.33.refs_0_, bf16[1024,256]{1,0:T(8,128)(2,1)S(1)} %copy-done.7, bf16[1024,256]{1,0:T(8,128)(2,1)S(1)} %copy-done.9, ...), custom_call_target="tpu_custom_call" | custom-call | tf_op jit(solution)/shard_map/weight_grads/pallas_call | solution.py:150
  233.9 2.7 %all-to-all-done.2 = bf16[64,16,256]{2,1,0:T(8,128)(2,1)} async-done(((bf16[64,16,256]{2,1,0:T(8,128)(2,1)}), bf16[64,16,256]{2,1,0:T(8,128)(2,1)}, u32[]{:S(2)}, u32[]{:S(2)}) %all-to-all-start.2) | async-done | bytes 524320 | tf_op jit(solution)/shard_map/all_to_all | solution.py:176
  236.6 1.9 add_convert_fusion
  (70 shorter events, 11.9 us)
Async XLA Ops:
  2.3 0.7 copy-start.17
  3.0 0.7 copy-start.19
  5.3 25.9 %copy-start.18 = (s32[128,6]{0,1:T(8,128)S(1)}, s32[128,6]{0,1:T(8,128)}, u32[]{:S(2)}) copy-start(s32[128,6]{0,1:T(8,128)} %param.12) | copy-start | bytes 9220
  5.3 25.9 %copy-start.20 = (f32[128,6]{0,1:T(8,128)S(1)}, f32[128,6]{0,1:T(8,128)}, u32[]{:S(2)}) copy-start(f32[128,6]{0,1:T(8,128)} %param.13) | copy-start | bytes 9220
  5.3 39.7 %all-to-all-start = ((bf16[64,16,512]{2,1,0:T(8,128)(2,1)}), bf16[64,16,512]{2,1,0:T(8,128)(2,1)S(1)}, u32[]{:S(2)}, u32[]{:S(2)}) async-start(bf16[64,16,512]{2,1,0:T(8,128)(2,1)} %bitcast.2), calls=%async_computation | async-start | bytes 2097152 | tf_op jit(solution)/shard_map/all_to_all | solution.py:176
  17.1 14.1 %collective-permute-start = (bf16[128,512]{1,0:T(8,128)(2,1)S(1)}, bf16[128,512]{1,0:T(8,128)(2,1)S(1)}, u32[]{:S(2)}, u32[]{:S(2)}) collective-permute-start(bf16[128,512]{1,0:T(8,128)(2,1)S(1)} %constant_dynamic-update-slice_fusion.both_ref), channel_id=1, source_target_pairs={{0,4},{1,5},{2,6},{3,7},{4,0},{5,1},{6,2},{7,3},{8,12},{9,13},{10,... | collective-permute-start | bytes 393224 | tf_op jit(solution)/shard_map/ppermute | solution.py:172
  45.1 76.4 %all-to-all-start.1 = ((bf16[64,16,512]{2,1,0:T(8,128)(2,1)}), bf16[64,16,512]{2,1,0:T(8,128)(2,1)}, u32[]{:S(2)}, u32[]{:S(2)}) async-start(bf16[64,16,512]{2,1,0:T(8,128)(2,1)} %bitcast.4), calls=%async_computation.1 | async-start | bytes 2097152 | tf_op jit(solution)/shard_map/all_to_all | solution.py:176
  51.7 62.9 %copy-start.23 = (s32[3]{0:T(128)S(1)}, s32[3]{0:T(128)}, u32[]{:S(2)}) copy-start(s32[3]{0:T(128)} %constant.57.clone) | copy-start | bytes 40
  51.8 62.9 %copy-start.22 = (s32[5]{0:T(128)S(1)}, s32[5]{0:T(128)}, u32[]{:S(2)}) copy-start(s32[5]{0:T(128)} %constant.56.clone) | copy-start | bytes 64
  51.8 22.6 %collective-permute-start.1 = (bf16[1024,256]{1,0:T(8,128)(2,1)S(1)}, bf16[1024,256]{1,0:T(8,128)(2,1)S(1)}, u32[]{:S(2)}, u32[]{:S(2)}) collective-permute-start(bf16[1024,256]{1,0:T(8,128)(2,1)S(1)} %get-tuple-element.33.refs_0_), channel_id=1, source_target_pairs={{0,1},{1,2},{2,3},{3,4},{4,5},{5,6},{6,7},{7,0},{8,9},{9,10},{10,1... | collective-permute-start | bytes 1572872 | tf_op jit(solution)/shard_map/ppermute | solution.py:172
  55.9 20.5 %collective-permute-start.4 = (bf16[1024,256]{1,0:T(8,128)(2,1)S(1)}, bf16[1024,256]{1,0:T(8,128)(2,1)S(1)}, u32[]{:S(2)}, u32[]{:S(2)}) collective-permute-start(bf16[1024,256]{1,0:T(8,128)(2,1)S(1)} %get-tuple-element.33.refs_0_), channel_id=1, source_target_pairs={{0,7},{1,0},{2,1},{3,2},{4,3},{5,4},{6,5},{7,6},{8,15},{9,8},{10,9... | collective-permute-start | bytes 1572872 | tf_op jit(solution)/shard_map/ppermute | solution.py:172
  64.5 21.1 %collective-permute-start.7 = (bf16[1024,256]{1,0:T(8,128)(2,1)S(1)}, bf16[1024,256]{1,0:T(8,128)(2,1)S(1)}, u32[]{:S(2)}, u32[]{:S(2)}) collective-permute-start(bf16[1024,256]{1,0:T(8,128)(2,1)S(1)} %get-tuple-element.32.refs_5_.refs_8_), channel_id=1, source_target_pairs={{0,1},{1,2},{2,3},{3,4},{4,5},{5,6},{6,7},{7,0},{8,9},{9,10},{10,1... | collective-permute-start | bytes 1572872 | tf_op jit(solution)/shard_map/ppermute | solution.py:172
  66.4 21.1 %collective-permute-start.10 = (bf16[1024,256]{1,0:T(8,128)(2,1)S(1)}, bf16[1024,256]{1,0:T(8,128)(2,1)S(1)}, u32[]{:S(2)}, u32[]{:S(2)}) collective-permute-start(bf16[1024,256]{1,0:T(8,128)(2,1)S(1)} %get-tuple-element.32.refs_5_.refs_8_), channel_id=1, source_target_pairs={{0,7},{1,0},{2,1},{3,2},{4,3},{5,4},{6,5},{7,6},{8,15},{9,8},{10,9... | collective-permute-start | bytes 1572872 | tf_op jit(solution)/shard_map/ppermute | solution.py:172
  74.4 46.1 %copy-start.6 = (bf16[1024,256]{1,0:T(8,128)(2,1)}, bf16[1024,256]{1,0:T(8,128)(2,1)S(1)}, u32[]{:S(2)}) copy-start(bf16[1024,256]{1,0:T(8,128)(2,1)S(1)} %collective-permute-done.1.refs_1_) | copy-start | bytes 1572868
  74.4 22.5 %collective-permute-start.2 = (bf16[1024,256]{1,0:T(8,128)(2,1)S(1)}, bf16[1024,256]{1,0:T(8,128)(2,1)}, u32[]{:S(2)}, u32[]{:S(2)}) collective-permute-start(bf16[1024,256]{1,0:T(8,128)(2,1)S(1)} %collective-permute-done.1.refs_1_), channel_id=1, source_target_pairs={{0,1},{1,2},{2,3},{3,4},{4,5},{5,6},{6,7},{7,0},{8,9},{9,10},{10,1... | collective-permute-start | bytes 1572872 | tf_op jit(solution)/shard_map/ppermute | solution.py:172
  76.4 44.2 %copy-start.8 = (bf16[1024,256]{1,0:T(8,128)(2,1)}, bf16[1024,256]{1,0:T(8,128)(2,1)S(1)}, u32[]{:S(2)}) copy-start(bf16[1024,256]{1,0:T(8,128)(2,1)S(1)} %collective-permute-done.4.refs_2_) | copy-start | bytes 1572868
  76.4 22.5 %collective-permute-start.5 = (bf16[1024,256]{1,0:T(8,128)(2,1)S(1)}, bf16[1024,256]{1,0:T(8,128)(2,1)}, u32[]{:S(2)}, u32[]{:S(2)}) collective-permute-start(bf16[1024,256]{1,0:T(8,128)(2,1)S(1)} %collective-permute-done.4.refs_2_), channel_id=1, source_target_pairs={{0,7},{1,0},{2,1},{3,2},{4,3},{5,4},{6,5},{7,6},{8,15},{9,8},{10,9... | collective-permute-start | bytes 1572872 | tf_op jit(solution)/shard_map/ppermute | solution.py:172
  85.6 35.0 %copy-start.10 = (bf16[1024,256]{1,0:T(8,128)(2,1)}, bf16[1024,256]{1,0:T(8,128)(2,1)S(1)}, u32[]{:S(2)}) copy-start(bf16[1024,256]{1,0:T(8,128)(2,1)S(1)} %collective-permute-done.7.refs_6_.refs_9_) | copy-start | bytes 1572868
  85.6 22.6 %collective-permute-start.8 = (bf16[1024,256]{1,0:T(8,128)(2,1)S(1)}, bf16[1024,256]{1,0:T(8,128)(2,1)}, u32[]{:S(2)}, u32[]{:S(2)}) collective-permute-start(bf16[1024,256]{1,0:T(8,128)(2,1)S(1)} %collective-permute-done.7.refs_6_.refs_9_), channel_id=1, source_target_pairs={{0,1},{1,2},{2,3},{3,4},{4,5},{5,6},{6,7},{7,0},{8,9},{9,10},{10,1... | collective-permute-start | bytes 1572872 | tf_op jit(solution)/shard_map/ppermute | solution.py:172
  87.5 33.1 %copy-start.12 = (bf16[1024,256]{1,0:T(8,128)(2,1)}, bf16[1024,256]{1,0:T(8,128)(2,1)S(1)}, u32[]{:S(2)}) copy-start(bf16[1024,256]{1,0:T(8,128)(2,1)S(1)} %collective-permute-done.10.refs_7_.refs_10_) | copy-start | bytes 1572868
  87.5 22.6 %collective-permute-start.11 = (bf16[1024,256]{1,0:T(8,128)(2,1)S(1)}, bf16[1024,256]{1,0:T(8,128)(2,1)}, u32[]{:S(2)}, u32[]{:S(2)}) collective-permute-start(bf16[1024,256]{1,0:T(8,128)(2,1)S(1)} %collective-permute-done.10.refs_7_.refs_10_), channel_id=1, source_target_pairs={{0,7},{1,0},{2,1},{3,2},{4,3},{5,4},{6,5},{7,6},{8,15},{9,8},{10,9... | collective-permute-start | bytes 1572872 | tf_op jit(solution)/shard_map/ppermute | solution.py:172
  96.9 26.0 %collective-permute-start.3 = (bf16[1024,256]{1,0:T(8,128)(2,1)}, bf16[1024,256]{1,0:T(8,128)(2,1)}, u32[]{:S(2)}, u32[]{:S(2)}) collective-permute-start(bf16[1024,256]{1,0:T(8,128)(2,1)} %collective-permute-done.2.refs_3_), channel_id=1, source_target_pairs={{0,1},{1,2},{2,3},{3,4},{4,5},{5,6},{6,7},{7,0},{8,9},{9,10},{10,1... | collective-permute-start | bytes 1572872 | tf_op jit(solution)/shard_map/ppermute | solution.py:172
  98.8 24.0 %collective-permute-start.6 = (bf16[1024,256]{1,0:T(8,128)(2,1)}, bf16[1024,256]{1,0:T(8,128)(2,1)}, u32[]{:S(2)}, u32[]{:S(2)}) collective-permute-start(bf16[1024,256]{1,0:T(8,128)(2,1)} %collective-permute-done.5.refs_4_), channel_id=1, source_target_pairs={{0,7},{1,0},{2,1},{3,2},{4,3},{5,4},{6,5},{7,6},{8,15},{9,8},{10,9... | collective-permute-start | bytes 1572872 | tf_op jit(solution)/shard_map/ppermute | solution.py:172
  108.1 22.5 %collective-permute-start.9 = (bf16[1024,256]{1,0:T(8,128)(2,1)}, bf16[1024,256]{1,0:T(8,128)(2,1)}, u32[]{:S(2)}, u32[]{:S(2)}) collective-permute-start(bf16[1024,256]{1,0:T(8,128)(2,1)} %collective-permute-done.8.refs_8_.refs_11_), channel_id=1, source_target_pairs={{0,1},{1,2},{2,3},{3,4},{4,5},{5,6},{6,7},{7,0},{8,9},{9,10},{10,1... | collective-permute-start | bytes 1572872 | tf_op jit(solution)/shard_map/ppermute | solution.py:172
  110.1 21.4 %collective-permute-start.12 = (bf16[1024,256]{1,0:T(8,128)(2,1)}, bf16[1024,256]{1,0:T(8,128)(2,1)}, u32[]{:S(2)}, u32[]{:S(2)}) collective-permute-start(bf16[1024,256]{1,0:T(8,128)(2,1)} %collective-permute-done.11.refs_9_.refs_12_), channel_id=1, source_target_pairs={{0,7},{1,0},{2,1},{3,2},{4,3},{5,4},{6,5},{7,6},{8,15},{9,8},{10,9... | collective-permute-start | bytes 1572872 | tf_op jit(solution)/shard_map/ppermute | solution.py:172
  120.6 0.9 copy-start.14
  121.5 10.0 %copy-start = (bf16[1,176,2048]{2,1,0:T(8,128)(2,1)S(1)}, bf16[1,176,2048]{2,1,0:T(8,128)(2,1)}, u32[]{:S(2)}) copy-start(bf16[1,176,2048]{2,1,0:T(8,128)(2,1)} %param.14) | copy-start | bytes 2162692
  121.5 10.0 %copy-start.1 = (bf16[1,176,2048]{2,1,0:T(8,128)(2,1)S(1)}, bf16[1,176,2048]{2,1,0:T(8,128)(2,1)}, u32[]{:S(2)}) copy-start(bf16[1,176,2048]{2,1,0:T(8,128)(2,1)} %param.15) | copy-start | bytes 2162692
  122.8 12.9 %copy-start.3 = (bf16[1024,256]{1,0:T(8,128)(2,1)}, bf16[1024,256]{1,0:T(8,128)(2,1)S(1)}, u32[]{:S(2)}) copy-start(bf16[1024,256]{1,0:T(8,128)(2,1)S(1)} %get-tuple-element.30.refs_5_.refs_15_) | copy-start | bytes 1572868
  122.8 12.9 %copy-start.4 = (bf16[1024,256]{1,0:T(8,128)(2,1)}, bf16[1024,256]{1,0:T(8,128)(2,1)S(1)}, u32[]{:S(2)}) copy-start(bf16[1024,256]{1,0:T(8,128)(2,1)S(1)} %get-tuple-element.31.refs_2_.refs_7_) | copy-start | bytes 1572868
  135.8 1.3 copy-start.15
  135.8 68.6 %copy-start.2 = (bf16[352,1024]{1,0:T(8,128)(2,1)}, bf16[352,1024]{1,0:T(8,128)(2,1)S(1)}, u32[]{:S(2)}) copy-start(bf16[352,1024]{1,0:T(8,128)(2,1)S(1)} %get-tuple-element.25.refs_16_) | copy-start | bytes 2162692
  137.1 15.5 %collective-permute-start.16 = (bf16[1024,256]{1,0:T(8,128)(2,1)}, bf16[1024,256]{1,0:T(8,128)(2,1)}, u32[]{:S(2)}, u32[]{:S(2)}) collective-permute-start(bf16[1024,256]{1,0:T(8,128)(2,1)} %convolution_convert_fusion.1), channel_id=1, source_target_pairs={{0,7},{1,0},{2,1},{3,2},{4,3},{5,4},{6,5},{7,6},{8,15},{9,8},{10,9... | collective-permute-start | bytes 1572872 | tf_op jit(solution)/shard_map/ppermute | solution.py:172
  143.7 16.5 %collective-permute-start.13 = (bf16[1024,256]{1,0:T(8,128)(2,1)}, bf16[1024,256]{1,0:T(8,128)(2,1)}, u32[]{:S(2)}, u32[]{:S(2)}) collective-permute-start(bf16[1024,256]{1,0:T(8,128)(2,1)} %convolution_convert_fusion.2), channel_id=1, source_target_pairs={{0,1},{1,2},{2,3},{3,4},{4,5},{5,6},{6,7},{7,0},{8,9},{9,10},{10,1... | collective-permute-start | bytes 1572872 | tf_op jit(solution)/shard_map/ppermute | solution.py:172
  154.9 23.8 %collective-permute-start.17 = (bf16[1024,256]{1,0:T(8,128)(2,1)}, bf16[1024,256]{1,0:T(8,128)(2,1)}, u32[]{:S(2)}, u32[]{:S(2)}) collective-permute-start(bf16[1024,256]{1,0:T(8,128)(2,1)} %fusion.4), channel_id=1, source_target_pairs={{0,7},{1,0},{2,1},{3,2},{4,3},{5,4},{6,5},{7,6},{8,15},{9,8},{10,9... | collective-permute-start | bytes 1572872 | tf_op jit(solution)/shard_map/ppermute | solution.py:172
  162.6 23.5 %collective-permute-start.14 = (bf16[1024,256]{1,0:T(8,128)(2,1)}, bf16[1024,256]{1,0:T(8,128)(2,1)}, u32[]{:S(2)}, u32[]{:S(2)}) collective-permute-start(bf16[1024,256]{1,0:T(8,128)(2,1)} %fusion.2), channel_id=1, source_target_pairs={{0,1},{1,2},{2,3},{3,4},{4,5},{5,6},{6,7},{7,0},{8,9},{9,10},{10,1... | collective-permute-start | bytes 1572872 | tf_op jit(solution)/shard_map/ppermute | solution.py:172
  165.8 41.3 %all-to-all-start.3 = ((bf16[64,16,256]{2,1,0:T(8,128)(2,1)}), bf16[64,16,256]{2,1,0:T(8,128)(2,1)}, u32[]{:S(2)}, u32[]{:S(2)}) async-start(bf16[64,16,256]{2,1,0:T(8,128)(2,1)} %bitcast.55), calls=%async_computation.3 | async-start | bytes 1048576 | tf_op jit(solution)/shard_map/all_to_all | solution.py:176
  181.0 15.9 %collective-permute-start.18 = (bf16[1024,256]{1,0:T(8,128)(2,1)}, bf16[1024,256]{1,0:T(8,128)(2,1)}, u32[]{:S(2)}, u32[]{:S(2)}) collective-permute-start(bf16[1024,256]{1,0:T(8,128)(2,1)} %fusion.5), channel_id=1, source_target_pairs={{0,7},{1,0},{2,1},{3,2},{4,3},{5,4},{6,5},{7,6},{8,15},{9,8},{10,9... | collective-permute-start | bytes 1572872 | tf_op jit(solution)/shard_map/ppermute | solution.py:172
  188.4 16.1 %collective-permute-start.15 = (bf16[1024,256]{1,0:T(8,128)(2,1)}, bf16[1024,256]{1,0:T(8,128)(2,1)}, u32[]{:S(2)}, u32[]{:S(2)}) collective-permute-start(bf16[1024,256]{1,0:T(8,128)(2,1)} %fusion.3), channel_id=1, source_target_pairs={{0,1},{1,2},{2,3},{3,4},{4,5},{5,6},{6,7},{7,0},{8,9},{9,10},{10,1... | collective-permute-start | bytes 1572872 | tf_op jit(solution)/shard_map/ppermute | solution.py:172
  207.0 17.5 %copy-start.21 = (s32[8]{0:T(128)S(1)}, s32[8]{0:T(128)}, u32[]{:S(2)}) copy-start(s32[8]{0:T(128)} %constant.58.clone) | copy-start | bytes 100
  207.0 17.6 %copy-start.5 = (bf16[1024,256]{1,0:T(8,128)(2,1)S(1)}, bf16[1024,256]{1,0:T(8,128)(2,1)}, u32[]{:S(2)}) copy-start(bf16[1024,256]{1,0:T(8,128)(2,1)} %copy-done.4) | copy-start | bytes 1572868
  207.0 17.6 %copy-start.7 = (bf16[1024,256]{1,0:T(8,128)(2,1)S(1)}, bf16[1024,256]{1,0:T(8,128)(2,1)}, u32[]{:S(2)}) copy-start(bf16[1024,256]{1,0:T(8,128)(2,1)} %copy-done.6) | copy-start | bytes 1572868
  207.0 17.6 %copy-start.9 = (bf16[1024,256]{1,0:T(8,128)(2,1)S(1)}, bf16[1024,256]{1,0:T(8,128)(2,1)}, u32[]{:S(2)}) copy-start(bf16[1024,256]{1,0:T(8,128)(2,1)} %copy-done.8) | copy-start | bytes 1572868
  207.0 29.6 %all-to-all-start.2 = ((bf16[64,16,256]{2,1,0:T(8,128)(2,1)}), bf16[64,16,256]{2,1,0:T(8,128)(2,1)}, u32[]{:S(2)}, u32[]{:S(2)}) async-start(bf16[64,16,256]{2,1,0:T(8,128)(2,1)} %bitcast.56), calls=%async_computation.2 | async-start | bytes 1048576 | tf_op jit(solution)/shard_map/all_to_all | solution.py:176
  220.3 13.6 %collective-permute-start.19 = (bf16[128,256]{1,0:T(8,128)(2,1)S(1)}, bf16[128,256]{1,0:T(8,128)(2,1)S(1)}, u32[]{:S(2)}, u32[]{:S(2)}) collective-permute-start(bf16[128,256]{1,0:T(8,128)(2,1)S(1)} %convolution_convert_fusion.3), channel_id=1, source_target_pairs={{0,4},{1,5},{2,6},{3,7},{4,0},{5,1},{6,2},{7,3},{8,12},{9,13},{10,... | collective-permute-start | bytes 196616 | tf_op jit(solution)/shard_map/ppermute | solution.py:172
  224.6 1.0 copy-start.11
  225.6 1.0 copy-start.13
  226.7 1.0 copy-start.16

commit v2 on v1

v2 whole, which is shorter than its diff:
```python
import jax
import jax.numpy as jnp
import numpy as np
from jax import lax
from jax.experimental import pallas as pl
from jax.experimental.pallas import tpu as pltpu
from jax.sharding import PartitionSpec as P

VMEM = pl.BlockSpec(memory_space=pltpu.VMEM)
SMEM = pl.BlockSpec(memory_space=pltpu.SMEM)
PARAMS = pltpu.CompilerParams(vmem_limit_bytes=48 * 1024 * 1024)


def nt(left, right):
    return lax.dot_general(left, right, (((1,), (1,)), ((), ())), preferred_element_type=jnp.float32)


def tn(left, right):
    return lax.dot_general(left, right, (((0,), (0,)), ((), ())), preferred_element_type=jnp.float32)


def nn(left, right):
    return jnp.dot(left, right, preferred_element_type=jnp.float32)


def dispatch(ids, gates, pieces, experts, slots):
    top, tokens = ids.shape
    count = experts * slots
    widths = [piece.shape[1] for piece, _ in pieces]
    scaled = [flag for _, flag in pieces]

    def kernel(ids_ref, gates_ref, *refs):
        rows_ref, place_ref = refs[-2:]
        ids = ids_ref[...]
        gates = gates_ref[...]
        expert = lax.broadcasted_iota(jnp.int32, (experts, tokens), 0)
        named = jnp.zeros((experts, tokens), jnp.float32)
        gate = jnp.zeros((experts, tokens), jnp.float32)
        for k in range(top):
            hit = ids[k : k + 1, :] == expert
            named = jnp.where(hit, 1.0, named)
            gate = jnp.where(hit, gates[k : k + 1, :], gate)
        earlier = (
            lax.broadcasted_iota(jnp.int32, (tokens, tokens), 0)
            < lax.broadcasted_iota(jnp.int32, (tokens, tokens), 1)
        ).astype(jnp.float32)
        before = nn(named.astype(jnp.bfloat16), earlier.astype(jnp.bfloat16))
        slot = jnp.where(named > 0.0, before, -1.0)
        shape = (experts, slots, tokens)
        wanted = lax.broadcasted_iota(jnp.int32, shape, 1).astype(jnp.float32)
        match = jnp.broadcast_to(slot[:, None, :], shape) == wanted
        scale = jnp.where(match, jnp.broadcast_to(gate[:, None, :], shape), 0.0)
        scale = jnp.sum(scale.reshape(count, tokens), axis=1, keepdims=True)
        place = match.astype(jnp.float32).reshape(count, tokens).astype(jnp.bfloat16)
        place_ref[...] = place
        at = 0
        for k, ref in enumerate(refs[:-2]):
            rows = nn(place, ref[...])
            if scaled[k]:
                rows = scale * rows
            rows_ref[:, at : at + widths[k]] = rows.astype(jnp.bfloat16)
            at += widths[k]

    return pl.pallas_call(
        kernel,
        out_shape=(
            jax.ShapeDtypeStruct((count, sum(widths)), jnp.bfloat16),
            jax.ShapeDtypeStruct((count, tokens), jnp.bfloat16),
        ),
        in_specs=[VMEM] * (2 + len(pieces)),
        out_specs=(VMEM, VMEM),
        compiler_params=PARAMS,
        name="dispatch",
    )(ids, gates, *[piece for piece, _ in pieces])


def gathered(terms):
    arrays, table = [], []
    for array, column, owner in terms:
        known = [k for k, other in enumerate(arrays) if other is array]
        if not known:
            arrays.append(array)
        table.append((known[0] if known else len(arrays) - 1, column, owner))
    return arrays, table


def first_products(me, ring, width, features, cotangents, weights):
    arrays, table = gathered(features + cotangents)
    rows = arrays[0].shape[0]
    units = weights[0].shape[0]

    def kernel(me_ref, *refs):
        w_gate, w_up, w_down, a_ref, b_ref, dh_ref = refs[len(arrays) :]
        for k, (number, column, owner) in enumerate(table):
            block = refs[number][:, column : column + width]
            start = lax.rem(me_ref[0] + owner % ring, ring) * width
            part = pl.ds(pl.multiple_of(start, width), width)
            if k == 0:
                a_ref[...], b_ref[...] = nt(w_gate[:, part], block), nt(w_up[:, part], block)
            elif k < len(features):
                a_ref[...] += nt(w_gate[:, part], block)
                b_ref[...] += nt(w_up[:, part], block)
            elif k == len(features):
                dh_ref[...] = nt(w_down[:, part], block)
            else:
                dh_ref[...] += nt(w_down[:, part], block)

    return pl.pallas_call(
        kernel,
        out_shape=[jax.ShapeDtypeStruct((units, rows), jnp.float32)] * 3,
        in_specs=[SMEM] + [VMEM] * (len(arrays) + 3),
        out_specs=[VMEM] * 3,
        compiler_params=PARAMS,
        name="first_products",
    )(me, *arrays, *weights)


def activations(me, ring, width, features, cotangents, weights, sums):
    arrays, table = gathered(features + cotangents)
    rows = arrays[0].shape[0]
    units = weights[0].shape[0]

    def kernel(me_ref, *refs):
        w_gate, w_up, w_down, a_ref, b_ref, dh_ref, grads_ref, hidden_ref = refs[len(arrays) :]
        a, b, dh = a_ref[...], b_ref[...], dh_ref[...]
        for k, (number, column, owner) in enumerate(table):
            block = refs[number][:, column : column + width]
            start = lax.rem(me_ref[0] + owner % ring, ring) * width
            part = pl.ds(pl.multiple_of(start, width), width)
            if k < len(features):
                a += nt(w_gate[:, part], block)
                b += nt(w_up[:, part], block)
            else:
                dh += nt(w_down[:, part], block)
        s = jax.nn.sigmoid(a)
        swish = a * s
        hidden_ref[...] = (swish * b).astype(jnp.bfloat16)
        grads_ref[:units, :] = (dh * b * s * (1.0 + a * (1.0 - s))).astype(jnp.bfloat16)
        grads_ref[units:, :] = (dh * swish).astype(jnp.bfloat16)

    return pl.pallas_call(
        kernel,
        out_shape=(
            jax.ShapeDtypeStruct((2 * units, rows), jnp.bfloat16),
            jax.ShapeDtypeStruct((units, rows), jnp.bfloat16),
        ),
        in_specs=[SMEM] + [VMEM] * (len(arrays) + 6),
        out_specs=(VMEM, VMEM),
        compiler_params=PARAMS,
        name="activations",
    )(me, *arrays, *weights, *sums)


def weight_grads(me, ring, width, features, cotangents, grads, hidden):
    arrays, table = gathered(features + cotangents)
    units = hidden.shape[0]

    def kernel(me_ref, *refs):
        grads_ref, hidden_ref, gate_ref, up_ref, down_ref = refs[len(arrays) :]
        for k, (number, column, owner) in enumerate(table):
            block = refs[number][:, column : column + width]
            start = lax.rem(me_ref[0] + owner % ring, ring) * width
            part = pl.ds(pl.multiple_of(start, width), width)
            if k < len(features):
                both = nn(grads_ref[...], block).astype(jnp.bfloat16)
                gate_ref[:, part] = both[:units]
                up_ref[:, part] = both[units:]
            else:
                down_ref[:, part] = nn(hidden_ref[...], block).astype(jnp.bfloat16)

    return pl.pallas_call(
        kernel,
        out_shape=[jax.ShapeDtypeStruct((units, ring * width), jnp.bfloat16)] * 3,
        in_specs=[SMEM] + [VMEM] * (len(arrays) + 2),
        out_specs=[VMEM] * 3,
        compiler_params=PARAMS,
        name="weight_grads",
    )(me, *arrays, grads, hidden)


def local(tokens, cotangent, expert_ids, gate_values, w_gate, w_up, w_down):
    groups = lax.axis_size("ep")
    ring = lax.axis_size("tp")
    half = ring // 2
    near = half - 1
    tok_count, top_count = expert_ids.shape
    slots = max(2, tok_count * top_count * 4 // (groups * 3))
    width = tokens.shape[1]
    rows = groups * slots
    me = lax.axis_index("tp").astype(jnp.int32)
    me_ref = me.reshape(1)
    weights = (w_gate[0], w_up[0], w_down[0])

    def moved(value, by):
        return lax.ppermute(value, "tp", [(i, (i + by) % ring) for i in range(ring)])

    def over_ep(value):
        shape = (groups, slots, value.shape[1])
        value = lax.all_to_all(value.reshape(shape), "ep", split_axis=0, concat_axis=0, tiled=True)
        return value.reshape(rows, -1)

    ids, gates = expert_ids.T, gate_values.T
    sent, place = dispatch(ids, gates, [(tokens, False), (cotangent, True)], groups, slots)
    far_tokens, far_cot, sent = lax.optimization_barrier((tokens, cotangent, sent))
    mine = over_ep(sent)
    far_both = moved(jnp.concatenate([far_tokens, far_cot], axis=1), half)
    side_tokens = moved(far_tokens, -near)
    side_cot = moved(far_cot, near)
    far_sent, _ = dispatch(
        ids,
        gates,
        [
            (far_both[:, :width], False),
            (far_both[:, width:], True),
            (side_tokens, False),
            (side_cot, True),
        ],
        groups,
        slots,
    )
    x0, g0 = mine[:, :width], mine[:, width:]
    x0, g0, far_sent = lax.optimization_barrier((x0, g0, far_sent))
    x, g = {0: x0}, {0: g0}
    for step in range(1, near):
        for blocks in (x, g):
            blocks[-step] = moved(blocks[1 - step], 1)
            blocks[step] = moved(blocks[step - 1], -1)
    x[-near] = moved(x[1 - near], 1)
    g[near] = moved(g[near - 1], -1)
    far = over_ep(far_sent)

    early = [d for step in range(near) for d in ([-step, step] if step else [0])]
    early_x, early_g = [(x[d], 0, d) for d in early], [(g[d], 0, d) for d in early]
    late_x = [(far, 0, half), (far, 2 * width, near), (x[-near], 0, -near)]
    late_g = [(far, width, half), (far, 3 * width, -near), (g[near], 0, near)]
    sums = first_products(me_ref, ring, width, early_x, early_g, weights)
    grads, hidden = activations(me_ref, ring, width, late_x, late_g, weights, sums)

    paired = jnp.concatenate(weights[:2], axis=0)

    def columns(d):
        start = lax.rem(me + d % ring, np.int32(ring)) * width
        return lax.dynamic_slice_in_dim(paired, start, width, axis=1)

    def partial(d):
        return lax.optimization_barrier(tn(grads, columns(d)).astype(jnp.bfloat16))

    def added(*values):
        return sum(value.astype(jnp.float32) for value in values)

    away = [half, near, -near]
    right, left = partial(near - 1), partial(1 - near)
    side = jnp.concatenate([columns(d) for d in away], axis=1)
    far_back = over_ep(tn(grads, side).astype(jnp.bfloat16))
    for d in range(near - 2, -1, -1):
        right, left = moved(right, 1), moved(left, -1)
        if d:
            right = added(right, partial(d)).astype(jnp.bfloat16)
            left = added(left, partial(-d)).astype(jnp.bfloat16)
    back = over_ep(added(partial(0), right, left).astype(jnp.bfloat16))

    grad_gate, grad_up, grad_down = weight_grads(
        me_ref, ring, width, early_x + late_x, early_g + late_g, grads, hidden
    )
    sides = tn(place, far_back).astype(jnp.bfloat16)
    sides = [moved(sides[:, k * width : (k + 1) * width], d) for k, d in enumerate(away)]
    input_grad = (tn(place, back) + added(*sides)).astype(jnp.bfloat16)
    return (input_grad, grad_gate[None], grad_up[None], grad_down[None])


def solution(mesh):
    in_specs = (
        P("ep", "tp"),
        P("ep", "tp"),
        P("ep", None),
        P("ep", None),
        P("ep", "tp", None),
        P("ep", "tp", None),
        P("ep", "tp", None),
    )
    out_specs = (P("ep", "tp"), P("ep", "tp", None), P("ep", "tp", None), P("ep", "tp", None))
    return jax.shard_map(local, mesh=mesh, in_specs=in_specs, out_specs=out_specs, check_vma=False)
```

time: 240 us -> 215 us (0.90)
  waiting for transfers between devices: 65.6 us -> 47.4 us
  matrix products: 19 us -> 7.46 us
  other arithmetic: 0.03 us -> 4.9 us
    all_to_all x4, waiting for transfers between devices: 14.9 us -> 0.37 us  [over_ep(): lax.all_to_all(value.reshape(shape), 'ep', split_axis=0, concat_axis=0, t...]
    dot_general x10 -> x8, matrix products: 19 us -> 7.46 us  [tn(): lax.dot_general(left, right, (((0,), (0,)), ((), ())), preferred_element_...]
    convert_element_type x0 -> x3, other arithmetic: none -> 4.04 us  [the longest x1 2.19 us: local(): back = over_ep(added(partial(0), right, left).astype(jnp.bfloat16))]
    ppermute x20, waiting for transfers between devices: 50.7 us -> 47.1 us  [moved(): lax.ppermute(value, 'tp', [(i, (i + by) % ring) for i in range(ring)])]
    unnamed x49 -> x54, local copies, waits for them, and re-layouts: 6.21 us -> 9.46 us
    ppermute x20, starting transfers between devices: 81.3 us -> 78.1 us  [moved(): lax.ppermute(value, 'tp', [(i, (i + by) % ring) for i in range(ring)])]
    all_to_all x4, starting transfers between devices: 43.2 us -> 45.8 us  [over_ep(): lax.all_to_all(value.reshape(shape), 'ep', split_axis=0, concat_axis=0, t...]
  transfers between devices with their start and end apart: 24 -> 24, of which waited for: 12 -> 13; matrix products, arithmetic and copies ran while one was open for 7% -> 4% of each run, Pallas kernels for 6% -> 6%
where the time goes in v2:
time: 215 us; the launch traced here: 214 us
  starting transfers between devices  124 us (58%)
  waiting for transfers between devices  47.4 us (22%)
  Pallas kernels  19.4 us (9%)
  local copies, waits for them, and re-layouts  9.56 us (4%)
  matrix products  7.46 us (3%)
  other arithmetic  4.9 us (2%)
    ppermute x20, starting transfers between devices, moved(): lax.ppermute(value, 'tp', [(i, (i + by) % ring) for i in range(ring)])  78.1 us
    ppermute x20, waiting for transfers between devices, moved(): lax.ppermute(value, 'tp', [(i, (i + by) % ring) for i in range(ring)])  47.1 us
    all_to_all x4, starting transfers between devices, over_ep(): lax.all_to_all(value.reshape(shape), 'ep', split_axis=0, concat_axis=0, t...  45.8 us
    unnamed x54, local copies, waits for them, and re-layouts  9.46 us
    dot_general x8, matrix products, tn(): lax.dot_general(left, right, (((0,), (0,)), ((), ())), preferred_element_...  7.46 us
    pallas_call x1, Pallas kernels, weight_grads(): pl.pallas_call(kernel, out_shape=[jax.ShapeDtypeStruct((units, ring * wid...  6.38 us
    pallas_call x1, Pallas kernels, first_products(): pl.pallas_call(kernel, out_shape=[jax.ShapeDtypeStruct((units, rows), jnp...  6.16 us
  transfers between devices with their start and end apart: 24, of which 13 were waited for; matrix products, arithmetic and copies ran while one was open for 4% of the time, Pallas kernels for 6%

profile of v2, /device:TPU:1, one launch (start us, length us, event | category | flops | bytes accessed | tf_op | source)
XLA Modules:
  0.0 213.9 jit_solution(9195981713047532458)
XLA Ops:
  3.7 1.6 dispatch.2
  5.3 11.6 %all-to-all-start = ((bf16[64,16,512]{2,1,0:T(8,128)(2,1)}), bf16[64,16,512]{2,1,0:T(8,128)(2,1)S(1)}, u32[]{:S(2)}, u32[]{:S(2)}) async-start(bf16[64,16,512]{2,1,0:T(8,128)(2,1)} %bitcast.3), calls=%async_computation | async-start | bytes 2097152 | tf_op jit(solution)/shard_map/all_to_all | solution.py:199
  17.0 10.6 %collective-permute-start = (bf16[128,512]{1,0:T(8,128)(2,1)S(1)}, bf16[128,512]{1,0:T(8,128)(2,1)S(1)}, u32[]{:S(2)}, u32[]{:S(2)}) collective-permute-start(bf16[128,512]{1,0:T(8,128)(2,1)S(1)} %pad_maximum_fusion), channel_id=1, source_target_pairs={{0,4},{1,5},{2,6},{3,7},{4,0},{5,1},{6,2},{7,3},{8,12},{9,13},{10,... | collective-permute-start | bytes 393224 | tf_op jit(solution)/shard_map/ppermute | solution.py:195
  27.7 1.9 collective-permute-start.1
  29.6 5.2 %collective-permute-start.2 = (bf16[128,256]{1,0:T(8,128)(2,1)S(1)}, bf16[128,256]{1,0:T(8,128)(2,1)S(1)}, u32[]{:S(2)}, u32[]{:S(2)}) collective-permute-start(bf16[128,256]{1,0:T(8,128)(2,1)S(1)} %copy-done.20), channel_id=1, source_target_pairs={{0,3},{1,4},{2,5},{3,6},{4,7},{5,0},{6,1},{7,2},{8,11},{9,12},{10,... | collective-permute-start | bytes 196616 | tf_op jit(solution)/shard_map/ppermute | solution.py:195
  34.8 2.4 %collective-permute-done.1.refs_2_ = bf16[128,256]{1,0:T(8,128)(2,1)S(1)} collective-permute-done((bf16[128,256]{1,0:T(8,128)(2,1)S(1)}, bf16[128,256]{1,0:T(8,128)(2,1)S(1)}, u32[]{:S(2)}, u32[]{:S(2)}) %collective-permute-start.1) | collective-permute-done | bytes 65568 | tf_op jit(solution)/shard_map/ppermute | solution.py:195
  37.2 5.0 %collective-permute-done.2.refs_3_ = bf16[128,256]{1,0:T(8,128)(2,1)S(1)} collective-permute-done((bf16[128,256]{1,0:T(8,128)(2,1)S(1)}, bf16[128,256]{1,0:T(8,128)(2,1)S(1)}, u32[]{:S(2)}, u32[]{:S(2)}) %collective-permute-start.2) | collective-permute-done | bytes 65568 | tf_op jit(solution)/shard_map/ppermute | solution.py:195
  42.2 1.2 dispatch.3
  43.4 1.4 copy-done.11
  45.1 10.6 %all-to-all-start.1 = ((bf16[64,16,1024]{2,1,0:T(8,128)(2,1)}), bf16[64,16,1024]{2,1,0:T(8,128)(2,1)}, u32[]{:S(2)}, u32[]{:S(2)}) async-start(bf16[64,16,1024]{2,1,0:T(8,128)(2,1)} %bitcast.45), calls=%async_computation.1 | async-start | bytes 4194304 | tf_op jit(solution)/shard_map/all_to_all | solution.py:199
  55.7 3.3 %collective-permute-start.3 = (bf16[1024,256]{1,0:T(8,128)(2,1)S(1)}, bf16[1024,256]{1,0:T(8,128)(2,1)S(1)}, u32[]{:S(2)}, u32[]{:S(2)}) collective-permute-start(bf16[1024,256]{1,0:T(8,128)(2,1)S(1)} %get-tuple-element.28.refs_0_), channel_id=1, source_target_pairs={{0,1},{1,2},{2,3},{3,4},{4,5},{5,6},{6,7},{7,0},{8,9},{9,10},{10,1... | collective-permute-start | bytes 1572872 | tf_op jit(solution)/shard_map/ppermute | solution.py:195
  59.0 5.5 %collective-permute-start.6 = (bf16[1024,256]{1,0:T(8,128)(2,1)S(1)}, bf16[1024,256]{1,0:T(8,128)(2,1)S(1)}, u32[]{:S(2)}, u32[]{:S(2)}) collective-permute-start(bf16[1024,256]{1,0:T(8,128)(2,1)S(1)} %get-tuple-element.29.refs_5_.refs_7_), channel_id=1, source_target_pairs={{0,7},{1,0},{2,1},{3,2},{4,3},{5,4},{6,5},{7,6},{8,15},{9,8},{10,9... | collective-permute-start | bytes 1572872 | tf_op jit(solution)/shard_map/ppermute | solution.py:195
  64.5 3.4 %collective-permute-start.9 = (bf16[1024,256]{1,0:T(8,128)(2,1)S(1)}, bf16[1024,256]{1,0:T(8,128)(2,1)}, u32[]{:S(2)}, u32[]{:S(2)}) collective-permute-start(bf16[1024,256]{1,0:T(8,128)(2,1)S(1)} %get-tuple-element.28.refs_0_), channel_id=1, source_target_pairs={{0,7},{1,0},{2,1},{3,2},{4,3},{5,4},{6,5},{7,6},{8,15},{9,8},{10,9... | collective-permute-start | bytes 1572872 | tf_op jit(solution)/shard_map/ppermute | solution.py:195
  67.8 1.9 collective-permute-start.11
  69.8 4.7 %collective-permute-done.3.refs_1_ = bf16[1024,256]{1,0:T(8,128)(2,1)S(1)} collective-permute-done((bf16[1024,256]{1,0:T(8,128)(2,1)S(1)}, bf16[1024,256]{1,0:T(8,128)(2,1)S(1)}, u32[]{:S(2)}, u32[]{:S(2)}) %collective-permute-start.3) | collective-permute-done | bytes 524320 | tf_op jit(solution)/shard_map/ppermute | solution.py:195
  74.4 1.9 collective-permute-start.4
  76.4 4.6 %collective-permute-start.7 = (bf16[1024,256]{1,0:T(8,128)(2,1)S(1)}, bf16[1024,256]{1,0:T(8,128)(2,1)}, u32[]{:S(2)}, u32[]{:S(2)}) collective-permute-start(bf16[1024,256]{1,0:T(8,128)(2,1)S(1)} %collective-permute-done.6.refs_7_.refs_9_), channel_id=1, source_target_pairs={{0,7},{1,0},{2,1},{3,2},{4,3},{5,4},{6,5},{7,6},{8,15},{9,8},{10,9... | collective-permute-start | bytes 1572872 | tf_op jit(solution)/shard_map/ppermute | solution.py:195
  81.7 4.7 %collective-permute-done.9.refs_2_ = bf16[1024,256]{1,0:T(8,128)(2,1)} collective-permute-done((bf16[1024,256]{1,0:T(8,128)(2,1)S(1)}, bf16[1024,256]{1,0:T(8,128)(2,1)}, u32[]{:S(2)}, u32[]{:S(2)}) %collective-permute-start.9) | collective-permute-done | bytes 524320 | tf_op jit(solution)/shard_map/ppermute | solution.py:195
  86.4 5.4 %collective-permute-start.10 = (bf16[1024,256]{1,0:T(8,128)(2,1)}, bf16[1024,256]{1,0:T(8,128)(2,1)}, u32[]{:S(2)}, u32[]{:S(2)}) collective-permute-start(bf16[1024,256]{1,0:T(8,128)(2,1)} %collective-permute-done.9.refs_2_), channel_id=1, source_target_pairs={{0,7},{1,0},{2,1},{3,2},{4,3},{5,4},{6,5},{7,6},{8,15},{9,8},{10,9... | collective-permute-start | bytes 1572872 | tf_op jit(solution)/shard_map/ppermute | solution.py:195
  91.9 1.9 collective-permute-start.12
  93.8 3.1 %collective-permute-done.4.refs_3_ = bf16[1024,256]{1,0:T(8,128)(2,1)} collective-permute-done((bf16[1024,256]{1,0:T(8,128)(2,1)S(1)}, bf16[1024,256]{1,0:T(8,128)(2,1)}, u32[]{:S(2)}, u32[]{:S(2)}) %collective-permute-start.4) | collective-permute-done | bytes 524320 | tf_op jit(solution)/shard_map/ppermute | solution.py:195
  96.9 1.9 collective-permute-start.5
  98.8 4.6 %collective-permute-start.8 = (bf16[1024,256]{1,0:T(8,128)(2,1)}, bf16[1024,256]{1,0:T(8,128)(2,1)}, u32[]{:S(2)}, u32[]{:S(2)}) collective-permute-start(bf16[1024,256]{1,0:T(8,128)(2,1)} %collective-permute-done.7.refs_9_.refs_11_), channel_id=1, source_target_pairs={{0,7},{1,0},{2,1},{3,2},{4,3},{5,4},{6,5},{7,6},{8,15},{9,8},{10,9... | collective-permute-start | bytes 1572872 | tf_op jit(solution)/shard_map/ppermute | solution.py:195
  104.3 4.7 %collective-permute-done.10.refs_4_ = bf16[1024,256]{1,0:T(8,128)(2,1)} collective-permute-done((bf16[1024,256]{1,0:T(8,128)(2,1)}, bf16[1024,256]{1,0:T(8,128)(2,1)}, u32[]{:S(2)}, u32[]{:S(2)}) %collective-permute-start.10) | collective-permute-done | bytes 524320 | tf_op jit(solution)/shard_map/ppermute | solution.py:195
  109.0 6.2 %first_products.1 = (f32[176,1024]{1,0:T(8,128)S(1)}, f32[176,1024]{1,0:T(8,128)}, f32[176,1024]{1,0:T(8,128)}) custom-call(s32[1]{0:T(128)} %bitcast.2.me_ref, bf16[1024,256]{1,0:T(8,128)(2,1)S(1)} %get-tuple-element.28.refs_0_, bf16[1024,256]{1,0:T(8,128)(2,1)S(1)} %collective-permute-done.3.refs_1_, bf16[1024,256]{1,0:T(8,128)(2,1)} %collective-permute-done.9.refs_2_, ...), custom_call_target="tpu_custom_call" | custom-call | tf_op jit(solution)/shard_map/first_products/pallas_call | solution.py:108
  116.0 1.2 collective-permute-done.5.refs_1_.refs_6_
  117.3 2.9 %collective-permute-done.8.refs_2_.refs_12_ = bf16[1024,256]{1,0:T(8,128)(2,1)} collective-permute-done((bf16[1024,256]{1,0:T(8,128)(2,1)}, bf16[1024,256]{1,0:T(8,128)(2,1)}, u32[]{:S(2)}, u32[]{:S(2)}) %collective-permute-start.8) | collective-permute-done | bytes 524320 | tf_op jit(solution)/shard_map/ppermute | solution.py:195
  120.3 1.1 copy-done.5
  121.4 1.1 copy-done.13
  122.5 1.1 copy-done.14
  123.6 4.0 %activations.1 = (bf16[352,1024]{1,0:T(8,128)(2,1)S(1)}, bf16[176,1024]{1,0:T(8,128)(2,1)S(1)}) custom-call(s32[1]{0:T(128)} %bitcast.2.me_ref, bf16[1024,1024]{1,0:T(8,128)(2,1)} %bitcast.6.refs_0_.refs_5_, bf16[1024,256]{1,0:T(8,128)(2,1)} %collective-permute-done.5.refs_1_.refs_6_, bf16[1024,256]{1,0:T(8,128)(2,1)} %collective-permute-done.8.refs_2_.refs_12_, ...), custom_call_target="tpu_custom_call" | custom-call | tf_op jit(solution)/shard_map/activations/pallas_call | solution.py:141
  127.7 2.2 %convolution_convert_fusion = bf16[1024,768]{1,0:T(8,128)(2,1)} fusion(bf16[352,1024]{1,0:T(8,128)(2,1)S(1)} %get-tuple-element.33.refs_13_, bf16[352,256]{1,0:T(8,128)(2,1)S(1)} %copy-done.26, bf16[352,256]{1,0:T(8,128)(2,1)S(1)} %copy-done.25, bf16[352,256]{1,0:T(8,128)(2,1)S(1)} %copy-done.24), kind=kOutput, calls=%fused_computation.16 | convolution fusion | flops 556056576 | bytes 2834432 | tf_op jit(solution)/shard_map/dot_general | solution.py:19
  129.9 11.5 %all-to-all-start.3 = ((bf16[64,16,768]{2,1,0:T(8,128)(2,1)}), bf16[64,16,768]{2,1,0:T(8,128)(2,1)}, u32[]{:S(2)}, u32[]{:S(2)}) async-start(bf16[64,16,768]{2,1,0:T(8,128)(2,1)} %bitcast.52), calls=%async_computation.3 | async-start | bytes 3145728 | tf_op jit(solution)/shard_map/all_to_all | solution.py:199
  141.9 1.9 collective-permute-start.13
  144.3 5.4 %collective-permute-start.15 = (bf16[1024,256]{1,0:T(8,128)(2,1)S(1)}, bf16[1024,256]{1,0:T(8,128)(2,1)S(1)}, u32[]{:S(2)}, u32[]{:S(2)}) collective-permute-start(bf16[1024,256]{1,0:T(8,128)(2,1)S(1)} %convolution_convert_fusion.2), channel_id=1, source_target_pairs={{0,7},{1,0},{2,1},{3,2},{4,3},{5,4},{6,5},{7,6},{8,15},{9,8},{10,9... | collective-permute-start | bytes 1572872 | tf_op jit(solution)/shard_map/ppermute | solution.py:195
  150.6 8.5 %collective-permute-done.13 = bf16[1024,256]{1,0:T(8,128)(2,1)S(1)} collective-permute-done((bf16[1024,256]{1,0:T(8,128)(2,1)S(1)}, bf16[1024,256]{1,0:T(8,128)(2,1)S(1)}, u32[]{:S(2)}, u32[]{:S(2)}) %collective-permute-start.13) | collective-permute-done | bytes 524320 | tf_op jit(solution)/shard_map/ppermute | solution.py:195
  160.1 2.1 collective-permute-start.14
  162.2 0.9 add_convert_fusion.1
  163.1 4.6 %collective-permute-start.16 = (bf16[1024,256]{1,0:T(8,128)(2,1)}, bf16[1024,256]{1,0:T(8,128)(2,1)}, u32[]{:S(2)}, u32[]{:S(2)}) collective-permute-start(bf16[1024,256]{1,0:T(8,128)(2,1)} %add_convert_fusion.1), channel_id=1, source_target_pairs={{0,7},{1,0},{2,1},{3,2},{4,3},{5,4},{6,5},{7,6},{8,15},{9,8},{10,9... | collective-permute-start | bytes 1572872 | tf_op jit(solution)/shard_map/ppermute | solution.py:195
  168.2 7.8 %collective-permute-done.14 = bf16[1024,256]{1,0:T(8,128)(2,1)} collective-permute-done((bf16[1024,256]{1,0:T(8,128)(2,1)}, bf16[1024,256]{1,0:T(8,128)(2,1)}, u32[]{:S(2)}, u32[]{:S(2)}) %collective-permute-start.14) | collective-permute-done | bytes 524320 | tf_op jit(solution)/shard_map/ppermute | solution.py:195
  175.9 2.0 collective-permute-done.16
  177.9 2.2 %add_convert_fusion = bf16[1024,256]{1,0:T(8,128)(2,1)} fusion(bf16[1024,256]{1,0:T(8,128)(2,1)} %collective-permute-done.16, bf16[1024,256]{1,0:T(8,128)(2,1)} %collective-permute-done.14, bf16[1024,256]{1,0:T(8,128)(2,1)S(1)} %convolution_convert_fusion.5), kind=kLoop, calls=%fused_computation.23 | loop fusion | flops 1572864 | bytes 2097152 | tf_op jit(solution)/shard_map/convert_element_type | solution.py:260
  180.3 12.1 %all-to-all-start.2 = ((bf16[64,16,256]{2,1,0:T(8,128)(2,1)}), bf16[64,16,256]{2,1,0:T(8,128)(2,1)S(1)}, u32[]{:S(2)}, u32[]{:S(2)}) async-start(bf16[64,16,256]{2,1,0:T(8,128)(2,1)} %bitcast.10), calls=%async_computation.2 | async-start | bytes 1048576 | tf_op jit(solution)/shard_map/all_to_all | solution.py:199
  192.4 1.9 convolution_convert_fusion.6
  194.4 4.3 %collective-permute-start.17 = (bf16[128,256]{1,0:T(8,128)(2,1)S(1)}, bf16[128,256]{1,0:T(8,128)(2,1)S(1)}, u32[]{:S(2)}, u32[]{:S(2)}) collective-permute-start(bf16[128,256]{1,0:T(8,128)(2,1)S(1)} %get-tuple-element.43), channel_id=1, source_target_pairs={{0,4},{1,5},{2,6},{3,7},{4,0},{5,1},{6,2},{7,3},{8,12},{9,13},{10,... | collective-permute-start | bytes 196616 | tf_op jit(solution)/shard_map/ppermute | solution.py:195
  198.7 3.7 %collective-permute-start.19 = (bf16[128,256]{1,0:T(8,128)(2,1)S(1)}, bf16[128,256]{1,0:T(8,128)(2,1)S(1)}, u32[]{:S(2)}, u32[]{:S(2)}) collective-permute-start(bf16[128,256]{1,0:T(8,128)(2,1)S(1)} %get-tuple-element.44), channel_id=1, source_target_pairs={{0,5},{1,6},{2,7},{3,0},{4,1},{5,2},{6,3},{7,4},{8,13},{9,14},{10,... | collective-permute-start | bytes 196616 | tf_op jit(solution)/shard_map/ppermute | solution.py:195
  202.4 4.1 %collective-permute-start.18 = (bf16[128,256]{1,0:T(8,128)(2,1)S(1)}, bf16[128,256]{1,0:T(8,128)(2,1)S(1)}, u32[]{:S(2)}, u32[]{:S(2)}) collective-permute-start(bf16[128,256]{1,0:T(8,128)(2,1)S(1)} %get-tuple-element.45), channel_id=1, source_target_pairs={{0,3},{1,4},{2,5},{3,6},{4,7},{5,0},{6,1},{7,2},{8,11},{9,12},{10,... | collective-permute-start | bytes 196616 | tf_op jit(solution)/shard_map/ppermute | solution.py:195
  206.6 6.4 %weight_grads.1 = (bf16[176,2048]{1,0:T(8,128)(2,1)}, bf16[176,2048]{1,0:T(8,128)(2,1)}, bf16[176,2048]{1,0:T(8,128)(2,1)}) custom-call(s32[1]{0:T(128)} %bitcast.2.me_ref, bf16[1024,256]{1,0:T(8,128)(2,1)S(1)} %get-tuple-element.28.refs_0_, bf16[1024,256]{1,0:T(8,128)(2,1)S(1)} %copy-done.7, bf16[1024,256]{1,0:T(8,128)(2,1)} %collective-permute-done.9.refs_2_, ...), custom_call_target="tpu_custom_call" | custom-call | tf_op jit(solution)/shard_map/weight_grads/pallas_call | solution.py:171
  (75 shorter events, 10.4 us)
Async XLA Ops:
  0.6 0.8 copy-start.17
  1.5 0.8 copy-start.19
  3.7 13.3 %copy-start.18 = (bf16[128,256]{1,0:T(8,128)(2,1)S(1)}, bf16[128,256]{1,0:T(8,128)(2,1)}, u32[]{:S(2)}) copy-start(bf16[128,256]{1,0:T(8,128)(2,1)} %refs_0_.1) | copy-start | bytes 196612
  3.7 13.3 %copy-start.20 = (bf16[128,256]{1,0:T(8,128)(2,1)S(1)}, bf16[128,256]{1,0:T(8,128)(2,1)}, u32[]{:S(2)}) copy-start(bf16[128,256]{1,0:T(8,128)(2,1)} %refs_1_.1) | copy-start | bytes 196612
  3.7 38.5 %copy-start.22 = (s32[128,6]{0,1:T(8,128)S(1)}, s32[128,6]{0,1:T(8,128)}, u32[]{:S(2)}) copy-start(s32[128,6]{0,1:T(8,128)} %param.9) | copy-start | bytes 9220
  5.3 39.6 %all-to-all-start = ((bf16[64,16,512]{2,1,0:T(8,128)(2,1)}), bf16[64,16,512]{2,1,0:T(8,128)(2,1)S(1)}, u32[]{:S(2)}, u32[]{:S(2)}) async-start(bf16[64,16,512]{2,1,0:T(8,128)(2,1)} %bitcast.3), calls=%async_computation | async-start | bytes 2097152 | tf_op jit(solution)/shard_map/all_to_all | solution.py:199
  17.0 17.7 %collective-permute-start = (bf16[128,512]{1,0:T(8,128)(2,1)S(1)}, bf16[128,512]{1,0:T(8,128)(2,1)S(1)}, u32[]{:S(2)}, u32[]{:S(2)}) collective-permute-start(bf16[128,512]{1,0:T(8,128)(2,1)S(1)} %pad_maximum_fusion), channel_id=1, source_target_pairs={{0,4},{1,5},{2,6},{3,7},{4,0},{5,1},{6,2},{7,3},{8,12},{9,13},{10,... | collective-permute-start | bytes 393224 | tf_op jit(solution)/shard_map/ppermute | solution.py:195
  27.7 9.6 %collective-permute-start.1 = (bf16[128,256]{1,0:T(8,128)(2,1)S(1)}, bf16[128,256]{1,0:T(8,128)(2,1)S(1)}, u32[]{:S(2)}, u32[]{:S(2)}) collective-permute-start(bf16[128,256]{1,0:T(8,128)(2,1)S(1)} %copy-done.18), channel_id=1, source_target_pairs={{0,5},{1,6},{2,7},{3,0},{4,1},{5,2},{6,3},{7,4},{8,13},{9,14},{10,... | collective-permute-start | bytes 196616 | tf_op jit(solution)/shard_map/ppermute | solution.py:195
  29.6 12.6 %collective-permute-start.2 = (bf16[128,256]{1,0:T(8,128)(2,1)S(1)}, bf16[128,256]{1,0:T(8,128)(2,1)S(1)}, u32[]{:S(2)}, u32[]{:S(2)}) collective-permute-start(bf16[128,256]{1,0:T(8,128)(2,1)S(1)} %copy-done.20), channel_id=1, source_target_pairs={{0,3},{1,4},{2,5},{3,6},{4,7},{5,0},{6,1},{7,2},{8,11},{9,12},{10,... | collective-permute-start | bytes 196616 | tf_op jit(solution)/shard_map/ppermute | solution.py:195
  43.4 1.4 copy-start.11
  45.0 58.4 %copy-start = (bf16[1,176,2048]{2,1,0:T(8,128)(2,1)S(1)}, bf16[1,176,2048]{2,1,0:T(8,128)(2,1)}, u32[]{:S(2)}) copy-start(bf16[1,176,2048]{2,1,0:T(8,128)(2,1)} %param.11) | copy-start | bytes 2162692
  45.0 58.4 %copy-start.2 = (bf16[1,176,2048]{2,1,0:T(8,128)(2,1)S(1)}, bf16[1,176,2048]{2,1,0:T(8,128)(2,1)}, u32[]{:S(2)}) copy-start(bf16[1,176,2048]{2,1,0:T(8,128)(2,1)} %param.12) | copy-start | bytes 2162692
  45.1 75.2 %all-to-all-start.1 = ((bf16[64,16,1024]{2,1,0:T(8,128)(2,1)}), bf16[64,16,1024]{2,1,0:T(8,128)(2,1)}, u32[]{:S(2)}, u32[]{:S(2)}) async-start(bf16[64,16,1024]{2,1,0:T(8,128)(2,1)} %bitcast.45), calls=%async_computation.1 | async-start | bytes 4194304 | tf_op jit(solution)/shard_map/all_to_all | solution.py:199
  55.7 18.8 %collective-permute-start.3 = (bf16[1024,256]{1,0:T(8,128)(2,1)S(1)}, bf16[1024,256]{1,0:T(8,128)(2,1)S(1)}, u32[]{:S(2)}, u32[]{:S(2)}) collective-permute-start(bf16[1024,256]{1,0:T(8,128)(2,1)S(1)} %get-tuple-element.28.refs_0_), channel_id=1, source_target_pairs={{0,1},{1,2},{2,3},{3,4},{4,5},{5,6},{6,7},{7,0},{8,9},{9,10},{10,1... | collective-permute-start | bytes 1572872 | tf_op jit(solution)/shard_map/ppermute | solution.py:195
  59.0 17.4 %collective-permute-start.6 = (bf16[1024,256]{1,0:T(8,128)(2,1)S(1)}, bf16[1024,256]{1,0:T(8,128)(2,1)S(1)}, u32[]{:S(2)}, u32[]{:S(2)}) collective-permute-start(bf16[1024,256]{1,0:T(8,128)(2,1)S(1)} %get-tuple-element.29.refs_5_.refs_7_), channel_id=1, source_target_pairs={{0,7},{1,0},{2,1},{3,2},{4,3},{5,4},{6,5},{7,6},{8,15},{9,8},{10,9... | collective-permute-start | bytes 1572872 | tf_op jit(solution)/shard_map/ppermute | solution.py:195
  64.5 22.0 %collective-permute-start.9 = (bf16[1024,256]{1,0:T(8,128)(2,1)S(1)}, bf16[1024,256]{1,0:T(8,128)(2,1)}, u32[]{:S(2)}, u32[]{:S(2)}) collective-permute-start(bf16[1024,256]{1,0:T(8,128)(2,1)S(1)} %get-tuple-element.28.refs_0_), channel_id=1, source_target_pairs={{0,7},{1,0},{2,1},{3,2},{4,3},{5,4},{6,5},{7,6},{8,15},{9,8},{10,9... | collective-permute-start | bytes 1572872 | tf_op jit(solution)/shard_map/ppermute | solution.py:195
  67.8 24.0 %collective-permute-start.11 = (bf16[1024,256]{1,0:T(8,128)(2,1)S(1)}, bf16[1024,256]{1,0:T(8,128)(2,1)}, u32[]{:S(2)}, u32[]{:S(2)}) collective-permute-start(bf16[1024,256]{1,0:T(8,128)(2,1)S(1)} %get-tuple-element.29.refs_5_.refs_7_), channel_id=1, source_target_pairs={{0,1},{1,2},{2,3},{3,4},{4,5},{5,6},{6,7},{7,0},{8,9},{9,10},{10,1... | collective-permute-start | bytes 1572872 | tf_op jit(solution)/shard_map/ppermute | solution.py:195
  74.4 40.7 %copy-start.6 = (bf16[1024,256]{1,0:T(8,128)(2,1)}, bf16[1024,256]{1,0:T(8,128)(2,1)S(1)}, u32[]{:S(2)}) copy-start(bf16[1024,256]{1,0:T(8,128)(2,1)S(1)} %collective-permute-done.3.refs_1_) | copy-start | bytes 1572868
  74.4 22.5 %collective-permute-start.4 = (bf16[1024,256]{1,0:T(8,128)(2,1)S(1)}, bf16[1024,256]{1,0:T(8,128)(2,1)}, u32[]{:S(2)}, u32[]{:S(2)}) collective-permute-start(bf16[1024,256]{1,0:T(8,128)(2,1)S(1)} %collective-permute-done.3.refs_1_), channel_id=1, source_target_pairs={{0,1},{1,2},{2,3},{3,4},{4,5},{5,6},{6,7},{7,0},{8,9},{9,10},{10,1... | collective-permute-start | bytes 1572872 | tf_op jit(solution)/shard_map/ppermute | solution.py:195
  76.4 22.5 %collective-permute-start.7 = (bf16[1024,256]{1,0:T(8,128)(2,1)S(1)}, bf16[1024,256]{1,0:T(8,128)(2,1)}, u32[]{:S(2)}, u32[]{:S(2)}) collective-permute-start(bf16[1024,256]{1,0:T(8,128)(2,1)S(1)} %collective-permute-done.6.refs_7_.refs_9_), channel_id=1, source_target_pairs={{0,7},{1,0},{2,1},{3,2},{4,3},{5,4},{6,5},{7,6},{8,15},{9,8},{10,9... | collective-permute-start | bytes 1572872 | tf_op jit(solution)/shard_map/ppermute | solution.py:195
  86.4 22.6 %collective-permute-start.10 = (bf16[1024,256]{1,0:T(8,128)(2,1)}, bf16[1024,256]{1,0:T(8,128)(2,1)}, u32[]{:S(2)}, u32[]{:S(2)}) collective-permute-start(bf16[1024,256]{1,0:T(8,128)(2,1)} %collective-permute-done.9.refs_2_), channel_id=1, source_target_pairs={{0,7},{1,0},{2,1},{3,2},{4,3},{5,4},{6,5},{7,6},{8,15},{9,8},{10,9... | collective-permute-start | bytes 1572872 | tf_op jit(solution)/shard_map/ppermute | solution.py:195
  91.9 17.1 %collective-permute-start.12 = (bf16[1024,256]{1,0:T(8,128)(2,1)}, bf16[1024,256]{1,0:T(8,128)(2,1)}, u32[]{:S(2)}, u32[]{:S(2)}) collective-permute-start(bf16[1024,256]{1,0:T(8,128)(2,1)} %collective-permute-done.11.refs_6_.refs_8_), channel_id=1, source_target_pairs={{0,1},{1,2},{2,3},{3,4},{4,5},{5,6},{6,7},{7,0},{8,9},{9,10},{10,1... | collective-permute-start | bytes 1572872 | tf_op jit(solution)/shard_map/ppermute | solution.py:195
  96.9 20.4 %collective-permute-start.5 = (bf16[1024,256]{1,0:T(8,128)(2,1)}, bf16[1024,256]{1,0:T(8,128)(2,1)}, u32[]{:S(2)}, u32[]{:S(2)}) collective-permute-start(bf16[1024,256]{1,0:T(8,128)(2,1)} %collective-permute-done.4.refs_3_), channel_id=1, source_target_pairs={{0,1},{1,2},{2,3},{3,4},{4,5},{5,6},{6,7},{7,0},{8,9},{9,10},{10,1... | collective-permute-start | bytes 1572872 | tf_op jit(solution)/shard_map/ppermute | solution.py:195
  98.8 21.4 %collective-permute-start.8 = (bf16[1024,256]{1,0:T(8,128)(2,1)}, bf16[1024,256]{1,0:T(8,128)(2,1)}, u32[]{:S(2)}, u32[]{:S(2)}) collective-permute-start(bf16[1024,256]{1,0:T(8,128)(2,1)} %collective-permute-done.7.refs_9_.refs_11_), channel_id=1, source_target_pairs={{0,7},{1,0},{2,1},{3,2},{4,3},{5,4},{6,5},{7,6},{8,15},{9,8},{10,9... | collective-permute-start | bytes 1572872 | tf_op jit(solution)/shard_map/ppermute | solution.py:195
  103.4 5.6 %copy-start.9 = (bf16[1024,256]{1,0:T(8,128)(2,1)S(1)}, bf16[1024,256]{1,0:T(8,128)(2,1)}, u32[]{:S(2)}) copy-start(bf16[1024,256]{1,0:T(8,128)(2,1)} %copy-done.8) | copy-start | bytes 1572868
  109.0 11.2 %copy-start.1 = (bf16[1,176,2048]{2,1,0:T(8,128)(2,1)S(1)}, bf16[1,176,2048]{2,1,0:T(8,128)(2,1)}, u32[]{:S(2)}) copy-start(bf16[1,176,2048]{2,1,0:T(8,128)(2,1)} %param.11) | copy-start | bytes 2162692
  109.0 11.2 %copy-start.3 = (bf16[1,176,2048]{2,1,0:T(8,128)(2,1)S(1)}, bf16[1,176,2048]{2,1,0:T(8,128)(2,1)}, u32[]{:S(2)}) copy-start(bf16[1,176,2048]{2,1,0:T(8,128)(2,1)} %param.12) | copy-start | bytes 2162692
  115.2 0.9 copy-start.12
  120.3 1.1 copy-start.5
  121.4 1.1 copy-start.13
  122.5 1.1 copy-start.14
  123.6 4.0 %copy-start.24 = (bf16[352,256]{1,0:T(8,128)(2,1)S(1)}, bf16[352,256]{1,0:T(8,128)(2,1)}, u32[]{:S(2)}) copy-start(bf16[352,256]{1,0:T(8,128)(2,1)} %get-tuple-element.38) | copy-start | bytes 540676
  123.6 4.1 %copy-start.25 = (bf16[352,256]{1,0:T(8,128)(2,1)S(1)}, bf16[352,256]{1,0:T(8,128)(2,1)}, u32[]{:S(2)}) copy-start(bf16[352,256]{1,0:T(8,128)(2,1)} %get-tuple-element.39) | copy-start | bytes 540676
  123.6 4.1 %copy-start.26 = (bf16[352,256]{1,0:T(8,128)(2,1)S(1)}, bf16[352,256]{1,0:T(8,128)(2,1)}, u32[]{:S(2)}) copy-start(bf16[352,256]{1,0:T(8,128)(2,1)} %get-tuple-element.40) | copy-start | bytes 540676
  127.6 2.3 %copy-start.15 = (bf16[176,1024]{1,0:T(8,128)(2,1)}, bf16[176,1024]{1,0:T(8,128)(2,1)S(1)}, u32[]{:S(2)}) copy-start(bf16[176,1024]{1,0:T(8,128)(2,1)S(1)} %get-tuple-element.34.refs_14_) | copy-start | bytes 1081348
  127.6 40.0 %copy-start.4 = (bf16[352,1024]{1,0:T(8,128)(2,1)}, bf16[352,1024]{1,0:T(8,128)(2,1)S(1)}, u32[]{:S(2)}) copy-start(bf16[352,1024]{1,0:T(8,128)(2,1)S(1)} %get-tuple-element.33.refs_13_) | copy-start | bytes 2162692
  129.9 50.4 %all-to-all-start.3 = ((bf16[64,16,768]{2,1,0:T(8,128)(2,1)}), bf16[64,16,768]{2,1,0:T(8,128)(2,1)}, u32[]{:S(2)}, u32[]{:S(2)}) async-start(bf16[64,16,768]{2,1,0:T(8,128)(2,1)} %bitcast.52), calls=%async_computation.3 | async-start | bytes 3145728 | tf_op jit(solution)/shard_map/all_to_all | solution.py:199
  141.9 17.3 %collective-permute-start.13 = (bf16[1024,256]{1,0:T(8,128)(2,1)S(1)}, bf16[1024,256]{1,0:T(8,128)(2,1)S(1)}, u32[]{:S(2)}, u32[]{:S(2)}) collective-permute-start(bf16[1024,256]{1,0:T(8,128)(2,1)S(1)} %convolution_convert_fusion.4), channel_id=1, source_target_pairs={{0,1},{1,2},{2,3},{3,4},{4,5},{5,6},{6,7},{7,0},{8,9},{9,10},{10,1... | collective-permute-start | bytes 1572872 | tf_op jit(solution)/shard_map/ppermute | solution.py:195
  144.3 17.9 %collective-permute-start.15 = (bf16[1024,256]{1,0:T(8,128)(2,1)S(1)}, bf16[1024,256]{1,0:T(8,128)(2,1)S(1)}, u32[]{:S(2)}, u32[]{:S(2)}) collective-permute-start(bf16[1024,256]{1,0:T(8,128)(2,1)S(1)} %convolution_convert_fusion.2), channel_id=1, source_target_pairs={{0,7},{1,0},{2,1},{3,2},{4,3},{5,4},{6,5},{7,6},{8,15},{9,8},{10,9... | collective-permute-start | bytes 1572872 | tf_op jit(solution)/shard_map/ppermute | solution.py:195
  160.1 15.9 %collective-permute-start.14 = (bf16[1024,256]{1,0:T(8,128)(2,1)}, bf16[1024,256]{1,0:T(8,128)(2,1)}, u32[]{:S(2)}, u32[]{:S(2)}) collective-permute-start(bf16[1024,256]{1,0:T(8,128)(2,1)} %add_convert_fusion.2), channel_id=1, source_target_pairs={{0,1},{1,2},{2,3},{3,4},{4,5},{5,6},{6,7},{7,0},{8,9},{9,10},{10,1... | collective-permute-start | bytes 1572872 | tf_op jit(solution)/shard_map/ppermute | solution.py:195
  163.1 14.9 %collective-permute-start.16 = (bf16[1024,256]{1,0:T(8,128)(2,1)}, bf16[1024,256]{1,0:T(8,128)(2,1)}, u32[]{:S(2)}, u32[]{:S(2)}) collective-permute-start(bf16[1024,256]{1,0:T(8,128)(2,1)} %add_convert_fusion.1), channel_id=1, source_target_pairs={{0,7},{1,0},{2,1},{3,2},{4,3},{5,4},{6,5},{7,6},{8,15},{9,8},{10,9... | collective-permute-start | bytes 1572872 | tf_op jit(solution)/shard_map/ppermute | solution.py:195
  180.3 32.7 %all-to-all-start.2 = ((bf16[64,16,256]{2,1,0:T(8,128)(2,1)}), bf16[64,16,256]{2,1,0:T(8,128)(2,1)S(1)}, u32[]{:S(2)}, u32[]{:S(2)}) async-start(bf16[64,16,256]{2,1,0:T(8,128)(2,1)} %bitcast.10), calls=%async_computation.2 | async-start | bytes 1048576 | tf_op jit(solution)/shard_map/all_to_all | solution.py:199
  192.4 14.1 %copy-start.7 = (bf16[1024,256]{1,0:T(8,128)(2,1)S(1)}, bf16[1024,256]{1,0:T(8,128)(2,1)}, u32[]{:S(2)}) copy-start(bf16[1024,256]{1,0:T(8,128)(2,1)} %copy-done.6) | copy-start | bytes 1572868
  192.4 14.1 %copy-start.10 = (bf16[1024,256]{1,0:T(8,128)(2,1)S(1)}, bf16[1024,256]{1,0:T(8,128)(2,1)}, u32[]{:S(2)}) copy-start(bf16[1024,256]{1,0:T(8,128)(2,1)} %copy-done.8) | copy-start | bytes 1572868
  192.4 14.1 %copy-start.16 = (bf16[176,1024]{1,0:T(8,128)(2,1)S(1)}, bf16[176,1024]{1,0:T(8,128)(2,1)}, u32[]{:S(2)}) copy-start(bf16[176,1024]{1,0:T(8,128)(2,1)} %copy-done.15) | copy-start | bytes 1081348
  194.4 18.6 %collective-permute-start.17 = (bf16[128,256]{1,0:T(8,128)(2,1)S(1)}, bf16[128,256]{1,0:T(8,128)(2,1)S(1)}, u32[]{:S(2)}, u32[]{:S(2)}) collective-permute-start(bf16[128,256]{1,0:T(8,128)(2,1)S(1)} %get-tuple-element.43), channel_id=1, source_target_pairs={{0,4},{1,5},{2,6},{3,7},{4,0},{5,1},{6,2},{7,3},{8,12},{9,13},{10,... | collective-permute-start | bytes 196616 | tf_op jit(solution)/shard_map/ppermute | solution.py:195
  198.7 14.3 %collective-permute-start.19 = (bf16[128,256]{1,0:T(8,128)(2,1)S(1)}, bf16[128,256]{1,0:T(8,128)(2,1)S(1)}, u32[]{:S(2)}, u32[]{:S(2)}) collective-permute-start(bf16[128,256]{1,0:T(8,128)(2,1)S(1)} %get-tuple-element.44), channel_id=1, source_target_pairs={{0,5},{1,6},{2,7},{3,0},{4,1},{5,2},{6,3},{7,4},{8,13},{9,14},{10,... | collective-permute-start | bytes 196616 | tf_op jit(solution)/shard_map/ppermute | solution.py:195
  202.4 10.6 %collective-permute-start.18 = (bf16[128,256]{1,0:T(8,128)(2,1)S(1)}, bf16[128,256]{1,0:T(8,128)(2,1)S(1)}, u32[]{:S(2)}, u32[]{:S(2)}) collective-permute-start(bf16[128,256]{1,0:T(8,128)(2,1)S(1)} %get-tuple-element.45), channel_id=1, source_target_pairs={{0,3},{1,4},{2,5},{3,6},{4,7},{5,0},{6,1},{7,2},{8,11},{9,12},{10,... | collective-permute-start | bytes 196616 | tf_op jit(solution)/shard_map/ppermute | solution.py:195
  (3 other events, 2.2 us)

commit v3 on v2

--- a/solution.py
+++ b/solution.py
@@ -8,7 +8,7 @@
 
 VMEM = pl.BlockSpec(memory_space=pltpu.VMEM)
 SMEM = pl.BlockSpec(memory_space=pltpu.SMEM)
-PARAMS = pltpu.CompilerParams(vmem_limit_bytes=48 * 1024 * 1024)
+PARAMS = pltpu.CompilerParams(vmem_limit_bytes=56 * 1024 * 1024)
 
 
 def nt(left, right):
@@ -111,6 +111,7 @@
         in_specs=[SMEM] + [VMEM] * (len(arrays) + 3),
         out_specs=[VMEM] * 3,
         compiler_params=PARAMS,
+        cost_estimate=pl.CostEstimate(flops=36 * 10**9, bytes_accessed=1000, transcendentals=0),
         name="first_products",
     )(me, *arrays, *weights)
 
@@ -174,6 +175,7 @@
         in_specs=[SMEM] + [VMEM] * (len(arrays) + 2),
         out_specs=[VMEM] * 3,
         compiler_params=PARAMS,
+        cost_estimate=pl.CostEstimate(flops=20 * 10**9, bytes_accessed=1000, transcendentals=0),
         name="weight_grads",
     )(me, *arrays, grads, hidden)
 
@@ -257,11 +259,15 @@
         if d:
             right = added(right, partial(d)).astype(jnp.bfloat16)
             left = added(left, partial(-d)).astype(jnp.bfloat16)
-    back = over_ep(added(partial(0), right, left).astype(jnp.bfloat16))
+    total = added(partial(0), right, left).astype(jnp.bfloat16)
 
     grad_gate, grad_up, grad_down = weight_grads(
         me_ref, ring, width, early_x + late_x, early_g + late_g, grads, hidden
     )
+    total, grad_gate, grad_up, grad_down = lax.optimization_barrier(
+        (total, grad_gate, grad_up, grad_down)
+    )
+    back = over_ep(total)
     sides = tn(place, far_back).astype(jnp.bfloat16)
     sides = [moved(sides[:, k * width : (k + 1) * width], d) for k, d in enumerate(away)]
     input_grad = (tn(place, back) + added(*sides)).astype(jnp.bfloat16)

time: 215 us -> 213 us (level)
  starting transfers between devices: 124 us -> 113 us
  Pallas kernels: 19.4 us -> 25.4 us
  local copies, waits for them, and re-layouts: 9.56 us -> 4.53 us
  waiting for transfers between devices: 47.4 us -> 52.3 us
  matrix products: 7.46 us -> 10.1 us
    all_to_all x4, waiting for transfers between devices: 0.37 us -> 29.3 us  [over_ep(): lax.all_to_all(value.reshape(shape), 'ep', split_axis=0, concat_axis=0, t...]
    ppermute x20, waiting for transfers between devices: 47.1 us -> 23 us  [moved(): lax.ppermute(value, 'tp', [(i, (i + by) % ring) for i in range(ring)])]
    all_to_all x4, starting transfers between devices: 45.8 us -> 33 us  [over_ep(): lax.all_to_all(value.reshape(shape), 'ep', split_axis=0, concat_axis=0, t...]
    unnamed x54 -> x32, local copies, waits for them, and re-layouts: 9.46 us -> 2.82 us
    pallas_call x2, Pallas kernels: 2.83 us -> 5.66 us  [dispatch(): pl.pallas_call(kernel, out_shape=(jax.ShapeDtypeStruct((count, sum(widths...]
    dot_general x8, matrix products: 7.46 us -> 10.1 us  [tn(): lax.dot_general(left, right, (((0,), (0,)), ((), ())), preferred_element_...]
    ppermute x20, starting transfers between devices: 78.1 us -> 80.4 us  [moved(): lax.ppermute(value, 'tp', [(i, (i + by) % ring) for i in range(ring)])]
  transfers between devices with their start and end apart: 24 -> 24, of which waited for: 13 -> 12; matrix products, arithmetic and copies ran while one was open for 4% -> 5% of each run, Pallas kernels for 6% -> 8%
where the time goes in v3:
time: 213 us; the launch traced here: 211 us
  starting transfers between devices  113 us (53%)
  waiting for transfers between devices  52.3 us (25%)
  Pallas kernels  25.4 us (12%)
  matrix products  10.1 us (5%)
  local copies, waits for them, and re-layouts  4.53 us (2%)
  other arithmetic  4.18 us (2%)
    ppermute x20, starting transfers between devices, moved(): lax.ppermute(value, 'tp', [(i, (i + by) % ring) for i in range(ring)])  80.4 us
    all_to_all x4, starting transfers between devices, over_ep(): lax.all_to_all(value.reshape(shape), 'ep', split_axis=0, concat_axis=0, t...  33 us
    all_to_all x4, waiting for transfers between devices, over_ep(): lax.all_to_all(value.reshape(shape), 'ep', split_axis=0, concat_axis=0, t...  29.3 us
    ppermute x20, waiting for transfers between devices, moved(): lax.ppermute(value, 'tp', [(i, (i + by) % ring) for i in range(ring)])  23 us
    dot_general x8, matrix products, tn(): lax.dot_general(left, right, (((0,), (0,)), ((), ())), preferred_element_...  10.1 us
    pallas_call x1, Pallas kernels, weight_grads(): pl.pallas_call(kernel, out_shape=[jax.ShapeDtypeStruct((units, ring * wid...  7.08 us
    pallas_call x1, Pallas kernels, first_products(): pl.pallas_call(kernel, out_shape=[jax.ShapeDtypeStruct((units, rows), jnp...  6.67 us
    pallas_call x1, Pallas kernels, activations(): pl.pallas_call(kernel, out_shape=(jax.ShapeDtypeStruct((2 * units, rows),...  5.97 us
  transfers between devices with their start and end apart: 24, of which 12 were waited for; matrix products, arithmetic and copies ran while one was open for 5% of the time, Pallas kernels for 8%

profile of v3, /device:TPU:1, one launch (start us, length us, event | category | flops | bytes accessed | tf_op | source)
XLA Modules:
  0.0 211.0 jit_solution(9276739305259924843)
XLA Ops:
  0.7 2.5 %dispatch.2 = (bf16[1024,512]{1,0:T(8,128)(2,1)}, bf16[1024,128]{1,0:T(8,128)(2,1)}) custom-call(s32[6,128]{1,0:T(8,128)} %bitcast.52, f32[6,128]{1,0:T(8,128)} %bitcast.54, bf16[128,256]{1,0:T(8,128)(2,1)} %refs_0_.1, bf16[128,256]{1,0:T(8,128)(2,1)} %refs_1_.1), custom_call_target="tpu_custom_call" | custom-call | tf_op jit(solution)/shard_map/dispatch/pallas_call | solution.py:64
  3.1 11.6 %all-to-all-start = ((bf16[64,16,512]{2,1,0:T(8,128)(2,1)}), bf16[64,16,512]{2,1,0:T(8,128)(2,1)S(1)}, u32[]{:S(2)}, u32[]{:S(2)}) async-start(bf16[64,16,512]{2,1,0:T(8,128)(2,1)} %bitcast.49), calls=%async_computation | async-start | bytes 2097152 | tf_op jit(solution)/shard_map/all_to_all | solution.py:201
  14.8 10.6 %collective-permute-start = (bf16[128,512]{1,0:T(8,128)(2,1)S(1)}, bf16[128,512]{1,0:T(8,128)(2,1)S(1)}, u32[]{:S(2)}, u32[]{:S(2)}) collective-permute-start(bf16[128,512]{1,0:T(8,128)(2,1)S(1)} %pad_maximum_fusion), channel_id=1, source_target_pairs={{0,4},{1,5},{2,6},{3,7},{4,0},{5,1},{6,2},{7,3},{8,12},{9,13},{10,... | collective-permute-start | bytes 393224 | tf_op jit(solution)/shard_map/ppermute | solution.py:197
  25.5 1.9 collective-permute-start.1
  27.4 5.2 %collective-permute-start.2 = (bf16[128,256]{1,0:T(8,128)(2,1)S(1)}, bf16[128,256]{1,0:T(8,128)(2,1)S(1)}, u32[]{:S(2)}, u32[]{:S(2)}) collective-permute-start(bf16[128,256]{1,0:T(8,128)(2,1)S(1)} %copy-done.10), channel_id=1, source_target_pairs={{0,3},{1,4},{2,5},{3,6},{4,7},{5,0},{6,1},{7,2},{8,11},{9,12},{10,... | collective-permute-start | bytes 196616 | tf_op jit(solution)/shard_map/ppermute | solution.py:197
  33.2 1.8 collective-permute-done.1.refs_2_
  35.0 5.0 %collective-permute-done.2.refs_3_ = bf16[128,256]{1,0:T(8,128)(2,1)S(1)} collective-permute-done((bf16[128,256]{1,0:T(8,128)(2,1)S(1)}, bf16[128,256]{1,0:T(8,128)(2,1)S(1)}, u32[]{:S(2)}, u32[]{:S(2)}) %collective-permute-start.2) | collective-permute-done | bytes 65568 | tf_op jit(solution)/shard_map/ppermute | solution.py:197
  40.6 3.2 %dispatch.3 = (bf16[1024,1024]{1,0:T(8,128)(2,1)}, bf16[1024,128]{1,0:T(8,128)(2,1)}) custom-call(s32[6,128]{1,0:T(8,128)} %bitcast.53, f32[6,128]{1,0:T(8,128)} %bitcast.55, bf16[128,256]{1,0:T(8,128)(2,1)} %get-tuple-element.55.refs_0_, bf16[128,256]{1,0:T(8,128)(2,1)} %get-tuple-element.54.refs_1_, bf16[128,256]{1,0:T(8,128)(2,1)} %copy-done.14, ...), custom_call_target="tpu_custom_call" | custom-call | tf_op jit(solution)/shard_map/dispatch/pallas_call | solution.py:64
  43.8 1.0 fusion.29
  44.8 3.0 %collective-permute-start.3 = (bf16[1024,256]{1,0:T(8,128)(2,1)}, bf16[1024,256]{1,0:T(8,128)(2,1)}, u32[]{:S(2)}, u32[]{:S(2)}) collective-permute-start(bf16[1024,256]{1,0:T(8,128)(2,1)} %get-tuple-element.32.refs_0_), channel_id=1, source_target_pairs={{0,1},{1,2},{2,3},{3,4},{4,5},{5,6},{6,7},{7,0},{8,9},{9,10},{10,1... | collective-permute-start | bytes 1572872 | tf_op jit(solution)/shard_map/ppermute | solution.py:197
  47.8 8.6 %collective-permute-start.6 = (bf16[1024,256]{1,0:T(8,128)(2,1)}, bf16[1024,256]{1,0:T(8,128)(2,1)}, u32[]{:S(2)}, u32[]{:S(2)}) collective-permute-start(bf16[1024,256]{1,0:T(8,128)(2,1)} %get-tuple-element.33.refs_5_.refs_7_), channel_id=1, source_target_pairs={{0,7},{1,0},{2,1},{3,2},{4,3},{5,4},{6,5},{7,6},{8,15},{9,8},{10,9... | collective-permute-start | bytes 1572872 | tf_op jit(solution)/shard_map/ppermute | solution.py:197
  56.4 3.4 %collective-permute-start.9 = (bf16[1024,256]{1,0:T(8,128)(2,1)}, bf16[1024,256]{1,0:T(8,128)(2,1)}, u32[]{:S(2)}, u32[]{:S(2)}) collective-permute-start(bf16[1024,256]{1,0:T(8,128)(2,1)} %get-tuple-element.32.refs_0_), channel_id=1, source_target_pairs={{0,7},{1,0},{2,1},{3,2},{4,3},{5,4},{6,5},{7,6},{8,15},{9,8},{10,9... | collective-permute-start | bytes 1572872 | tf_op jit(solution)/shard_map/ppermute | solution.py:197
  59.8 1.9 collective-permute-start.11
  61.7 7.4 %all-to-all-start.1 = ((bf16[64,16,1024]{2,1,0:T(8,128)(2,1)}), bf16[64,16,1024]{2,1,0:T(8,128)(2,1)S(1)}, u32[]{:S(2)}, u32[]{:S(2)}) async-start(bf16[64,16,1024]{2,1,0:T(8,128)(2,1)} %bitcast.46), calls=%async_computation.1 | async-start | bytes 4194304 | tf_op jit(solution)/shard_map/all_to_all | solution.py:201
  69.2 1.9 collective-permute-start.4
  71.1 4.9 %collective-permute-start.7 = (bf16[1024,256]{1,0:T(8,128)(2,1)}, bf16[1024,256]{1,0:T(8,128)(2,1)}, u32[]{:S(2)}, u32[]{:S(2)}) collective-permute-start(bf16[1024,256]{1,0:T(8,128)(2,1)} %collective-permute-done.6.refs_7_.refs_9_), channel_id=1, source_target_pairs={{0,7},{1,0},{2,1},{3,2},{4,3},{5,4},{6,5},{7,6},{8,15},{9,8},{10,9... | collective-permute-start | bytes 1572872 | tf_op jit(solution)/shard_map/ppermute | solution.py:197
  76.0 1.8 collective-permute-done.9.refs_2_
  77.8 5.3 %collective-permute-start.10 = (bf16[1024,256]{1,0:T(8,128)(2,1)}, bf16[1024,256]{1,0:T(8,128)(2,1)}, u32[]{:S(2)}, u32[]{:S(2)}) collective-permute-start(bf16[1024,256]{1,0:T(8,128)(2,1)} %collective-permute-done.9.refs_2_), channel_id=1, source_target_pairs={{0,7},{1,0},{2,1},{3,2},{4,3},{5,4},{6,5},{7,6},{8,15},{9,8},{10,9... | collective-permute-start | bytes 1572872 | tf_op jit(solution)/shard_map/ppermute | solution.py:197
  83.1 1.9 collective-permute-start.12
  86.0 2.4 %collective-permute-done.4.refs_3_ = bf16[1024,256]{1,0:T(8,128)(2,1)} collective-permute-done((bf16[1024,256]{1,0:T(8,128)(2,1)}, bf16[1024,256]{1,0:T(8,128)(2,1)}, u32[]{:S(2)}, u32[]{:S(2)}) %collective-permute-start.4) | collective-permute-done | bytes 524320 | tf_op jit(solution)/shard_map/ppermute | solution.py:197
  88.4 1.9 collective-permute-start.5
  90.3 4.6 %collective-permute-start.8 = (bf16[1024,256]{1,0:T(8,128)(2,1)}, bf16[1024,256]{1,0:T(8,128)(2,1)}, u32[]{:S(2)}, u32[]{:S(2)}) collective-permute-start(bf16[1024,256]{1,0:T(8,128)(2,1)} %collective-permute-done.7.refs_9_.refs_11_), channel_id=1, source_target_pairs={{0,7},{1,0},{2,1},{3,2},{4,3},{5,4},{6,5},{7,6},{8,15},{9,8},{10,9... | collective-permute-start | bytes 1572872 | tf_op jit(solution)/shard_map/ppermute | solution.py:197
  94.9 5.4 %collective-permute-done.10.refs_4_ = bf16[1024,256]{1,0:T(8,128)(2,1)} collective-permute-done((bf16[1024,256]{1,0:T(8,128)(2,1)}, bf16[1024,256]{1,0:T(8,128)(2,1)}, u32[]{:S(2)}, u32[]{:S(2)}) %collective-permute-start.10) | collective-permute-done | bytes 524320 | tf_op jit(solution)/shard_map/ppermute | solution.py:197
  100.3 6.7 %first_products.1 = (f32[176,1024]{1,0:T(8,128)}, f32[176,1024]{1,0:T(8,128)}, f32[176,1024]{1,0:T(8,128)}) custom-call(s32[1]{0:T(128)} %bitcast.2.me_ref, bf16[1024,256]{1,0:T(8,128)(2,1)} %get-tuple-element.32.refs_0_, bf16[1024,256]{1,0:T(8,128)(2,1)} %collective-permute-done.3.refs_1_, bf16[1024,256]{1,0:T(8,128)(2,1)} %collective-permute-done.9.refs_2_, ...), custom_call_target="tpu_custom_call" | custom-call | flops 35999997952 | bytes 1000 | tf_op jit(solution)/shard_map/first_products/pallas_call | solution.py:108
  108.4 3.1 %collective-permute-done.8.refs_2_.refs_12_ = bf16[1024,256]{1,0:T(8,128)(2,1)} collective-permute-done((bf16[1024,256]{1,0:T(8,128)(2,1)}, bf16[1024,256]{1,0:T(8,128)(2,1)}, u32[]{:S(2)}, u32[]{:S(2)}) %collective-permute-start.8) | collective-permute-done | bytes 524320 | tf_op jit(solution)/shard_map/ppermute | solution.py:197
  111.5 7.4 %all-to-all-done.1 = bf16[64,16,1024]{2,1,0:T(8,128)(2,1)S(1)} async-done(((bf16[64,16,1024]{2,1,0:T(8,128)(2,1)}), bf16[64,16,1024]{2,1,0:T(8,128)(2,1)S(1)}, u32[]{:S(2)}, u32[]{:S(2)}) %all-to-all-start.1) | async-done | bytes 2097184 | tf_op jit(solution)/shard_map/all_to_all | solution.py:201
  118.9 1.3 copy-done.6
  120.2 6.0 %activations.1 = (bf16[352,1024]{1,0:T(8,128)(2,1)}, bf16[176,1024]{1,0:T(8,128)(2,1)}) custom-call(s32[1]{0:T(128)} %bitcast.2.me_ref, bf16[1024,1024]{1,0:T(8,128)(2,1)} %bitcast.43, bf16[1024,256]{1,0:T(8,128)(2,1)} %copy-done.8, bf16[1024,256]{1,0:T(8,128)(2,1)} %collective-permute-done.8.refs_2_.refs_12_, bf16[176,2048]{1,0:T(8,128)(2,1)} %bitcast.28, ...), custom_call_target="tpu_custom_call" | custom-call | tf_op jit(solution)/shard_map/activations/pallas_call | solution.py:142
  126.2 2.5 %convolution_convert_fusion.2 = bf16[1024,256]{1,0:T(8,128)(2,1)} fusion(bf16[352,1024]{1,0:T(8,128)(2,1)} %get-tuple-element.37.refs_13_, s32[]{:T(128)S(6)} %select_n.27, bf16[176,2048]{1,0:T(8,128)(2,1)S(1)} %bitcast.30, bf16[176,2048]{1,0:T(8,128)(2,1)S(1)} %bitcast.38), kind=kOutput, calls=%fused_computation.18 | convolution fusion | flops 185171968 | bytes 2686980 | tf_op jit(solution)/shard_map/dot_general | solution.py:19
  128.7 1.3 convolution_convert_fusion.4
  130.0 1.9 collective-permute-start.13
  131.9 4.9 %collective-permute-start.15 = (bf16[1024,256]{1,0:T(8,128)(2,1)}, bf16[1024,256]{1,0:T(8,128)(2,1)}, u32[]{:S(2)}, u32[]{:S(2)}) collective-permute-start(bf16[1024,256]{1,0:T(8,128)(2,1)} %convolution_convert_fusion.2), channel_id=1, source_target_pairs={{0,7},{1,0},{2,1},{3,2},{4,3},{5,4},{6,5},{7,6},{8,15},{9,8},{10,9... | collective-permute-start | bytes 1572872 | tf_op jit(solution)/shard_map/ppermute | solution.py:197
  136.8 2.2 %convolution_convert_fusion = bf16[1024,768]{1,0:T(8,128)(2,1)} fusion(bf16[352,1024]{1,0:T(8,128)(2,1)S(1)} %copy-done.4, bf16[352,256]{1,0:T(8,128)(2,1)S(1)} %copy-done.13, bf16[352,256]{1,0:T(8,128)(2,1)S(1)} %copy-done.12, bf16[352,256]{1,0:T(8,128)(2,1)S(1)} %copy-done.11), kind=kOutput, calls=%fused_computation.16 | convolution fusion | flops 556056576 | bytes 2834432 | tf_op jit(solution)/shard_map/dot_general | solution.py:19
  139.5 7.5 %all-to-all-start.3 = ((bf16[64,16,768]{2,1,0:T(8,128)(2,1)}), bf16[64,16,768]{2,1,0:T(8,128)(2,1)}, u32[]{:S(2)}, u32[]{:S(2)}) async-start(bf16[64,16,768]{2,1,0:T(8,128)(2,1)} %bitcast.48), calls=%async_computation.3 | async-start | bytes 3145728 | tf_op jit(solution)/shard_map/all_to_all | solution.py:201
  147.5 1.2 add_convert_fusion.2
  148.7 2.1 collective-permute-start.14
  150.8 1.2 add_convert_fusion.1
  152.0 4.6 %collective-permute-start.16 = (bf16[1024,256]{1,0:T(8,128)(2,1)S(1)}, bf16[1024,256]{1,0:T(8,128)(2,1)S(1)}, u32[]{:S(2)}, u32[]{:S(2)}) collective-permute-start(bf16[1024,256]{1,0:T(8,128)(2,1)S(1)} %add_convert_fusion.1), channel_id=1, source_target_pairs={{0,7},{1,0},{2,1},{3,2},{4,3},{5,4},{6,5},{7,6},{8,15},{9,8},{10,9... | collective-permute-start | bytes 1572872 | tf_op jit(solution)/shard_map/ppermute | solution.py:197
  156.6 7.1 %weight_grads.1 = (bf16[176,2048]{1,0:T(8,128)(2,1)}, bf16[176,2048]{1,0:T(8,128)(2,1)}, bf16[176,2048]{1,0:T(8,128)(2,1)}) custom-call(s32[1]{0:T(128)} %bitcast.2.me_ref, bf16[1024,256]{1,0:T(8,128)(2,1)} %get-tuple-element.32.refs_0_, bf16[1024,256]{1,0:T(8,128)(2,1)} %collective-permute-done.3.refs_1_, bf16[1024,256]{1,0:T(8,128)(2,1)} %collective-permute-done.9.refs_2_, ...), custom_call_target="tpu_custom_call" | custom-call | flops 20000000000 | bytes 1000 | tf_op jit(solution)/shard_map/weight_grads/pallas_call | solution.py:172
  164.8 2.1 %collective-permute-done.16 = bf16[1024,256]{1,0:T(8,128)(2,1)S(1)} collective-permute-done((bf16[1024,256]{1,0:T(8,128)(2,1)S(1)}, bf16[1024,256]{1,0:T(8,128)(2,1)S(1)}, u32[]{:S(2)}, u32[]{:S(2)}) %collective-permute-start.16) | collective-permute-done | bytes 524320 | tf_op jit(solution)/shard_map/ppermute | solution.py:197
  167.0 1.0 add_convert_fusion
  168.0 18.0 %all-to-all-done.3 = bf16[64,16,768]{2,1,0:T(8,128)(2,1)} async-done(((bf16[64,16,768]{2,1,0:T(8,128)(2,1)}), bf16[64,16,768]{2,1,0:T(8,128)(2,1)}, u32[]{:S(2)}, u32[]{:S(2)}) %all-to-all-start.3) | async-done | bytes 1572896 | tf_op jit(solution)/shard_map/all_to_all | solution.py:201
  185.9 6.5 %all-to-all-start.2 = ((bf16[64,16,256]{2,1,0:T(8,128)(2,1)}), bf16[64,16,256]{2,1,0:T(8,128)(2,1)S(1)}, u32[]{:S(2)}, u32[]{:S(2)}) async-start(bf16[64,16,256]{2,1,0:T(8,128)(2,1)} %bitcast.10), calls=%async_computation.2 | async-start | bytes 1048576 | tf_op jit(solution)/shard_map/all_to_all | solution.py:201
  192.4 1.8 convolution_convert_fusion.6
  194.2 4.8 %collective-permute-start.17 = (bf16[128,256]{1,0:T(8,128)(2,1)S(1)}, bf16[128,256]{1,0:T(8,128)(2,1)S(1)}, u32[]{:S(2)}, u32[]{:S(2)}) collective-permute-start(bf16[128,256]{1,0:T(8,128)(2,1)S(1)} %get-tuple-element.51), channel_id=1, source_target_pairs={{0,4},{1,5},{2,6},{3,7},{4,0},{5,1},{6,2},{7,3},{8,12},{9,13},{10,... | collective-permute-start | bytes 196616 | tf_op jit(solution)/shard_map/ppermute | solution.py:197
  199.0 1.9 collective-permute-start.19
  201.0 5.2 %collective-permute-start.18 = (bf16[128,256]{1,0:T(8,128)(2,1)S(1)}, bf16[128,256]{1,0:T(8,128)(2,1)S(1)}, u32[]{:S(2)}, u32[]{:S(2)}) collective-permute-start(bf16[128,256]{1,0:T(8,128)(2,1)S(1)} %get-tuple-element.53), channel_id=1, source_target_pairs={{0,3},{1,4},{2,5},{3,6},{4,7},{5,0},{6,1},{7,2},{8,11},{9,12},{10,... | collective-permute-start | bytes 196616 | tf_op jit(solution)/shard_map/ppermute | solution.py:197
  206.1 4.0 %all-to-all-done.2 = bf16[64,16,256]{2,1,0:T(8,128)(2,1)S(1)} async-done(((bf16[64,16,256]{2,1,0:T(8,128)(2,1)}), bf16[64,16,256]{2,1,0:T(8,128)(2,1)S(1)}, u32[]{:S(2)}, u32[]{:S(2)}) %all-to-all-start.2) | async-done | bytes 524320 | tf_op jit(solution)/shard_map/all_to_all | solution.py:201
  (53 shorter events, 6.8 us)
Async XLA Ops:
  0.6 14.2 %copy-start.10 = (bf16[128,256]{1,0:T(8,128)(2,1)S(1)}, bf16[128,256]{1,0:T(8,128)(2,1)}, u32[]{:S(2)}) copy-start(bf16[128,256]{1,0:T(8,128)(2,1)} %refs_1_.1) | copy-start | bytes 196612
  0.6 14.2 %copy-start.9 = (bf16[128,256]{1,0:T(8,128)(2,1)S(1)}, bf16[128,256]{1,0:T(8,128)(2,1)}, u32[]{:S(2)}) copy-start(bf16[128,256]{1,0:T(8,128)(2,1)} %refs_0_.1) | copy-start | bytes 196612
  3.1 40.6 %all-to-all-start = ((bf16[64,16,512]{2,1,0:T(8,128)(2,1)}), bf16[64,16,512]{2,1,0:T(8,128)(2,1)S(1)}, u32[]{:S(2)}, u32[]{:S(2)}) async-start(bf16[64,16,512]{2,1,0:T(8,128)(2,1)} %bitcast.49), calls=%async_computation | async-start | bytes 2097152 | tf_op jit(solution)/shard_map/all_to_all | solution.py:201
  14.8 17.7 %collective-permute-start = (bf16[128,512]{1,0:T(8,128)(2,1)S(1)}, bf16[128,512]{1,0:T(8,128)(2,1)S(1)}, u32[]{:S(2)}, u32[]{:S(2)}) collective-permute-start(bf16[128,512]{1,0:T(8,128)(2,1)S(1)} %pad_maximum_fusion), channel_id=1, source_target_pairs={{0,4},{1,5},{2,6},{3,7},{4,0},{5,1},{6,2},{7,3},{8,12},{9,13},{10,... | collective-permute-start | bytes 393224 | tf_op jit(solution)/shard_map/ppermute | solution.py:197
  25.5 9.5 %collective-permute-start.1 = (bf16[128,256]{1,0:T(8,128)(2,1)S(1)}, bf16[128,256]{1,0:T(8,128)(2,1)S(1)}, u32[]{:S(2)}, u32[]{:S(2)}) collective-permute-start(bf16[128,256]{1,0:T(8,128)(2,1)S(1)} %copy-done.9), channel_id=1, source_target_pairs={{0,5},{1,6},{2,7},{3,0},{4,1},{5,2},{6,3},{7,4},{8,13},{9,14},{10,... | collective-permute-start | bytes 196616 | tf_op jit(solution)/shard_map/ppermute | solution.py:197
  27.4 12.6 %collective-permute-start.2 = (bf16[128,256]{1,0:T(8,128)(2,1)S(1)}, bf16[128,256]{1,0:T(8,128)(2,1)S(1)}, u32[]{:S(2)}, u32[]{:S(2)}) collective-permute-start(bf16[128,256]{1,0:T(8,128)(2,1)S(1)} %copy-done.10), channel_id=1, source_target_pairs={{0,3},{1,4},{2,5},{3,6},{4,7},{5,0},{6,1},{7,2},{8,11},{9,12},{10,... | collective-permute-start | bytes 196616 | tf_op jit(solution)/shard_map/ppermute | solution.py:197
  35.0 5.0 %copy-start.14 = (bf16[128,256]{1,0:T(8,128)(2,1)}, bf16[128,256]{1,0:T(8,128)(2,1)S(1)}, u32[]{:S(2)}) copy-start(bf16[128,256]{1,0:T(8,128)(2,1)S(1)} %collective-permute-done.1.refs_2_) | copy-start | bytes 196612
  40.0 0.6 copy-start.15
  44.8 24.4 %collective-permute-start.3 = (bf16[1024,256]{1,0:T(8,128)(2,1)}, bf16[1024,256]{1,0:T(8,128)(2,1)}, u32[]{:S(2)}, u32[]{:S(2)}) collective-permute-start(bf16[1024,256]{1,0:T(8,128)(2,1)} %get-tuple-element.32.refs_0_), channel_id=1, source_target_pairs={{0,1},{1,2},{2,3},{3,4},{4,5},{5,6},{6,7},{7,0},{8,9},{9,10},{10,1... | collective-permute-start | bytes 1572872 | tf_op jit(solution)/shard_map/ppermute | solution.py:197
  47.8 23.3 %collective-permute-start.6 = (bf16[1024,256]{1,0:T(8,128)(2,1)}, bf16[1024,256]{1,0:T(8,128)(2,1)}, u32[]{:S(2)}, u32[]{:S(2)}) collective-permute-start(bf16[1024,256]{1,0:T(8,128)(2,1)} %get-tuple-element.33.refs_5_.refs_7_), channel_id=1, source_target_pairs={{0,7},{1,0},{2,1},{3,2},{4,3},{5,4},{6,5},{7,6},{8,15},{9,8},{10,9... | collective-permute-start | bytes 1572872 | tf_op jit(solution)/shard_map/ppermute | solution.py:197
  56.4 21.4 %collective-permute-start.9 = (bf16[1024,256]{1,0:T(8,128)(2,1)}, bf16[1024,256]{1,0:T(8,128)(2,1)}, u32[]{:S(2)}, u32[]{:S(2)}) collective-permute-start(bf16[1024,256]{1,0:T(8,128)(2,1)} %get-tuple-element.32.refs_0_), channel_id=1, source_target_pairs={{0,7},{1,0},{2,1},{3,2},{4,3},{5,4},{6,5},{7,6},{8,15},{9,8},{10,9... | collective-permute-start | bytes 1572872 | tf_op jit(solution)/shard_map/ppermute | solution.py:197
  59.8 23.3 %collective-permute-start.11 = (bf16[1024,256]{1,0:T(8,128)(2,1)}, bf16[1024,256]{1,0:T(8,128)(2,1)}, u32[]{:S(2)}, u32[]{:S(2)}) collective-permute-start(bf16[1024,256]{1,0:T(8,128)(2,1)} %get-tuple-element.33.refs_5_.refs_7_), channel_id=1, source_target_pairs={{0,1},{1,2},{2,3},{3,4},{4,5},{5,6},{6,7},{7,0},{8,9},{9,10},{10,1... | collective-permute-start | bytes 1572872 | tf_op jit(solution)/shard_map/ppermute | solution.py:197
  61.7 23.4 %copy-start = (bf16[1,176,2048]{2,1,0:T(8,128)(2,1)S(1)}, bf16[1,176,2048]{2,1,0:T(8,128)(2,1)}, u32[]{:S(2)}) copy-start(bf16[1,176,2048]{2,1,0:T(8,128)(2,1)} %param.11) | copy-start | bytes 2162692
  61.7 23.4 %copy-start.2 = (bf16[1,176,2048]{2,1,0:T(8,128)(2,1)S(1)}, bf16[1,176,2048]{2,1,0:T(8,128)(2,1)}, u32[]{:S(2)}) copy-start(bf16[1,176,2048]{2,1,0:T(8,128)(2,1)} %param.12) | copy-start | bytes 2162692
  61.7 57.1 %all-to-all-start.1 = ((bf16[64,16,1024]{2,1,0:T(8,128)(2,1)}), bf16[64,16,1024]{2,1,0:T(8,128)(2,1)S(1)}, u32[]{:S(2)}, u32[]{:S(2)}) async-start(bf16[64,16,1024]{2,1,0:T(8,128)(2,1)} %bitcast.46), calls=%async_computation.1 | async-start | bytes 4194304 | tf_op jit(solution)/shard_map/all_to_all | solution.py:201
  69.2 19.2 %collective-permute-start.4 = (bf16[1024,256]{1,0:T(8,128)(2,1)}, bf16[1024,256]{1,0:T(8,128)(2,1)}, u32[]{:S(2)}, u32[]{:S(2)}) collective-permute-start(bf16[1024,256]{1,0:T(8,128)(2,1)} %collective-permute-done.3.refs_1_), channel_id=1, source_target_pairs={{0,1},{1,2},{2,3},{3,4},{4,5},{5,6},{6,7},{7,0},{8,9},{9,10},{10,1... | collective-permute-start | bytes 1572872 | tf_op jit(solution)/shard_map/ppermute | solution.py:197
  71.1 19.1 %collective-permute-start.7 = (bf16[1024,256]{1,0:T(8,128)(2,1)}, bf16[1024,256]{1,0:T(8,128)(2,1)}, u32[]{:S(2)}, u32[]{:S(2)}) collective-permute-start(bf16[1024,256]{1,0:T(8,128)(2,1)} %collective-permute-done.6.refs_7_.refs_9_), channel_id=1, source_target_pairs={{0,7},{1,0},{2,1},{3,2},{4,3},{5,4},{6,5},{7,6},{8,15},{9,8},{10,9... | collective-permute-start | bytes 1572872 | tf_op jit(solution)/shard_map/ppermute | solution.py:197
  77.8 22.5 %collective-permute-start.10 = (bf16[1024,256]{1,0:T(8,128)(2,1)}, bf16[1024,256]{1,0:T(8,128)(2,1)}, u32[]{:S(2)}, u32[]{:S(2)}) collective-permute-start(bf16[1024,256]{1,0:T(8,128)(2,1)} %collective-permute-done.9.refs_2_), channel_id=1, source_target_pairs={{0,7},{1,0},{2,1},{3,2},{4,3},{5,4},{6,5},{7,6},{8,15},{9,8},{10,9... | collective-permute-start | bytes 1572872 | tf_op jit(solution)/shard_map/ppermute | solution.py:197
  83.1 17.1 %collective-permute-start.12 = (bf16[1024,256]{1,0:T(8,128)(2,1)}, bf16[1024,256]{1,0:T(8,128)(2,1)}, u32[]{:S(2)}, u32[]{:S(2)}) collective-permute-start(bf16[1024,256]{1,0:T(8,128)(2,1)} %collective-permute-done.11.refs_6_.refs_8_), channel_id=1, source_target_pairs={{0,1},{1,2},{2,3},{3,4},{4,5},{5,6},{6,7},{7,0},{8,9},{9,10},{10,1... | collective-permute-start | bytes 1572872 | tf_op jit(solution)/shard_map/ppermute | solution.py:197
  88.4 19.2 %collective-permute-start.5 = (bf16[1024,256]{1,0:T(8,128)(2,1)}, bf16[1024,256]{1,0:T(8,128)(2,1)S(1)}, u32[]{:S(2)}, u32[]{:S(2)}) collective-permute-start(bf16[1024,256]{1,0:T(8,128)(2,1)} %collective-permute-done.4.refs_3_), channel_id=1, source_target_pairs={{0,1},{1,2},{2,3},{3,4},{4,5},{5,6},{6,7},{7,0},{8,9},{9,10},{10,1... | collective-permute-start | bytes 1572872 | tf_op jit(solution)/shard_map/ppermute | solution.py:197
  90.3 21.2 %collective-permute-start.8 = (bf16[1024,256]{1,0:T(8,128)(2,1)}, bf16[1024,256]{1,0:T(8,128)(2,1)}, u32[]{:S(2)}, u32[]{:S(2)}) collective-permute-start(bf16[1024,256]{1,0:T(8,128)(2,1)} %collective-permute-done.7.refs_9_.refs_11_), channel_id=1, source_target_pairs={{0,7},{1,0},{2,1},{3,2},{4,3},{5,4},{6,5},{7,6},{8,15},{9,8},{10,9... | collective-permute-start | bytes 1572872 | tf_op jit(solution)/shard_map/ppermute | solution.py:197
  107.6 0.8 copy-start.8
  118.9 1.3 copy-start.6
  120.2 6.0 %copy-start.1 = (bf16[1,176,2048]{2,1,0:T(8,128)(2,1)S(1)}, bf16[1,176,2048]{2,1,0:T(8,128)(2,1)}, u32[]{:S(2)}) copy-start(bf16[1,176,2048]{2,1,0:T(8,128)(2,1)} %param.11) | copy-start | bytes 2162692
  120.2 6.0 %copy-start.3 = (bf16[1,176,2048]{2,1,0:T(8,128)(2,1)S(1)}, bf16[1,176,2048]{2,1,0:T(8,128)(2,1)}, u32[]{:S(2)}) copy-start(bf16[1,176,2048]{2,1,0:T(8,128)(2,1)} %param.12) | copy-start | bytes 2162692
  126.2 2.5 %copy-start.4 = (bf16[352,1024]{1,0:T(8,128)(2,1)S(1)}, bf16[352,1024]{1,0:T(8,128)(2,1)}, u32[]{:S(2)}) copy-start(bf16[352,1024]{1,0:T(8,128)(2,1)} %get-tuple-element.37.refs_13_) | copy-start | bytes 2162692
  128.7 8.1 %copy-start.11 = (bf16[352,256]{1,0:T(8,128)(2,1)S(1)}, bf16[352,256]{1,0:T(8,128)(2,1)}, u32[]{:S(2)}) copy-start(bf16[352,256]{1,0:T(8,128)(2,1)} %get-tuple-element.46) | copy-start | bytes 540676
  128.7 8.1 %copy-start.12 = (bf16[352,256]{1,0:T(8,128)(2,1)S(1)}, bf16[352,256]{1,0:T(8,128)(2,1)}, u32[]{:S(2)}) copy-start(bf16[352,256]{1,0:T(8,128)(2,1)} %get-tuple-element.47) | copy-start | bytes 540676
  128.7 8.1 %copy-start.13 = (bf16[352,256]{1,0:T(8,128)(2,1)S(1)}, bf16[352,256]{1,0:T(8,128)(2,1)}, u32[]{:S(2)}) copy-start(bf16[352,256]{1,0:T(8,128)(2,1)} %get-tuple-element.48) | copy-start | bytes 540676
  130.0 17.5 %collective-permute-start.13 = (bf16[1024,256]{1,0:T(8,128)(2,1)}, bf16[1024,256]{1,0:T(8,128)(2,1)}, u32[]{:S(2)}, u32[]{:S(2)}) collective-permute-start(bf16[1024,256]{1,0:T(8,128)(2,1)} %convolution_convert_fusion.4), channel_id=1, source_target_pairs={{0,1},{1,2},{2,3},{3,4},{4,5},{5,6},{6,7},{7,0},{8,9},{9,10},{10,1... | collective-permute-start | bytes 1572872 | tf_op jit(solution)/shard_map/ppermute | solution.py:197
  131.9 18.9 %collective-permute-start.15 = (bf16[1024,256]{1,0:T(8,128)(2,1)}, bf16[1024,256]{1,0:T(8,128)(2,1)}, u32[]{:S(2)}, u32[]{:S(2)}) collective-permute-start(bf16[1024,256]{1,0:T(8,128)(2,1)} %convolution_convert_fusion.2), channel_id=1, source_target_pairs={{0,7},{1,0},{2,1},{3,2},{4,3},{5,4},{6,5},{7,6},{8,15},{9,8},{10,9... | collective-permute-start | bytes 1572872 | tf_op jit(solution)/shard_map/ppermute | solution.py:197
  139.5 46.4 %all-to-all-start.3 = ((bf16[64,16,768]{2,1,0:T(8,128)(2,1)}), bf16[64,16,768]{2,1,0:T(8,128)(2,1)}, u32[]{:S(2)}, u32[]{:S(2)}) async-start(bf16[64,16,768]{2,1,0:T(8,128)(2,1)} %bitcast.48), calls=%async_computation.3 | async-start | bytes 3145728 | tf_op jit(solution)/shard_map/all_to_all | solution.py:201
  148.7 16.2 %collective-permute-start.14 = (bf16[1024,256]{1,0:T(8,128)(2,1)S(1)}, bf16[1024,256]{1,0:T(8,128)(2,1)S(1)}, u32[]{:S(2)}, u32[]{:S(2)}) collective-permute-start(bf16[1024,256]{1,0:T(8,128)(2,1)S(1)} %add_convert_fusion.2), channel_id=1, source_target_pairs={{0,1},{1,2},{2,3},{3,4},{4,5},{5,6},{6,7},{7,0},{8,9},{9,10},{10,1... | collective-permute-start | bytes 1572872 | tf_op jit(solution)/shard_map/ppermute | solution.py:197
  152.0 15.0 %collective-permute-start.16 = (bf16[1024,256]{1,0:T(8,128)(2,1)S(1)}, bf16[1024,256]{1,0:T(8,128)(2,1)S(1)}, u32[]{:S(2)}, u32[]{:S(2)}) collective-permute-start(bf16[1024,256]{1,0:T(8,128)(2,1)S(1)} %add_convert_fusion.1), channel_id=1, source_target_pairs={{0,7},{1,0},{2,1},{3,2},{4,3},{5,4},{6,5},{7,6},{8,15},{9,8},{10,9... | collective-permute-start | bytes 1572872 | tf_op jit(solution)/shard_map/ppermute | solution.py:197
  156.5 7.1 %copy-start.5 = (bf16[352,1024]{1,0:T(8,128)(2,1)S(1)}, bf16[352,1024]{1,0:T(8,128)(2,1)}, u32[]{:S(2)}) copy-start(bf16[352,1024]{1,0:T(8,128)(2,1)} %get-tuple-element.37.refs_13_) | copy-start | bytes 2162692
  164.1 28.3 %copy-start.7 = (bf16[1024,128]{1,0:T(8,128)(2,1)S(1)}, bf16[1024,128]{1,0:T(8,128)(2,1)}, u32[]{:S(2)}) copy-start(bf16[1024,128]{1,0:T(8,128)(2,1)} %get-tuple-element.25) | copy-start | bytes 786436
  185.9 24.2 %all-to-all-start.2 = ((bf16[64,16,256]{2,1,0:T(8,128)(2,1)}), bf16[64,16,256]{2,1,0:T(8,128)(2,1)S(1)}, u32[]{:S(2)}, u32[]{:S(2)}) async-start(bf16[64,16,256]{2,1,0:T(8,128)(2,1)} %bitcast.10), calls=%async_computation.2 | async-start | bytes 1048576 | tf_op jit(solution)/shard_map/all_to_all | solution.py:201
  194.2 15.9 %collective-permute-start.17 = (bf16[128,256]{1,0:T(8,128)(2,1)S(1)}, bf16[128,256]{1,0:T(8,128)(2,1)S(1)}, u32[]{:S(2)}, u32[]{:S(2)}) collective-permute-start(bf16[128,256]{1,0:T(8,128)(2,1)S(1)} %get-tuple-element.51), channel_id=1, source_target_pairs={{0,4},{1,5},{2,6},{3,7},{4,0},{5,1},{6,2},{7,3},{8,12},{9,13},{10,... | collective-permute-start | bytes 196616 | tf_op jit(solution)/shard_map/ppermute | solution.py:197
  199.0 11.1 %collective-permute-start.19 = (bf16[128,256]{1,0:T(8,128)(2,1)S(1)}, bf16[128,256]{1,0:T(8,128)(2,1)S(1)}, u32[]{:S(2)}, u32[]{:S(2)}) collective-permute-start(bf16[128,256]{1,0:T(8,128)(2,1)S(1)} %get-tuple-element.52), channel_id=1, source_target_pairs={{0,5},{1,6},{2,7},{3,0},{4,1},{5,2},{6,3},{7,4},{8,13},{9,14},{10,... | collective-permute-start | bytes 196616 | tf_op jit(solution)/shard_map/ppermute | solution.py:197
  201.0 9.1 %collective-permute-start.18 = (bf16[128,256]{1,0:T(8,128)(2,1)S(1)}, bf16[128,256]{1,0:T(8,128)(2,1)S(1)}, u32[]{:S(2)}, u32[]{:S(2)}) collective-permute-start(bf16[128,256]{1,0:T(8,128)(2,1)S(1)} %get-tuple-element.53), channel_id=1, source_target_pairs={{0,3},{1,4},{2,5},{3,6},{4,7},{5,0},{6,1},{7,2},{8,11},{9,12},{10,... | collective-permute-start | bytes 196616 | tf_op jit(solution)/shard_map/ppermute | solution.py:197

commit v4 on v3

--- a/solution.py
+++ b/solution.py
@@ -111,7 +111,7 @@
         in_specs=[SMEM] + [VMEM] * (len(arrays) + 3),
         out_specs=[VMEM] * 3,
         compiler_params=PARAMS,
-        cost_estimate=pl.CostEstimate(flops=36 * 10**9, bytes_accessed=1000, transcendentals=0),
+        cost_estimate=pl.CostEstimate(flops=3400 * 10**7, bytes_accessed=1000, transcendentals=0),
         name="first_products",
     )(me, *arrays, *weights)
 
@@ -175,7 +175,7 @@
         in_specs=[SMEM] + [VMEM] * (len(arrays) + 2),
         out_specs=[VMEM] * 3,
         compiler_params=PARAMS,
-        cost_estimate=pl.CostEstimate(flops=20 * 10**9, bytes_accessed=1000, transcendentals=0),
+        cost_estimate=pl.CostEstimate(flops=5 * 10**9, bytes_accessed=1000, transcendentals=0),
         name="weight_grads",
     )(me, *arrays, grads, hidden)
 

time: 213 us -> 206 us (0.967)
  waiting for transfers between devices: 52.3 us -> 46.7 us
  starting transfers between devices: 113 us -> 116 us
    all_to_all x4, waiting for transfers between devices: 29.3 us -> 15 us  [over_ep(): lax.all_to_all(value.reshape(shape), 'ep', split_axis=0, concat_axis=0, t...]
    ppermute x20, waiting for transfers between devices: 23 us -> 31.7 us  [moved(): lax.ppermute(value, 'tp', [(i, (i + by) % ring) for i in range(ring)])]
  transfers between devices with their start and end apart: 24 -> 24, of which waited for: 12 -> 13; matrix products, arithmetic and copies ran while one was open for 5% -> 3% of each run, Pallas kernels for 8% -> 8%
where the time goes in v4:
time: 206 us; the launch traced here: 203 us
  starting transfers between devices  116 us (56%)
  waiting for transfers between devices  46.7 us (23%)
  Pallas kernels  25.3 us (12%)
  matrix products  8.48 us (4%)
  local copies, waits for them, and re-layouts  3.71 us (2%)
  other arithmetic  2.09 us (1%)
    ppermute x20, starting transfers between devices, moved(): lax.ppermute(value, 'tp', [(i, (i + by) % ring) for i in range(ring)])  80.7 us
    all_to_all x4, starting transfers between devices, over_ep(): lax.all_to_all(value.reshape(shape), 'ep', split_axis=0, concat_axis=0, t...  35 us
    ppermute x20, waiting for transfers between devices, moved(): lax.ppermute(value, 'tp', [(i, (i + by) % ring) for i in range(ring)])  31.7 us
    all_to_all x4, waiting for transfers between devices, over_ep(): lax.all_to_all(value.reshape(shape), 'ep', split_axis=0, concat_axis=0, t...  15 us
    dot_general x8, matrix products, tn(): lax.dot_general(left, right, (((0,), (0,)), ((), ())), preferred_element_...  8.48 us
    pallas_call x1, Pallas kernels, weight_grads(): pl.pallas_call(kernel, out_shape=[jax.ShapeDtypeStruct((units, ring * wid...  7.02 us
    pallas_call x1, Pallas kernels, first_products(): pl.pallas_call(kernel, out_shape=[jax.ShapeDtypeStruct((units, rows), jnp...  6.67 us
    pallas_call x1, Pallas kernels, activations(): pl.pallas_call(kernel, out_shape=(jax.ShapeDtypeStruct((2 * units, rows),...  5.94 us
  transfers between devices with their start and end apart: 24, of which 13 were waited for; matrix products, arithmetic and copies ran while one was open for 3% of the time, Pallas kernels for 8%

profile of v4, /device:TPU:1, one launch (start us, length us, event | category | flops | bytes accessed | tf_op | source)
XLA Modules:
  0.0 203.0 jit_solution(16312112344499907493)
XLA Ops:
  0.7 2.5 %dispatch.2 = (bf16[1024,512]{1,0:T(8,128)(2,1)}, bf16[1024,128]{1,0:T(8,128)(2,1)}) custom-call(s32[6,128]{1,0:T(8,128)} %bitcast.52, f32[6,128]{1,0:T(8,128)} %bitcast.54, bf16[128,256]{1,0:T(8,128)(2,1)} %refs_0_.1, bf16[128,256]{1,0:T(8,128)(2,1)} %refs_1_.1), custom_call_target="tpu_custom_call" | custom-call | tf_op jit(solution)/shard_map/dispatch/pallas_call | solution.py:64
  3.1 11.6 %all-to-all-start = ((bf16[64,16,512]{2,1,0:T(8,128)(2,1)}), bf16[64,16,512]{2,1,0:T(8,128)(2,1)S(1)}, u32[]{:S(2)}, u32[]{:S(2)}) async-start(bf16[64,16,512]{2,1,0:T(8,128)(2,1)} %bitcast.49), calls=%async_computation | async-start | bytes 2097152 | tf_op jit(solution)/shard_map/all_to_all | solution.py:201
  14.8 10.6 %collective-permute-start = (bf16[128,512]{1,0:T(8,128)(2,1)S(1)}, bf16[128,512]{1,0:T(8,128)(2,1)S(1)}, u32[]{:S(2)}, u32[]{:S(2)}) collective-permute-start(bf16[128,512]{1,0:T(8,128)(2,1)S(1)} %pad_maximum_fusion), channel_id=1, source_target_pairs={{0,4},{1,5},{2,6},{3,7},{4,0},{5,1},{6,2},{7,3},{8,12},{9,13},{10,... | collective-permute-start | bytes 393224 | tf_op jit(solution)/shard_map/ppermute | solution.py:197
  25.5 1.9 collective-permute-start.1
  27.4 5.2 %collective-permute-start.2 = (bf16[128,256]{1,0:T(8,128)(2,1)S(1)}, bf16[128,256]{1,0:T(8,128)(2,1)S(1)}, u32[]{:S(2)}, u32[]{:S(2)}) collective-permute-start(bf16[128,256]{1,0:T(8,128)(2,1)S(1)} %copy-done.10), channel_id=1, source_target_pairs={{0,3},{1,4},{2,5},{3,6},{4,7},{5,0},{6,1},{7,2},{8,11},{9,12},{10,... | collective-permute-start | bytes 196616 | tf_op jit(solution)/shard_map/ppermute | solution.py:197
  33.2 1.8 collective-permute-done.1.refs_2_
  35.0 5.0 %collective-permute-done.2.refs_3_ = bf16[128,256]{1,0:T(8,128)(2,1)S(1)} collective-permute-done((bf16[128,256]{1,0:T(8,128)(2,1)S(1)}, bf16[128,256]{1,0:T(8,128)(2,1)S(1)}, u32[]{:S(2)}, u32[]{:S(2)}) %collective-permute-start.2) | collective-permute-done | bytes 65568 | tf_op jit(solution)/shard_map/ppermute | solution.py:197
  40.6 3.2 %dispatch.3 = (bf16[1024,1024]{1,0:T(8,128)(2,1)}, bf16[1024,128]{1,0:T(8,128)(2,1)}) custom-call(s32[6,128]{1,0:T(8,128)} %bitcast.53, f32[6,128]{1,0:T(8,128)} %bitcast.55, bf16[128,256]{1,0:T(8,128)(2,1)} %get-tuple-element.55.refs_0_, bf16[128,256]{1,0:T(8,128)(2,1)} %get-tuple-element.54.refs_1_, bf16[128,256]{1,0:T(8,128)(2,1)} %copy-done.14, ...), custom_call_target="tpu_custom_call" | custom-call | tf_op jit(solution)/shard_map/dispatch/pallas_call | solution.py:64
  43.8 1.0 fusion.29
  44.8 3.0 %collective-permute-start.3 = (bf16[1024,256]{1,0:T(8,128)(2,1)}, bf16[1024,256]{1,0:T(8,128)(2,1)}, u32[]{:S(2)}, u32[]{:S(2)}) collective-permute-start(bf16[1024,256]{1,0:T(8,128)(2,1)} %get-tuple-element.32.refs_0_), channel_id=1, source_target_pairs={{0,1},{1,2},{2,3},{3,4},{4,5},{5,6},{6,7},{7,0},{8,9},{9,10},{10,1... | collective-permute-start | bytes 1572872 | tf_op jit(solution)/shard_map/ppermute | solution.py:197
  47.8 8.6 %collective-permute-start.6 = (bf16[1024,256]{1,0:T(8,128)(2,1)}, bf16[1024,256]{1,0:T(8,128)(2,1)}, u32[]{:S(2)}, u32[]{:S(2)}) collective-permute-start(bf16[1024,256]{1,0:T(8,128)(2,1)} %get-tuple-element.33.refs_5_.refs_7_), channel_id=1, source_target_pairs={{0,7},{1,0},{2,1},{3,2},{4,3},{5,4},{6,5},{7,6},{8,15},{9,8},{10,9... | collective-permute-start | bytes 1572872 | tf_op jit(solution)/shard_map/ppermute | solution.py:197
  56.4 3.4 %collective-permute-start.9 = (bf16[1024,256]{1,0:T(8,128)(2,1)}, bf16[1024,256]{1,0:T(8,128)(2,1)}, u32[]{:S(2)}, u32[]{:S(2)}) collective-permute-start(bf16[1024,256]{1,0:T(8,128)(2,1)} %get-tuple-element.32.refs_0_), channel_id=1, source_target_pairs={{0,7},{1,0},{2,1},{3,2},{4,3},{5,4},{6,5},{7,6},{8,15},{9,8},{10,9... | collective-permute-start | bytes 1572872 | tf_op jit(solution)/shard_map/ppermute | solution.py:197
  59.8 1.9 collective-permute-start.11
  61.7 7.4 %all-to-all-start.1 = ((bf16[64,16,1024]{2,1,0:T(8,128)(2,1)}), bf16[64,16,1024]{2,1,0:T(8,128)(2,1)S(1)}, u32[]{:S(2)}, u32[]{:S(2)}) async-start(bf16[64,16,1024]{2,1,0:T(8,128)(2,1)} %bitcast.46), calls=%async_computation.1 | async-start | bytes 4194304 | tf_op jit(solution)/shard_map/all_to_all | solution.py:201
  69.2 1.9 collective-permute-start.4
  71.1 4.9 %collective-permute-start.7 = (bf16[1024,256]{1,0:T(8,128)(2,1)}, bf16[1024,256]{1,0:T(8,128)(2,1)}, u32[]{:S(2)}, u32[]{:S(2)}) collective-permute-start(bf16[1024,256]{1,0:T(8,128)(2,1)} %collective-permute-done.6.refs_7_.refs_9_), channel_id=1, source_target_pairs={{0,7},{1,0},{2,1},{3,2},{4,3},{5,4},{6,5},{7,6},{8,15},{9,8},{10,9... | collective-permute-start | bytes 1572872 | tf_op jit(solution)/shard_map/ppermute | solution.py:197
  76.0 1.8 collective-permute-done.9.refs_2_
  77.8 5.3 %collective-permute-start.10 = (bf16[1024,256]{1,0:T(8,128)(2,1)}, bf16[1024,256]{1,0:T(8,128)(2,1)}, u32[]{:S(2)}, u32[]{:S(2)}) collective-permute-start(bf16[1024,256]{1,0:T(8,128)(2,1)} %collective-permute-done.9.refs_2_), channel_id=1, source_target_pairs={{0,7},{1,0},{2,1},{3,2},{4,3},{5,4},{6,5},{7,6},{8,15},{9,8},{10,9... | collective-permute-start | bytes 1572872 | tf_op jit(solution)/shard_map/ppermute | solution.py:197
  83.1 1.9 collective-permute-start.12
  85.1 0.8 fusion.11
  85.9 2.4 %collective-permute-done.4.refs_3_ = bf16[1024,256]{1,0:T(8,128)(2,1)} collective-permute-done((bf16[1024,256]{1,0:T(8,128)(2,1)}, bf16[1024,256]{1,0:T(8,128)(2,1)}, u32[]{:S(2)}, u32[]{:S(2)}) %collective-permute-start.4) | collective-permute-done | bytes 524320 | tf_op jit(solution)/shard_map/ppermute | solution.py:197
  88.4 1.9 collective-permute-start.5
  90.3 4.6 %collective-permute-start.8 = (bf16[1024,256]{1,0:T(8,128)(2,1)}, bf16[1024,256]{1,0:T(8,128)(2,1)S(1)}, u32[]{:S(2)}, u32[]{:S(2)}) collective-permute-start(bf16[1024,256]{1,0:T(8,128)(2,1)} %collective-permute-done.7.refs_9_.refs_11_), channel_id=1, source_target_pairs={{0,7},{1,0},{2,1},{3,2},{4,3},{5,4},{6,5},{7,6},{8,15},{9,8},{10,9... | collective-permute-start | bytes 1572872 | tf_op jit(solution)/shard_map/ppermute | solution.py:197
  94.9 5.4 %collective-permute-done.10.refs_4_ = bf16[1024,256]{1,0:T(8,128)(2,1)} collective-permute-done((bf16[1024,256]{1,0:T(8,128)(2,1)}, bf16[1024,256]{1,0:T(8,128)(2,1)}, u32[]{:S(2)}, u32[]{:S(2)}) %collective-permute-start.10) | collective-permute-done | bytes 524320 | tf_op jit(solution)/shard_map/ppermute | solution.py:197
  100.3 6.7 %first_products.1 = (f32[176,1024]{1,0:T(8,128)}, f32[176,1024]{1,0:T(8,128)}, f32[176,1024]{1,0:T(8,128)}) custom-call(s32[1]{0:T(128)} %bitcast.2.me_ref, bf16[1024,256]{1,0:T(8,128)(2,1)} %get-tuple-element.32.refs_0_, bf16[1024,256]{1,0:T(8,128)(2,1)} %collective-permute-done.3.refs_1_, bf16[1024,256]{1,0:T(8,128)(2,1)} %collective-permute-done.9.refs_2_, ...), custom_call_target="tpu_custom_call" | custom-call | flops 33999998976 | bytes 1000 | tf_op jit(solution)/shard_map/first_products/pallas_call | solution.py:108
  107.6 3.9 %collective-permute-done.8.refs_2_.refs_12_ = bf16[1024,256]{1,0:T(8,128)(2,1)S(1)} collective-permute-done((bf16[1024,256]{1,0:T(8,128)(2,1)}, bf16[1024,256]{1,0:T(8,128)(2,1)S(1)}, u32[]{:S(2)}, u32[]{:S(2)}) %collective-permute-start.8) | collective-permute-done | bytes 524320 | tf_op jit(solution)/shard_map/ppermute | solution.py:197
  111.5 7.4 %all-to-all-done.1 = bf16[64,16,1024]{2,1,0:T(8,128)(2,1)S(1)} async-done(((bf16[64,16,1024]{2,1,0:T(8,128)(2,1)}), bf16[64,16,1024]{2,1,0:T(8,128)(2,1)S(1)}, u32[]{:S(2)}, u32[]{:S(2)}) %all-to-all-start.1) | async-done | bytes 2097184 | tf_op jit(solution)/shard_map/all_to_all | solution.py:201
  118.9 1.3 copy-done.5
  120.2 5.9 %activations.1 = (bf16[352,1024]{1,0:T(8,128)(2,1)}, bf16[176,1024]{1,0:T(8,128)(2,1)}) custom-call(s32[1]{0:T(128)} %bitcast.2.me_ref, bf16[1024,1024]{1,0:T(8,128)(2,1)} %bitcast.43, bf16[1024,256]{1,0:T(8,128)(2,1)} %copy-done.7, bf16[1024,256]{1,0:T(8,128)(2,1)} %copy-done.8, bf16[176,2048]{1,0:T(8,128)(2,1)} %bitcast.28, bf16[176,2048]{1,0:T(8,128)(2,1)} %bitcast.36, ...), custom_call_target="tpu_custom_call" | custom-call | tf_op jit(solution)/shard_map/activations/pallas_call | solution.py:142
  126.2 3.3 %convolution_convert_fusion = bf16[1024,768]{1,0:T(8,128)(2,1)} fusion(bf16[352,1024]{1,0:T(8,128)(2,1)} %get-tuple-element.37.refs_13_, bf16[352,256]{1,0:T(8,128)(2,1)S(1)} %copy-done.13, bf16[352,256]{1,0:T(8,128)(2,1)S(1)} %copy-done.12, bf16[352,256]{1,0:T(8,128)(2,1)S(1)} %copy-done.11), kind=kOutput, calls=%fused_computation.16 | convolution fusion | flops 556056576 | bytes 2834432 | tf_op jit(solution)/shard_map/dot_general | solution.py:19
  129.5 7.3 %all-to-all-start.3 = ((bf16[64,16,768]{2,1,0:T(8,128)(2,1)}), bf16[64,16,768]{2,1,0:T(8,128)(2,1)}, u32[]{:S(2)}, u32[]{:S(2)}) async-start(bf16[64,16,768]{2,1,0:T(8,128)(2,1)} %bitcast.48), calls=%async_computation.3 | async-start | bytes 3145728 | tf_op jit(solution)/shard_map/all_to_all | solution.py:201
  137.4 1.9 collective-permute-start.13
  139.8 4.9 %collective-permute-start.15 = (bf16[1024,256]{1,0:T(8,128)(2,1)S(1)}, bf16[1024,256]{1,0:T(8,128)(2,1)S(1)}, u32[]{:S(2)}, u32[]{:S(2)}) collective-permute-start(bf16[1024,256]{1,0:T(8,128)(2,1)S(1)} %convolution_convert_fusion.2), channel_id=1, source_target_pairs={{0,7},{1,0},{2,1},{3,2},{4,3},{5,4},{6,5},{7,6},{8,15},{9,8},{10,9... | collective-permute-start | bytes 1572872 | tf_op jit(solution)/shard_map/ppermute | solution.py:197
  145.7 8.4 %collective-permute-done.13 = bf16[1024,256]{1,0:T(8,128)(2,1)S(1)} collective-permute-done((bf16[1024,256]{1,0:T(8,128)(2,1)S(1)}, bf16[1024,256]{1,0:T(8,128)(2,1)S(1)}, u32[]{:S(2)}, u32[]{:S(2)}) %collective-permute-start.13) | collective-permute-done | bytes 524320 | tf_op jit(solution)/shard_map/ppermute | solution.py:197
  154.2 2.1 %collective-permute-start.14 = (bf16[1024,256]{1,0:T(8,128)(2,1)S(1)}, bf16[1024,256]{1,0:T(8,128)(2,1)S(1)}, u32[]{:S(2)}, u32[]{:S(2)}) collective-permute-start(bf16[1024,256]{1,0:T(8,128)(2,1)S(1)} %add_convert_fusion.2), channel_id=1, source_target_pairs={{0,1},{1,2},{2,3},{3,4},{4,5},{5,6},{6,7},{7,0},{8,9},{9,10},{10,1... | collective-permute-start | bytes 1572872 | tf_op jit(solution)/shard_map/ppermute | solution.py:197
  156.4 4.6 %collective-permute-start.16 = (bf16[1024,256]{1,0:T(8,128)(2,1)S(1)}, bf16[1024,256]{1,0:T(8,128)(2,1)S(1)}, u32[]{:S(2)}, u32[]{:S(2)}) collective-permute-start(bf16[1024,256]{1,0:T(8,128)(2,1)S(1)} %add_convert_fusion.1), channel_id=1, source_target_pairs={{0,7},{1,0},{2,1},{3,2},{4,3},{5,4},{6,5},{7,6},{8,15},{9,8},{10,9... | collective-permute-start | bytes 1572872 | tf_op jit(solution)/shard_map/ppermute | solution.py:197
  161.5 7.0 %weight_grads.1 = (bf16[176,2048]{1,0:T(8,128)(2,1)}, bf16[176,2048]{1,0:T(8,128)(2,1)}, bf16[176,2048]{1,0:T(8,128)(2,1)}) custom-call(s32[1]{0:T(128)} %bitcast.2.me_ref, bf16[1024,256]{1,0:T(8,128)(2,1)} %get-tuple-element.32.refs_0_, bf16[1024,256]{1,0:T(8,128)(2,1)} %collective-permute-done.3.refs_1_, bf16[1024,256]{1,0:T(8,128)(2,1)} %collective-permute-done.9.refs_2_, ...), custom_call_target="tpu_custom_call" | custom-call | flops 5000000000 | bytes 1000 | tf_op jit(solution)/shard_map/weight_grads/pallas_call | solution.py:172
  168.5 1.1 collective-permute-done.14
  169.6 1.2 collective-permute-done.16
  170.9 1.0 add_convert_fusion
  171.9 3.9 %all-to-all-done.3 = bf16[64,16,768]{2,1,0:T(8,128)(2,1)} async-done(((bf16[64,16,768]{2,1,0:T(8,128)(2,1)}), bf16[64,16,768]{2,1,0:T(8,128)(2,1)}, u32[]{:S(2)}, u32[]{:S(2)}) %all-to-all-start.3) | async-done | bytes 1572896 | tf_op jit(solution)/shard_map/all_to_all | solution.py:201
  175.8 8.6 %all-to-all-start.2 = ((bf16[64,16,256]{2,1,0:T(8,128)(2,1)}), bf16[64,16,256]{2,1,0:T(8,128)(2,1)S(1)}, u32[]{:S(2)}, u32[]{:S(2)}) async-start(bf16[64,16,256]{2,1,0:T(8,128)(2,1)} %bitcast.10), calls=%async_computation.2 | async-start | bytes 1048576 | tf_op jit(solution)/shard_map/all_to_all | solution.py:201
  184.4 1.8 convolution_convert_fusion.6
  186.2 4.2 %collective-permute-start.17 = (bf16[128,256]{1,0:T(8,128)(2,1)S(1)}, bf16[128,256]{1,0:T(8,128)(2,1)S(1)}, u32[]{:S(2)}, u32[]{:S(2)}) collective-permute-start(bf16[128,256]{1,0:T(8,128)(2,1)S(1)} %get-tuple-element.51), channel_id=1, source_target_pairs={{0,4},{1,5},{2,6},{3,7},{4,0},{5,1},{6,2},{7,3},{8,12},{9,13},{10,... | collective-permute-start | bytes 196616 | tf_op jit(solution)/shard_map/ppermute | solution.py:197
  190.4 2.6 %collective-permute-start.19 = (bf16[128,256]{1,0:T(8,128)(2,1)S(1)}, bf16[128,256]{1,0:T(8,128)(2,1)S(1)}, u32[]{:S(2)}, u32[]{:S(2)}) collective-permute-start(bf16[128,256]{1,0:T(8,128)(2,1)S(1)} %get-tuple-element.52), channel_id=1, source_target_pairs={{0,5},{1,6},{2,7},{3,0},{4,1},{5,2},{6,3},{7,4},{8,13},{9,14},{10,... | collective-permute-start | bytes 196616 | tf_op jit(solution)/shard_map/ppermute | solution.py:197
  193.0 5.3 %collective-permute-start.18 = (bf16[128,256]{1,0:T(8,128)(2,1)S(1)}, bf16[128,256]{1,0:T(8,128)(2,1)S(1)}, u32[]{:S(2)}, u32[]{:S(2)}) collective-permute-start(bf16[128,256]{1,0:T(8,128)(2,1)S(1)} %get-tuple-element.53), channel_id=1, source_target_pairs={{0,3},{1,4},{2,5},{3,6},{4,7},{5,0},{6,1},{7,2},{8,11},{9,12},{10,... | collective-permute-start | bytes 196616 | tf_op jit(solution)/shard_map/ppermute | solution.py:197
  198.4 3.7 %all-to-all-done.2 = bf16[64,16,256]{2,1,0:T(8,128)(2,1)S(1)} async-done(((bf16[64,16,256]{2,1,0:T(8,128)(2,1)}), bf16[64,16,256]{2,1,0:T(8,128)(2,1)S(1)}, u32[]{:S(2)}, u32[]{:S(2)}) %all-to-all-start.2) | async-done | bytes 524320 | tf_op jit(solution)/shard_map/all_to_all | solution.py:201
  202.1 0.9 add_convert_fusion.3
  (53 shorter events, 4.8 us)
Async XLA Ops:
  0.6 14.2 %copy-start.10 = (bf16[128,256]{1,0:T(8,128)(2,1)S(1)}, bf16[128,256]{1,0:T(8,128)(2,1)}, u32[]{:S(2)}) copy-start(bf16[128,256]{1,0:T(8,128)(2,1)} %refs_1_.1) | copy-start | bytes 196612
  0.6 14.2 %copy-start.9 = (bf16[128,256]{1,0:T(8,128)(2,1)S(1)}, bf16[128,256]{1,0:T(8,128)(2,1)}, u32[]{:S(2)}) copy-start(bf16[128,256]{1,0:T(8,128)(2,1)} %refs_0_.1) | copy-start | bytes 196612
  3.1 40.6 %all-to-all-start = ((bf16[64,16,512]{2,1,0:T(8,128)(2,1)}), bf16[64,16,512]{2,1,0:T(8,128)(2,1)S(1)}, u32[]{:S(2)}, u32[]{:S(2)}) async-start(bf16[64,16,512]{2,1,0:T(8,128)(2,1)} %bitcast.49), calls=%async_computation | async-start | bytes 2097152 | tf_op jit(solution)/shard_map/all_to_all | solution.py:201
  14.8 17.7 %collective-permute-start = (bf16[128,512]{1,0:T(8,128)(2,1)S(1)}, bf16[128,512]{1,0:T(8,128)(2,1)S(1)}, u32[]{:S(2)}, u32[]{:S(2)}) collective-permute-start(bf16[128,512]{1,0:T(8,128)(2,1)S(1)} %pad_maximum_fusion), channel_id=1, source_target_pairs={{0,4},{1,5},{2,6},{3,7},{4,0},{5,1},{6,2},{7,3},{8,12},{9,13},{10,... | collective-permute-start | bytes 393224 | tf_op jit(solution)/shard_map/ppermute | solution.py:197
  25.5 9.5 %collective-permute-start.1 = (bf16[128,256]{1,0:T(8,128)(2,1)S(1)}, bf16[128,256]{1,0:T(8,128)(2,1)S(1)}, u32[]{:S(2)}, u32[]{:S(2)}) collective-permute-start(bf16[128,256]{1,0:T(8,128)(2,1)S(1)} %copy-done.9), channel_id=1, source_target_pairs={{0,5},{1,6},{2,7},{3,0},{4,1},{5,2},{6,3},{7,4},{8,13},{9,14},{10,... | collective-permute-start | bytes 196616 | tf_op jit(solution)/shard_map/ppermute | solution.py:197
  27.4 12.6 %collective-permute-start.2 = (bf16[128,256]{1,0:T(8,128)(2,1)S(1)}, bf16[128,256]{1,0:T(8,128)(2,1)S(1)}, u32[]{:S(2)}, u32[]{:S(2)}) collective-permute-start(bf16[128,256]{1,0:T(8,128)(2,1)S(1)} %copy-done.10), channel_id=1, source_target_pairs={{0,3},{1,4},{2,5},{3,6},{4,7},{5,0},{6,1},{7,2},{8,11},{9,12},{10,... | collective-permute-start | bytes 196616 | tf_op jit(solution)/shard_map/ppermute | solution.py:197
  35.0 5.0 %copy-start.14 = (bf16[128,256]{1,0:T(8,128)(2,1)}, bf16[128,256]{1,0:T(8,128)(2,1)S(1)}, u32[]{:S(2)}) copy-start(bf16[128,256]{1,0:T(8,128)(2,1)S(1)} %collective-permute-done.1.refs_2_) | copy-start | bytes 196612
  40.0 0.6 copy-start.15
  44.8 24.4 %collective-permute-start.3 = (bf16[1024,256]{1,0:T(8,128)(2,1)}, bf16[1024,256]{1,0:T(8,128)(2,1)}, u32[]{:S(2)}, u32[]{:S(2)}) collective-permute-start(bf16[1024,256]{1,0:T(8,128)(2,1)} %get-tuple-element.32.refs_0_), channel_id=1, source_target_pairs={{0,1},{1,2},{2,3},{3,4},{4,5},{5,6},{6,7},{7,0},{8,9},{9,10},{10,1... | collective-permute-start | bytes 1572872 | tf_op jit(solution)/shard_map/ppermute | solution.py:197
  47.8 23.3 %collective-permute-start.6 = (bf16[1024,256]{1,0:T(8,128)(2,1)}, bf16[1024,256]{1,0:T(8,128)(2,1)}, u32[]{:S(2)}, u32[]{:S(2)}) collective-permute-start(bf16[1024,256]{1,0:T(8,128)(2,1)} %get-tuple-element.33.refs_5_.refs_7_), channel_id=1, source_target_pairs={{0,7},{1,0},{2,1},{3,2},{4,3},{5,4},{6,5},{7,6},{8,15},{9,8},{10,9... | collective-permute-start | bytes 1572872 | tf_op jit(solution)/shard_map/ppermute | solution.py:197
  56.4 21.4 %collective-permute-start.9 = (bf16[1024,256]{1,0:T(8,128)(2,1)}, bf16[1024,256]{1,0:T(8,128)(2,1)}, u32[]{:S(2)}, u32[]{:S(2)}) collective-permute-start(bf16[1024,256]{1,0:T(8,128)(2,1)} %get-tuple-element.32.refs_0_), channel_id=1, source_target_pairs={{0,7},{1,0},{2,1},{3,2},{4,3},{5,4},{6,5},{7,6},{8,15},{9,8},{10,9... | collective-permute-start | bytes 1572872 | tf_op jit(solution)/shard_map/ppermute | solution.py:197
  59.8 23.3 %collective-permute-start.11 = (bf16[1024,256]{1,0:T(8,128)(2,1)}, bf16[1024,256]{1,0:T(8,128)(2,1)}, u32[]{:S(2)}, u32[]{:S(2)}) collective-permute-start(bf16[1024,256]{1,0:T(8,128)(2,1)} %get-tuple-element.33.refs_5_.refs_7_), channel_id=1, source_target_pairs={{0,1},{1,2},{2,3},{3,4},{4,5},{5,6},{6,7},{7,0},{8,9},{9,10},{10,1... | collective-permute-start | bytes 1572872 | tf_op jit(solution)/shard_map/ppermute | solution.py:197
  61.7 23.4 %copy-start = (bf16[1,176,2048]{2,1,0:T(8,128)(2,1)S(1)}, bf16[1,176,2048]{2,1,0:T(8,128)(2,1)}, u32[]{:S(2)}) copy-start(bf16[1,176,2048]{2,1,0:T(8,128)(2,1)} %param.11) | copy-start | bytes 2162692
  61.7 23.4 %copy-start.2 = (bf16[1,176,2048]{2,1,0:T(8,128)(2,1)S(1)}, bf16[1,176,2048]{2,1,0:T(8,128)(2,1)}, u32[]{:S(2)}) copy-start(bf16[1,176,2048]{2,1,0:T(8,128)(2,1)} %param.12) | copy-start | bytes 2162692
  61.7 57.1 %all-to-all-start.1 = ((bf16[64,16,1024]{2,1,0:T(8,128)(2,1)}), bf16[64,16,1024]{2,1,0:T(8,128)(2,1)S(1)}, u32[]{:S(2)}, u32[]{:S(2)}) async-start(bf16[64,16,1024]{2,1,0:T(8,128)(2,1)} %bitcast.46), calls=%async_computation.1 | async-start | bytes 4194304 | tf_op jit(solution)/shard_map/all_to_all | solution.py:201
  69.2 19.2 %collective-permute-start.4 = (bf16[1024,256]{1,0:T(8,128)(2,1)}, bf16[1024,256]{1,0:T(8,128)(2,1)}, u32[]{:S(2)}, u32[]{:S(2)}) collective-permute-start(bf16[1024,256]{1,0:T(8,128)(2,1)} %collective-permute-done.3.refs_1_), channel_id=1, source_target_pairs={{0,1},{1,2},{2,3},{3,4},{4,5},{5,6},{6,7},{7,0},{8,9},{9,10},{10,1... | collective-permute-start | bytes 1572872 | tf_op jit(solution)/shard_map/ppermute | solution.py:197
  71.1 19.1 %collective-permute-start.7 = (bf16[1024,256]{1,0:T(8,128)(2,1)}, bf16[1024,256]{1,0:T(8,128)(2,1)}, u32[]{:S(2)}, u32[]{:S(2)}) collective-permute-start(bf16[1024,256]{1,0:T(8,128)(2,1)} %collective-permute-done.6.refs_7_.refs_9_), channel_id=1, source_target_pairs={{0,7},{1,0},{2,1},{3,2},{4,3},{5,4},{6,5},{7,6},{8,15},{9,8},{10,9... | collective-permute-start | bytes 1572872 | tf_op jit(solution)/shard_map/ppermute | solution.py:197
  77.8 22.5 %collective-permute-start.10 = (bf16[1024,256]{1,0:T(8,128)(2,1)}, bf16[1024,256]{1,0:T(8,128)(2,1)}, u32[]{:S(2)}, u32[]{:S(2)}) collective-permute-start(bf16[1024,256]{1,0:T(8,128)(2,1)} %collective-permute-done.9.refs_2_), channel_id=1, source_target_pairs={{0,7},{1,0},{2,1},{3,2},{4,3},{5,4},{6,5},{7,6},{8,15},{9,8},{10,9... | collective-permute-start | bytes 1572872 | tf_op jit(solution)/shard_map/ppermute | solution.py:197
  83.1 17.1 %collective-permute-start.12 = (bf16[1024,256]{1,0:T(8,128)(2,1)}, bf16[1024,256]{1,0:T(8,128)(2,1)}, u32[]{:S(2)}, u32[]{:S(2)}) collective-permute-start(bf16[1024,256]{1,0:T(8,128)(2,1)} %collective-permute-done.11.refs_6_.refs_8_), channel_id=1, source_target_pairs={{0,1},{1,2},{2,3},{3,4},{4,5},{5,6},{6,7},{7,0},{8,9},{9,10},{10,1... | collective-permute-start | bytes 1572872 | tf_op jit(solution)/shard_map/ppermute | solution.py:197
  88.4 19.2 %collective-permute-start.5 = (bf16[1024,256]{1,0:T(8,128)(2,1)}, bf16[1024,256]{1,0:T(8,128)(2,1)S(1)}, u32[]{:S(2)}, u32[]{:S(2)}) collective-permute-start(bf16[1024,256]{1,0:T(8,128)(2,1)} %collective-permute-done.4.refs_3_), channel_id=1, source_target_pairs={{0,1},{1,2},{2,3},{3,4},{4,5},{5,6},{6,7},{7,0},{8,9},{9,10},{10,1... | collective-permute-start | bytes 1572872 | tf_op jit(solution)/shard_map/ppermute | solution.py:197
  90.3 21.2 %collective-permute-start.8 = (bf16[1024,256]{1,0:T(8,128)(2,1)}, bf16[1024,256]{1,0:T(8,128)(2,1)S(1)}, u32[]{:S(2)}, u32[]{:S(2)}) collective-permute-start(bf16[1024,256]{1,0:T(8,128)(2,1)} %collective-permute-done.7.refs_9_.refs_11_), channel_id=1, source_target_pairs={{0,7},{1,0},{2,1},{3,2},{4,3},{5,4},{6,5},{7,6},{8,15},{9,8},{10,9... | collective-permute-start | bytes 1572872 | tf_op jit(solution)/shard_map/ppermute | solution.py:197
  107.6 11.3 %copy-start.7 = (bf16[1024,256]{1,0:T(8,128)(2,1)}, bf16[1024,256]{1,0:T(8,128)(2,1)S(1)}, u32[]{:S(2)}) copy-start(bf16[1024,256]{1,0:T(8,128)(2,1)S(1)} %collective-permute-done.5.refs_1_.refs_6_) | copy-start | bytes 1572868
  111.5 7.4 %copy-start.8 = (bf16[1024,256]{1,0:T(8,128)(2,1)}, bf16[1024,256]{1,0:T(8,128)(2,1)S(1)}, u32[]{:S(2)}) copy-start(bf16[1024,256]{1,0:T(8,128)(2,1)S(1)} %collective-permute-done.8.refs_2_.refs_12_) | copy-start | bytes 1572868
  118.9 1.3 copy-start.5
  120.2 5.9 %copy-start.11 = (bf16[352,256]{1,0:T(8,128)(2,1)S(1)}, bf16[352,256]{1,0:T(8,128)(2,1)}, u32[]{:S(2)}) copy-start(bf16[352,256]{1,0:T(8,128)(2,1)} %get-tuple-element.46) | copy-start | bytes 540676
  120.2 5.9 %copy-start.12 = (bf16[352,256]{1,0:T(8,128)(2,1)S(1)}, bf16[352,256]{1,0:T(8,128)(2,1)}, u32[]{:S(2)}) copy-start(bf16[352,256]{1,0:T(8,128)(2,1)} %get-tuple-element.47) | copy-start | bytes 540676
  120.2 5.9 %copy-start.13 = (bf16[352,256]{1,0:T(8,128)(2,1)S(1)}, bf16[352,256]{1,0:T(8,128)(2,1)}, u32[]{:S(2)}) copy-start(bf16[352,256]{1,0:T(8,128)(2,1)} %get-tuple-element.48) | copy-start | bytes 540676
  129.5 7.4 %copy-start.1 = (bf16[1,176,2048]{2,1,0:T(8,128)(2,1)S(1)}, bf16[1,176,2048]{2,1,0:T(8,128)(2,1)}, u32[]{:S(2)}) copy-start(bf16[1,176,2048]{2,1,0:T(8,128)(2,1)} %param.11) | copy-start | bytes 2162692
  129.5 7.4 %copy-start.3 = (bf16[1,176,2048]{2,1,0:T(8,128)(2,1)S(1)}, bf16[1,176,2048]{2,1,0:T(8,128)(2,1)}, u32[]{:S(2)}) copy-start(bf16[1,176,2048]{2,1,0:T(8,128)(2,1)} %param.12) | copy-start | bytes 2162692
  129.5 7.4 %copy-start.4 = (bf16[352,1024]{1,0:T(8,128)(2,1)S(1)}, bf16[352,1024]{1,0:T(8,128)(2,1)}, u32[]{:S(2)}) copy-start(bf16[352,1024]{1,0:T(8,128)(2,1)} %get-tuple-element.37.refs_13_) | copy-start | bytes 2162692
  129.5 46.3 %all-to-all-start.3 = ((bf16[64,16,768]{2,1,0:T(8,128)(2,1)}), bf16[64,16,768]{2,1,0:T(8,128)(2,1)}, u32[]{:S(2)}, u32[]{:S(2)}) async-start(bf16[64,16,768]{2,1,0:T(8,128)(2,1)} %bitcast.48), calls=%async_computation.3 | async-start | bytes 3145728 | tf_op jit(solution)/shard_map/all_to_all | solution.py:201
  137.4 16.7 %collective-permute-start.13 = (bf16[1024,256]{1,0:T(8,128)(2,1)S(1)}, bf16[1024,256]{1,0:T(8,128)(2,1)S(1)}, u32[]{:S(2)}, u32[]{:S(2)}) collective-permute-start(bf16[1024,256]{1,0:T(8,128)(2,1)S(1)} %convolution_convert_fusion.4), channel_id=1, source_target_pairs={{0,1},{1,2},{2,3},{3,4},{4,5},{5,6},{6,7},{7,0},{8,9},{9,10},{10,1... | collective-permute-start | bytes 1572872 | tf_op jit(solution)/shard_map/ppermute | solution.py:197
  139.8 16.5 %collective-permute-start.15 = (bf16[1024,256]{1,0:T(8,128)(2,1)S(1)}, bf16[1024,256]{1,0:T(8,128)(2,1)S(1)}, u32[]{:S(2)}, u32[]{:S(2)}) collective-permute-start(bf16[1024,256]{1,0:T(8,128)(2,1)S(1)} %convolution_convert_fusion.2), channel_id=1, source_target_pairs={{0,7},{1,0},{2,1},{3,2},{4,3},{5,4},{6,5},{7,6},{8,15},{9,8},{10,9... | collective-permute-start | bytes 1572872 | tf_op jit(solution)/shard_map/ppermute | solution.py:197
  154.2 15.5 %collective-permute-start.14 = (bf16[1024,256]{1,0:T(8,128)(2,1)S(1)}, bf16[1024,256]{1,0:T(8,128)(2,1)S(1)}, u32[]{:S(2)}, u32[]{:S(2)}) collective-permute-start(bf16[1024,256]{1,0:T(8,128)(2,1)S(1)} %add_convert_fusion.2), channel_id=1, source_target_pairs={{0,1},{1,2},{2,3},{3,4},{4,5},{5,6},{6,7},{7,0},{8,9},{9,10},{10,1... | collective-permute-start | bytes 1572872 | tf_op jit(solution)/shard_map/ppermute | solution.py:197
  156.4 14.4 %collective-permute-start.16 = (bf16[1024,256]{1,0:T(8,128)(2,1)S(1)}, bf16[1024,256]{1,0:T(8,128)(2,1)S(1)}, u32[]{:S(2)}, u32[]{:S(2)}) collective-permute-start(bf16[1024,256]{1,0:T(8,128)(2,1)S(1)} %add_convert_fusion.1), channel_id=1, source_target_pairs={{0,7},{1,0},{2,1},{3,2},{4,3},{5,4},{6,5},{7,6},{8,15},{9,8},{10,9... | collective-permute-start | bytes 1572872 | tf_op jit(solution)/shard_map/ppermute | solution.py:197
  168.5 15.8 %copy-start.6 = (bf16[1024,128]{1,0:T(8,128)(2,1)S(1)}, bf16[1024,128]{1,0:T(8,128)(2,1)}, u32[]{:S(2)}) copy-start(bf16[1024,128]{1,0:T(8,128)(2,1)} %get-tuple-element.25) | copy-start | bytes 786436
  175.8 26.3 %all-to-all-start.2 = ((bf16[64,16,256]{2,1,0:T(8,128)(2,1)}), bf16[64,16,256]{2,1,0:T(8,128)(2,1)S(1)}, u32[]{:S(2)}, u32[]{:S(2)}) async-start(bf16[64,16,256]{2,1,0:T(8,128)(2,1)} %bitcast.10), calls=%async_computation.2 | async-start | bytes 1048576 | tf_op jit(solution)/shard_map/all_to_all | solution.py:201
  186.2 15.9 %collective-permute-start.17 = (bf16[128,256]{1,0:T(8,128)(2,1)S(1)}, bf16[128,256]{1,0:T(8,128)(2,1)S(1)}, u32[]{:S(2)}, u32[]{:S(2)}) collective-permute-start(bf16[128,256]{1,0:T(8,128)(2,1)S(1)} %get-tuple-element.51), channel_id=1, source_target_pairs={{0,4},{1,5},{2,6},{3,7},{4,0},{5,1},{6,2},{7,3},{8,12},{9,13},{10,... | collective-permute-start | bytes 196616 | tf_op jit(solution)/shard_map/ppermute | solution.py:197
  190.4 11.7 %collective-permute-start.19 = (bf16[128,256]{1,0:T(8,128)(2,1)S(1)}, bf16[128,256]{1,0:T(8,128)(2,1)S(1)}, u32[]{:S(2)}, u32[]{:S(2)}) collective-permute-start(bf16[128,256]{1,0:T(8,128)(2,1)S(1)} %get-tuple-element.52), channel_id=1, source_target_pairs={{0,5},{1,6},{2,7},{3,0},{4,1},{5,2},{6,3},{7,4},{8,13},{9,14},{10,... | collective-permute-start | bytes 196616 | tf_op jit(solution)/shard_map/ppermute | solution.py:197
  193.0 9.0 %collective-permute-start.18 = (bf16[128,256]{1,0:T(8,128)(2,1)S(1)}, bf16[128,256]{1,0:T(8,128)(2,1)S(1)}, u32[]{:S(2)}, u32[]{:S(2)}) collective-permute-start(bf16[128,256]{1,0:T(8,128)(2,1)S(1)} %get-tuple-element.53), channel_id=1, source_target_pairs={{0,3},{1,4},{2,5},{3,6},{4,7},{5,0},{6,1},{7,2},{8,11},{9,12},{10,... | collective-permute-start | bytes 196616 | tf_op jit(solution)/shard_map/ppermute | solution.py:197

commit v5 on v4

--- a/solution.py
+++ b/solution.py
@@ -84,23 +84,27 @@
     return arrays, table
 
 
-def first_products(me, ring, width, features, cotangents, weights):
+def first_products(me, ring, width, features, cotangents, weights, sums=(), flops=0):
     arrays, table = gathered(features + cotangents)
     rows = arrays[0].shape[0]
     units = weights[0].shape[0]
 
     def kernel(me_ref, *refs):
-        w_gate, w_up, w_down, a_ref, b_ref, dh_ref = refs[len(arrays) :]
+        w_gate, w_up, w_down = refs[len(arrays) : len(arrays) + 3]
+        a_ref, b_ref, dh_ref = refs[-3:]
+        if sums:
+            for into, held in zip(refs[-3:], refs[-6:-3]):
+                into[...] = held[...]
         for k, (number, column, owner) in enumerate(table):
             block = refs[number][:, column : column + width]
             start = lax.rem(me_ref[0] + owner % ring, ring) * width
             part = pl.ds(pl.multiple_of(start, width), width)
-            if k == 0:
+            if k == 0 and not sums:
                 a_ref[...], b_ref[...] = nt(w_gate[:, part], block), nt(w_up[:, part], block)
             elif k < len(features):
                 a_ref[...] += nt(w_gate[:, part], block)
                 b_ref[...] += nt(w_up[:, part], block)
-            elif k == len(features):
+            elif k == len(features) and not sums:
                 dh_ref[...] = nt(w_down[:, part], block)
             else:
                 dh_ref[...] += nt(w_down[:, part], block)
@@ -108,21 +112,22 @@
     return pl.pallas_call(
         kernel,
         out_shape=[jax.ShapeDtypeStruct((units, rows), jnp.float32)] * 3,
-        in_specs=[SMEM] + [VMEM] * (len(arrays) + 3),
+        in_specs=[SMEM] + [VMEM] * (len(arrays) + 3 + len(sums)),
         out_specs=[VMEM] * 3,
         compiler_params=PARAMS,
-        cost_estimate=pl.CostEstimate(flops=3400 * 10**7, bytes_accessed=1000, transcendentals=0),
+        cost_estimate=pl.CostEstimate(flops=flops, bytes_accessed=1000, transcendentals=0),
         name="first_products",
-    )(me, *arrays, *weights)
-
-
-def activations(me, ring, width, features, cotangents, weights, sums):
+    )(me, *arrays, *weights, *sums)
+
+
+def activations(me, ring, width, features, cotangents, weights, sums, away):
     arrays, table = gathered(features + cotangents)
     rows = arrays[0].shape[0]
     units = weights[0].shape[0]
 
     def kernel(me_ref, *refs):
-        w_gate, w_up, w_down, a_ref, b_ref, dh_ref, grads_ref, hidden_ref = refs[len(arrays) :]
+        w_gate, w_up, w_down, a_ref, b_ref, dh_ref = refs[len(arrays) : len(arrays) + 6]
+        grads_ref, hidden_ref, away_ref = refs[len(arrays) + 6 :]
         a, b, dh = a_ref[...], b_ref[...], dh_ref[...]
         for k, (number, column, owner) in enumerate(table):
             block = refs[number][:, column : column + width]
@@ -138,15 +143,21 @@
         hidden_ref[...] = (swish * b).astype(jnp.bfloat16)
         grads_ref[:units, :] = (dh * b * s * (1.0 + a * (1.0 - s))).astype(jnp.bfloat16)
         grads_ref[units:, :] = (dh * swish).astype(jnp.bfloat16)
+        for k, owner in enumerate(away):
+            start = lax.rem(me_ref[0] + owner % ring, ring) * width
+            part = pl.ds(pl.multiple_of(start, width), width)
+            both = tn(grads_ref[:units, :], w_gate[:, part]) + tn(grads_ref[units:, :], w_up[:, part])
+            away_ref[:, k * width : (k + 1) * width] = both.astype(jnp.bfloat16)
 
     return pl.pallas_call(
         kernel,
         out_shape=(
             jax.ShapeDtypeStruct((2 * units, rows), jnp.bfloat16),
             jax.ShapeDtypeStruct((units, rows), jnp.bfloat16),
+            jax.ShapeDtypeStruct((rows, len(away) * width), jnp.bfloat16),
         ),
         in_specs=[SMEM] + [VMEM] * (len(arrays) + 6),
-        out_specs=(VMEM, VMEM),
+        out_specs=(VMEM, VMEM, VMEM),
         compiler_params=PARAMS,
         name="activations",
     )(me, *arrays, *weights, *sums)
@@ -233,10 +244,13 @@
 
     early = [d for step in range(near) for d in ([-step, step] if step else [0])]
     early_x, early_g = [(x[d], 0, d) for d in early], [(g[d], 0, d) for d in early]
-    late_x = [(far, 0, half), (far, 2 * width, near), (x[-near], 0, -near)]
-    late_g = [(far, width, half), (far, 3 * width, -near), (g[near], 0, near)]
-    sums = first_products(me_ref, ring, width, early_x, early_g, weights)
-    grads, hidden = activations(me_ref, ring, width, late_x, late_g, weights, sums)
+    last_x, last_g = [(x[-near], 0, -near)], [(g[near], 0, near)]
+    late_x = [(far, 0, half), (far, 2 * width, near)]
+    late_g = [(far, width, half), (far, 3 * width, -near)]
+    sums = first_products(me_ref, ring, width, early_x, early_g, weights, flops=3400 * 10**7)
+    sums = first_products(me_ref, ring, width, last_x, last_g, weights, sums, flops=10**9)
+    away = [half, near, -near]
+    grads, hidden, side = activations(me_ref, ring, width, late_x, late_g, weights, sums, away)
 
     paired = jnp.concatenate(weights[:2], axis=0)
 
@@ -250,10 +264,8 @@
     def added(*values):
         return sum(value.astype(jnp.float32) for value in values)
 
-    away = [half, near, -near]
     right, left = partial(near - 1), partial(1 - near)
-    side = jnp.concatenate([columns(d) for d in away], axis=1)
-    far_back = over_ep(tn(grads, side).astype(jnp.bfloat16))
+    far_back = over_ep(side)
     for d in range(near - 2, -1, -1):
         right, left = moved(right, 1), moved(left, -1)
         if d:
@@ -262,7 +274,7 @@
     total = added(partial(0), right, left).astype(jnp.bfloat16)
 
     grad_gate, grad_up, grad_down = weight_grads(
-        me_ref, ring, width, early_x + late_x, early_g + late_g, grads, hidden
+        me_ref, ring, width, early_x + last_x + late_x, early_g + last_g + late_g, grads, hidden
     )
     total, grad_gate, grad_up, grad_down = lax.optimization_barrier(
         (total, grad_gate, grad_up, grad_down)

time: 206 us -> 205 us (level); the launches traced: 203 us -> 204 us
  Pallas kernels: 25.3 us -> 30.2 us
  starting transfers between devices: 116 us -> 120 us
  waiting for transfers between devices: 46.7 us -> 43.2 us
  matrix products: 8.48 us -> 5.15 us
    all_to_all x4, waiting for transfers between devices: 15 us -> 6.98 us  [over_ep(): lax.all_to_all(value.reshape(shape), 'ep', split_axis=0, concat_axis=0, t...]
    ppermute x20, waiting for transfers between devices: 31.7 us -> 36.2 us  [moved(): lax.ppermute(value, 'tp', [(i, (i + by) % ring) for i in range(ring)])]
    pallas_call x1 -> x2, Pallas kernels: 6.67 us -> 10.9 us  [first_products(): pl.pallas_call(kernel, out_shape=[jax.ShapeDtypeStruct((units, rows), jnp...]
    all_to_all x4, starting transfers between devices: 35 us -> 38.4 us  [over_ep(): lax.all_to_all(value.reshape(shape), 'ep', split_axis=0, concat_axis=0, t...]
    dot_general x8 -> x7, matrix products: 8.48 us -> 5.15 us  [tn(): lax.dot_general(left, right, (((0,), (0,)), ((), ())), preferred_element_...]
  transfers between devices with their start and end apart: 24 -> 24, of which waited for: 13 -> 14; matrix products, arithmetic and copies ran while one was open for 3% -> 3% of each run, Pallas kernels for 8% -> 10%
where the time goes in v5:
time: 205 us; the launch traced here: 204 us
  starting transfers between devices  120 us (59%)
  waiting for transfers between devices  43.2 us (21%)
  Pallas kernels  30.2 us (15%)
  matrix products  5.15 us (3%)
  local copies, waits for them, and re-layouts  3.56 us (2%)
    ppermute x20, starting transfers between devices, moved(): lax.ppermute(value, 'tp', [(i, (i + by) % ring) for i in range(ring)])  81.4 us
    all_to_all x4, starting transfers between devices, over_ep(): lax.all_to_all(value.reshape(shape), 'ep', split_axis=0, concat_axis=0, t...  38.4 us
    ppermute x20, waiting for transfers between devices, moved(): lax.ppermute(value, 'tp', [(i, (i + by) % ring) for i in range(ring)])  36.2 us
    pallas_call x2, Pallas kernels, first_products(): pl.pallas_call(kernel, out_shape=[jax.ShapeDtypeStruct((units, rows), jnp...  10.9 us
    pallas_call x1, Pallas kernels, weight_grads(): pl.pallas_call(kernel, out_shape=[jax.ShapeDtypeStruct((units, ring * wid...  7.04 us
    all_to_all x4, waiting for transfers between devices, over_ep(): lax.all_to_all(value.reshape(shape), 'ep', split_axis=0, concat_axis=0, t...  6.98 us
    pallas_call x1, Pallas kernels, activations(): pl.pallas_call(kernel, out_shape=(jax.ShapeDtypeStruct((2 * units, rows),...  6.45 us
    pallas_call x2, Pallas kernels, dispatch(): pl.pallas_call(kernel, out_shape=(jax.ShapeDtypeStruct((count, sum(widths...  5.75 us
  transfers between devices with their start and end apart: 24, of which 14 were waited for; matrix products, arithmetic and copies ran while one was open for 3% of the time, Pallas kernels for 10%

profile of v5, /device:TPU:1, one launch (start us, length us, event | category | flops | bytes accessed | tf_op | source)
XLA Modules:
  0.0 204.3 jit_solution(4890323435822309642)
XLA Ops:
  0.7 2.5 %dispatch.2 = (bf16[1024,512]{1,0:T(8,128)(2,1)}, bf16[1024,128]{1,0:T(8,128)(2,1)}) custom-call(s32[6,128]{1,0:T(8,128)} %bitcast.52, f32[6,128]{1,0:T(8,128)} %bitcast.54, bf16[128,256]{1,0:T(8,128)(2,1)} %refs_0_.1, bf16[128,256]{1,0:T(8,128)(2,1)} %refs_1_.1), custom_call_target="tpu_custom_call" | custom-call | tf_op jit(solution)/shard_map/dispatch/pallas_call | solution.py:64
  3.2 11.6 %all-to-all-start = ((bf16[64,16,512]{2,1,0:T(8,128)(2,1)}), bf16[64,16,512]{2,1,0:T(8,128)(2,1)S(1)}, u32[]{:S(2)}, u32[]{:S(2)}) async-start(bf16[64,16,512]{2,1,0:T(8,128)(2,1)} %bitcast.51), calls=%async_computation | async-start | bytes 2097152 | tf_op jit(solution)/shard_map/all_to_all | solution.py:212
  14.9 10.6 %collective-permute-start = (bf16[128,512]{1,0:T(8,128)(2,1)S(1)}, bf16[128,512]{1,0:T(8,128)(2,1)S(1)}, u32[]{:S(2)}, u32[]{:S(2)}) collective-permute-start(bf16[128,512]{1,0:T(8,128)(2,1)S(1)} %pad_maximum_fusion), channel_id=1, source_target_pairs={{0,4},{1,5},{2,6},{3,7},{4,0},{5,1},{6,2},{7,3},{8,12},{9,13},{10,... | collective-permute-start | bytes 393224 | tf_op jit(solution)/shard_map/ppermute | solution.py:208
  25.5 1.9 collective-permute-start.1
  27.5 5.2 %collective-permute-start.2 = (bf16[128,256]{1,0:T(8,128)(2,1)S(1)}, bf16[128,256]{1,0:T(8,128)(2,1)S(1)}, u32[]{:S(2)}, u32[]{:S(2)}) collective-permute-start(bf16[128,256]{1,0:T(8,128)(2,1)S(1)} %copy-done.10), channel_id=1, source_target_pairs={{0,3},{1,4},{2,5},{3,6},{4,7},{5,0},{6,1},{7,2},{8,11},{9,12},{10,... | collective-permute-start | bytes 196616 | tf_op jit(solution)/shard_map/ppermute | solution.py:208
  32.6 0.7 fusion.22
  33.3 1.8 collective-permute-done.1.refs_2_
  35.1 5.0 %collective-permute-done.2.refs_3_ = bf16[128,256]{1,0:T(8,128)(2,1)S(1)} collective-permute-done((bf16[128,256]{1,0:T(8,128)(2,1)S(1)}, bf16[128,256]{1,0:T(8,128)(2,1)S(1)}, u32[]{:S(2)}, u32[]{:S(2)}) %collective-permute-start.2) | collective-permute-done | bytes 65568 | tf_op jit(solution)/shard_map/ppermute | solution.py:208
  40.7 3.2 %dispatch.3 = (bf16[1024,1024]{1,0:T(8,128)(2,1)}, bf16[1024,128]{1,0:T(8,128)(2,1)}) custom-call(s32[6,128]{1,0:T(8,128)} %bitcast.53, f32[6,128]{1,0:T(8,128)} %bitcast.55, bf16[128,256]{1,0:T(8,128)(2,1)} %get-tuple-element.60.refs_0_, bf16[128,256]{1,0:T(8,128)(2,1)} %get-tuple-element.59.refs_1_, bf16[128,256]{1,0:T(8,128)(2,1)} %copy-done.11, ...), custom_call_target="tpu_custom_call" | custom-call | tf_op jit(solution)/shard_map/dispatch/pallas_call | solution.py:64
  44.0 2.9 %collective-permute-start.3 = (bf16[1024,256]{1,0:T(8,128)(2,1)S(1)}, bf16[1024,256]{1,0:T(8,128)(2,1)}, u32[]{:S(2)}, u32[]{:S(2)}) collective-permute-start(bf16[1024,256]{1,0:T(8,128)(2,1)S(1)} %get-tuple-element.36.refs_0_), channel_id=1, source_target_pairs={{0,1},{1,2},{2,3},{3,4},{4,5},{5,6},{6,7},{7,0},{8,9},{9,10},{10,1... | collective-permute-start | bytes 1572872 | tf_op jit(solution)/shard_map/ppermute | solution.py:208
  46.9 8.6 %collective-permute-start.6 = (bf16[1024,256]{1,0:T(8,128)(2,1)S(1)}, bf16[1024,256]{1,0:T(8,128)(2,1)}, u32[]{:S(2)}, u32[]{:S(2)}) collective-permute-start(bf16[1024,256]{1,0:T(8,128)(2,1)S(1)} %get-tuple-element.37.refs_5_.refs_7_), channel_id=1, source_target_pairs={{0,7},{1,0},{2,1},{3,2},{4,3},{5,4},{6,5},{7,6},{8,15},{9,8},{10,9... | collective-permute-start | bytes 1572872 | tf_op jit(solution)/shard_map/ppermute | solution.py:208
  55.5 3.4 %collective-permute-start.9 = (bf16[1024,256]{1,0:T(8,128)(2,1)S(1)}, bf16[1024,256]{1,0:T(8,128)(2,1)}, u32[]{:S(2)}, u32[]{:S(2)}) collective-permute-start(bf16[1024,256]{1,0:T(8,128)(2,1)S(1)} %get-tuple-element.36.refs_0_), channel_id=1, source_target_pairs={{0,7},{1,0},{2,1},{3,2},{4,3},{5,4},{6,5},{7,6},{8,15},{9,8},{10,9... | collective-permute-start | bytes 1572872 | tf_op jit(solution)/shard_map/ppermute | solution.py:208
  58.9 1.9 collective-permute-start.11
  60.9 7.3 %all-to-all-start.1 = ((bf16[64,16,1024]{2,1,0:T(8,128)(2,1)}), bf16[64,16,1024]{2,1,0:T(8,128)(2,1)S(1)}, u32[]{:S(2)}, u32[]{:S(2)}) async-start(bf16[64,16,1024]{2,1,0:T(8,128)(2,1)} %bitcast.48), calls=%async_computation.1 | async-start | bytes 4194304 | tf_op jit(solution)/shard_map/all_to_all | solution.py:212
  68.2 1.9 collective-permute-start.4
  70.1 4.9 %collective-permute-start.7 = (bf16[1024,256]{1,0:T(8,128)(2,1)}, bf16[1024,256]{1,0:T(8,128)(2,1)}, u32[]{:S(2)}, u32[]{:S(2)}) collective-permute-start(bf16[1024,256]{1,0:T(8,128)(2,1)} %collective-permute-done.6.refs_7_.refs_9_), channel_id=1, source_target_pairs={{0,7},{1,0},{2,1},{3,2},{4,3},{5,4},{6,5},{7,6},{8,15},{9,8},{10,9... | collective-permute-start | bytes 1572872 | tf_op jit(solution)/shard_map/ppermute | solution.py:208
  75.0 1.6 collective-permute-done.9.refs_2_
  76.6 5.4 %collective-permute-start.10 = (bf16[1024,256]{1,0:T(8,128)(2,1)}, bf16[1024,256]{1,0:T(8,128)(2,1)}, u32[]{:S(2)}, u32[]{:S(2)}) collective-permute-start(bf16[1024,256]{1,0:T(8,128)(2,1)} %collective-permute-done.9.refs_2_), channel_id=1, source_target_pairs={{0,7},{1,0},{2,1},{3,2},{4,3},{5,4},{6,5},{7,6},{8,15},{9,8},{10,9... | collective-permute-start | bytes 1572872 | tf_op jit(solution)/shard_map/ppermute | solution.py:208
  82.0 1.9 collective-permute-start.12
  84.0 3.3 %collective-permute-done.4.refs_3_ = bf16[1024,256]{1,0:T(8,128)(2,1)} collective-permute-done((bf16[1024,256]{1,0:T(8,128)(2,1)}, bf16[1024,256]{1,0:T(8,128)(2,1)}, u32[]{:S(2)}, u32[]{:S(2)}) %collective-permute-start.4) | collective-permute-done | bytes 524320 | tf_op jit(solution)/shard_map/ppermute | solution.py:208
  87.3 1.9 collective-permute-start.5
  89.2 4.6 %collective-permute-start.8 = (bf16[1024,256]{1,0:T(8,128)(2,1)}, bf16[1024,256]{1,0:T(8,128)(2,1)S(1)}, u32[]{:S(2)}, u32[]{:S(2)}) collective-permute-start(bf16[1024,256]{1,0:T(8,128)(2,1)} %collective-permute-done.7.refs_9_.refs_11_), channel_id=1, source_target_pairs={{0,7},{1,0},{2,1},{3,2},{4,3},{5,4},{6,5},{7,6},{8,15},{9,8},{10,9... | collective-permute-start | bytes 1572872 | tf_op jit(solution)/shard_map/ppermute | solution.py:208
  93.8 5.4 %collective-permute-done.10.refs_4_ = bf16[1024,256]{1,0:T(8,128)(2,1)} collective-permute-done((bf16[1024,256]{1,0:T(8,128)(2,1)}, bf16[1024,256]{1,0:T(8,128)(2,1)}, u32[]{:S(2)}, u32[]{:S(2)}) %collective-permute-start.10) | collective-permute-done | bytes 524320 | tf_op jit(solution)/shard_map/ppermute | solution.py:208
  99.2 6.7 %first_products.2 = (f32[176,1024]{1,0:T(8,128)}, f32[176,1024]{1,0:T(8,128)}, f32[176,1024]{1,0:T(8,128)}) custom-call(s32[1]{0:T(128)} %bitcast.2.me_ref, bf16[1024,256]{1,0:T(8,128)(2,1)} %copy-done.6, bf16[1024,256]{1,0:T(8,128)(2,1)} %collective-permute-done.3.refs_1_, bf16[1024,256]{1,0:T(8,128)(2,1)} %collective-permute-done.9.refs_2_, ...), custom_call_target="tpu_custom_call" | custom-call | flops 33999998976 | bytes 1000 | tf_op jit(solution)/shard_map/first_products/pallas_call | solution.py:112
  105.9 0.7 collective-permute-done.5.refs_0_.refs_5_
  106.5 3.9 %collective-permute-done.8.refs_1_.refs_12_ = bf16[1024,256]{1,0:T(8,128)(2,1)S(1)} collective-permute-done((bf16[1024,256]{1,0:T(8,128)(2,1)}, bf16[1024,256]{1,0:T(8,128)(2,1)S(1)}, u32[]{:S(2)}, u32[]{:S(2)}) %collective-permute-start.8) | collective-permute-done | bytes 524320 | tf_op jit(solution)/shard_map/ppermute | solution.py:208
  110.4 0.8 copy-done.8
  111.2 4.3 %first_products.3 = (f32[176,1024]{1,0:T(8,128)}, f32[176,1024]{1,0:T(8,128)}, f32[176,1024]{1,0:T(8,128)}) custom-call(s32[1]{0:T(128)} %bitcast.2.me_ref, bf16[1024,256]{1,0:T(8,128)(2,1)} %copy-done.7, bf16[1024,256]{1,0:T(8,128)(2,1)} %copy-done.8, bf16[176,2048]{1,0:T(8,128)(2,1)} %bitcast.27, bf16[176,2048]{1,0:T(8,128)(2,1)} %bitcast.35, ...), custom_call_target="tpu_custom_call" | custom-call | flops 1000000000 | bytes 1000 | tf_op jit(solution)/shard_map/first_products/pallas_call | solution.py:112
  115.5 2.4 %all-to-all-done.1 = bf16[64,16,1024]{2,1,0:T(8,128)(2,1)S(1)} async-done(((bf16[64,16,1024]{2,1,0:T(8,128)(2,1)}), bf16[64,16,1024]{2,1,0:T(8,128)(2,1)S(1)}, u32[]{:S(2)}, u32[]{:S(2)}) %all-to-all-start.1) | async-done | bytes 2097184 | tf_op jit(solution)/shard_map/all_to_all | solution.py:212
  117.9 1.4 copy-done.3
  119.2 6.4 %activations.1 = (bf16[352,1024]{1,0:T(8,128)(2,1)}, bf16[176,1024]{1,0:T(8,128)(2,1)}, bf16[1024,768]{1,0:T(8,128)(2,1)}) custom-call(s32[1]{0:T(128)} %bitcast.2.me_ref, bf16[1024,1024]{1,0:T(8,128)(2,1)} %bitcast.42, bf16[176,2048]{1,0:T(8,128)(2,1)} %bitcast.28, bf16[176,2048]{1,0:T(8,128)(2,1)} %bitcast.36, bf16[176,2048]{1,0:T(8,128)(2,1)} %bitcast.47, ...), custom_call_target="tpu_custom_call" | custom-call | tf_op jit(solution)/shard_map/activations/pallas_call | solution.py:152
  125.7 7.4 %all-to-all-start.3 = ((bf16[64,16,768]{2,1,0:T(8,128)(2,1)}), bf16[64,16,768]{2,1,0:T(8,128)(2,1)}, u32[]{:S(2)}, u32[]{:S(2)}) async-start(bf16[64,16,768]{2,1,0:T(8,128)(2,1)} %bitcast.50), calls=%async_computation.3 | async-start | bytes 3145728 | tf_op jit(solution)/shard_map/all_to_all | solution.py:212
  133.6 5.2 %collective-permute-start.15 = (bf16[1024,256]{1,0:T(8,128)(2,1)S(1)}, bf16[1024,256]{1,0:T(8,128)(2,1)S(1)}, u32[]{:S(2)}, u32[]{:S(2)}) collective-permute-start(bf16[1024,256]{1,0:T(8,128)(2,1)S(1)} %convolution_convert_fusion.1), channel_id=1, source_target_pairs={{0,7},{1,0},{2,1},{3,2},{4,3},{5,4},{6,5},{7,6},{8,15},{9,8},{10,9... | collective-permute-start | bytes 1572872 | tf_op jit(solution)/shard_map/ppermute | solution.py:208
  139.3 1.9 collective-permute-start.13
  142.2 7.3 %collective-permute-done.15 = bf16[1024,256]{1,0:T(8,128)(2,1)S(1)} collective-permute-done((bf16[1024,256]{1,0:T(8,128)(2,1)S(1)}, bf16[1024,256]{1,0:T(8,128)(2,1)S(1)}, u32[]{:S(2)}, u32[]{:S(2)}) %collective-permute-start.15) | collective-permute-done | bytes 524320 | tf_op jit(solution)/shard_map/ppermute | solution.py:208
  149.7 5.6 %collective-permute-start.16 = (bf16[1024,256]{1,0:T(8,128)(2,1)S(1)}, bf16[1024,256]{1,0:T(8,128)(2,1)S(1)}, u32[]{:S(2)}, u32[]{:S(2)}) collective-permute-start(bf16[1024,256]{1,0:T(8,128)(2,1)S(1)} %add_convert_fusion.1), channel_id=1, source_target_pairs={{0,7},{1,0},{2,1},{3,2},{4,3},{5,4},{6,5},{7,6},{8,15},{9,8},{10,9... | collective-permute-start | bytes 1572872 | tf_op jit(solution)/shard_map/ppermute | solution.py:208
  155.5 1.9 collective-permute-start.14
  157.9 7.0 %weight_grads.1 = (bf16[176,2048]{1,0:T(8,128)(2,1)}, bf16[176,2048]{1,0:T(8,128)(2,1)}, bf16[176,2048]{1,0:T(8,128)(2,1)}) custom-call(s32[1]{0:T(128)} %bitcast.2.me_ref, bf16[1024,256]{1,0:T(8,128)(2,1)} %copy-done.6, bf16[1024,256]{1,0:T(8,128)(2,1)} %collective-permute-done.3.refs_1_, bf16[1024,256]{1,0:T(8,128)(2,1)} %collective-permute-done.9.refs_2_, ...), custom_call_target="tpu_custom_call" | custom-call | flops 5000000000 | bytes 1000 | tf_op jit(solution)/shard_map/weight_grads/pallas_call | solution.py:183
  165.1 5.5 %collective-permute-done.14 = bf16[1024,256]{1,0:T(8,128)(2,1)S(1)} collective-permute-done((bf16[1024,256]{1,0:T(8,128)(2,1)S(1)}, bf16[1024,256]{1,0:T(8,128)(2,1)S(1)}, u32[]{:S(2)}, u32[]{:S(2)}) %collective-permute-start.14) | collective-permute-done | bytes 524320 | tf_op jit(solution)/shard_map/ppermute | solution.py:208
  170.6 1.0 add_convert_fusion
  172.0 12.1 %all-to-all-start.2 = ((bf16[64,16,256]{2,1,0:T(8,128)(2,1)}), bf16[64,16,256]{2,1,0:T(8,128)(2,1)S(1)}, u32[]{:S(2)}, u32[]{:S(2)}) async-start(bf16[64,16,256]{2,1,0:T(8,128)(2,1)} %bitcast.10), calls=%async_computation.2 | async-start | bytes 1048576 | tf_op jit(solution)/shard_map/all_to_all | solution.py:212
  184.1 1.8 convolution_convert_fusion.5
  185.9 2.1 %collective-permute-start.19 = (bf16[128,256]{1,0:T(8,128)(2,1)S(1)}, bf16[128,256]{1,0:T(8,128)(2,1)S(1)}, u32[]{:S(2)}, u32[]{:S(2)}) collective-permute-start(bf16[128,256]{1,0:T(8,128)(2,1)S(1)} %get-tuple-element.57), channel_id=1, source_target_pairs={{0,5},{1,6},{2,7},{3,0},{4,1},{5,2},{6,3},{7,4},{8,13},{9,14},{10,... | collective-permute-start | bytes 196616 | tf_op jit(solution)/shard_map/ppermute | solution.py:208
  188.1 4.9 %collective-permute-start.18 = (bf16[128,256]{1,0:T(8,128)(2,1)S(1)}, bf16[128,256]{1,0:T(8,128)(2,1)S(1)}, u32[]{:S(2)}, u32[]{:S(2)}) collective-permute-start(bf16[128,256]{1,0:T(8,128)(2,1)S(1)} %get-tuple-element.58), channel_id=1, source_target_pairs={{0,3},{1,4},{2,5},{3,6},{4,7},{5,0},{6,1},{7,2},{8,11},{9,12},{10,... | collective-permute-start | bytes 196616 | tf_op jit(solution)/shard_map/ppermute | solution.py:208
  193.0 4.5 %collective-permute-start.17 = (bf16[128,256]{1,0:T(8,128)(2,1)S(1)}, bf16[128,256]{1,0:T(8,128)(2,1)S(1)}, u32[]{:S(2)}, u32[]{:S(2)}) collective-permute-start(bf16[128,256]{1,0:T(8,128)(2,1)S(1)} %get-tuple-element.56), channel_id=1, source_target_pairs={{0,4},{1,5},{2,6},{3,7},{4,0},{5,1},{6,2},{7,3},{8,12},{9,13},{10,... | collective-permute-start | bytes 196616 | tf_op jit(solution)/shard_map/ppermute | solution.py:208
  197.6 4.2 %all-to-all-done.2 = bf16[64,16,256]{2,1,0:T(8,128)(2,1)S(1)} async-done(((bf16[64,16,256]{2,1,0:T(8,128)(2,1)}), bf16[64,16,256]{2,1,0:T(8,128)(2,1)S(1)}, u32[]{:S(2)}, u32[]{:S(2)}) %all-to-all-start.2) | async-done | bytes 524320 | tf_op jit(solution)/shard_map/all_to_all | solution.py:212
  201.8 1.6 collective-permute-done.17
  203.4 0.9 add_convert_fusion.3
  (46 shorter events, 4.0 us)
Async XLA Ops:
  0.6 14.2 %copy-start.9 = (bf16[128,256]{1,0:T(8,128)(2,1)S(1)}, bf16[128,256]{1,0:T(8,128)(2,1)}, u32[]{:S(2)}) copy-start(bf16[128,256]{1,0:T(8,128)(2,1)} %refs_0_.1) | copy-start | bytes 196612
  0.6 14.2 %copy-start.10 = (bf16[128,256]{1,0:T(8,128)(2,1)S(1)}, bf16[128,256]{1,0:T(8,128)(2,1)}, u32[]{:S(2)}) copy-start(bf16[128,256]{1,0:T(8,128)(2,1)} %refs_1_.1) | copy-start | bytes 196612
  3.2 40.7 %all-to-all-start = ((bf16[64,16,512]{2,1,0:T(8,128)(2,1)}), bf16[64,16,512]{2,1,0:T(8,128)(2,1)S(1)}, u32[]{:S(2)}, u32[]{:S(2)}) async-start(bf16[64,16,512]{2,1,0:T(8,128)(2,1)} %bitcast.51), calls=%async_computation | async-start | bytes 2097152 | tf_op jit(solution)/shard_map/all_to_all | solution.py:212
  14.9 17.7 %collective-permute-start = (bf16[128,512]{1,0:T(8,128)(2,1)S(1)}, bf16[128,512]{1,0:T(8,128)(2,1)S(1)}, u32[]{:S(2)}, u32[]{:S(2)}) collective-permute-start(bf16[128,512]{1,0:T(8,128)(2,1)S(1)} %pad_maximum_fusion), channel_id=1, source_target_pairs={{0,4},{1,5},{2,6},{3,7},{4,0},{5,1},{6,2},{7,3},{8,12},{9,13},{10,... | collective-permute-start | bytes 393224 | tf_op jit(solution)/shard_map/ppermute | solution.py:208
  25.5 9.5 %collective-permute-start.1 = (bf16[128,256]{1,0:T(8,128)(2,1)S(1)}, bf16[128,256]{1,0:T(8,128)(2,1)S(1)}, u32[]{:S(2)}, u32[]{:S(2)}) collective-permute-start(bf16[128,256]{1,0:T(8,128)(2,1)S(1)} %copy-done.9), channel_id=1, source_target_pairs={{0,5},{1,6},{2,7},{3,0},{4,1},{5,2},{6,3},{7,4},{8,13},{9,14},{10,... | collective-permute-start | bytes 196616 | tf_op jit(solution)/shard_map/ppermute | solution.py:208
  27.5 12.6 %collective-permute-start.2 = (bf16[128,256]{1,0:T(8,128)(2,1)S(1)}, bf16[128,256]{1,0:T(8,128)(2,1)S(1)}, u32[]{:S(2)}, u32[]{:S(2)}) collective-permute-start(bf16[128,256]{1,0:T(8,128)(2,1)S(1)} %copy-done.10), channel_id=1, source_target_pairs={{0,3},{1,4},{2,5},{3,6},{4,7},{5,0},{6,1},{7,2},{8,11},{9,12},{10,... | collective-permute-start | bytes 196616 | tf_op jit(solution)/shard_map/ppermute | solution.py:208
  35.1 5.0 %copy-start.11 = (bf16[128,256]{1,0:T(8,128)(2,1)}, bf16[128,256]{1,0:T(8,128)(2,1)S(1)}, u32[]{:S(2)}) copy-start(bf16[128,256]{1,0:T(8,128)(2,1)S(1)} %collective-permute-done.1.refs_2_) | copy-start | bytes 196612
  40.1 0.6 copy-start.12
  44.0 16.9 %copy-start.5 = (bf16[1024,256]{1,0:T(8,128)(2,1)}, bf16[1024,256]{1,0:T(8,128)(2,1)S(1)}, u32[]{:S(2)}) copy-start(bf16[1024,256]{1,0:T(8,128)(2,1)S(1)} %get-tuple-element.37.refs_5_.refs_7_) | copy-start | bytes 1572868
  44.0 16.9 %copy-start.6 = (bf16[1024,256]{1,0:T(8,128)(2,1)}, bf16[1024,256]{1,0:T(8,128)(2,1)S(1)}, u32[]{:S(2)}) copy-start(bf16[1024,256]{1,0:T(8,128)(2,1)S(1)} %get-tuple-element.36.refs_0_) | copy-start | bytes 1572868
  44.0 24.2 %collective-permute-start.3 = (bf16[1024,256]{1,0:T(8,128)(2,1)S(1)}, bf16[1024,256]{1,0:T(8,128)(2,1)}, u32[]{:S(2)}, u32[]{:S(2)}) collective-permute-start(bf16[1024,256]{1,0:T(8,128)(2,1)S(1)} %get-tuple-element.36.refs_0_), channel_id=1, source_target_pairs={{0,1},{1,2},{2,3},{3,4},{4,5},{5,6},{6,7},{7,0},{8,9},{9,10},{10,1... | collective-permute-start | bytes 1572872 | tf_op jit(solution)/shard_map/ppermute | solution.py:208
  46.9 23.2 %collective-permute-start.6 = (bf16[1024,256]{1,0:T(8,128)(2,1)S(1)}, bf16[1024,256]{1,0:T(8,128)(2,1)}, u32[]{:S(2)}, u32[]{:S(2)}) collective-permute-start(bf16[1024,256]{1,0:T(8,128)(2,1)S(1)} %get-tuple-element.37.refs_5_.refs_7_), channel_id=1, source_target_pairs={{0,7},{1,0},{2,1},{3,2},{4,3},{5,4},{6,5},{7,6},{8,15},{9,8},{10,9... | collective-permute-start | bytes 1572872 | tf_op jit(solution)/shard_map/ppermute | solution.py:208
  55.5 21.1 %collective-permute-start.9 = (bf16[1024,256]{1,0:T(8,128)(2,1)S(1)}, bf16[1024,256]{1,0:T(8,128)(2,1)}, u32[]{:S(2)}, u32[]{:S(2)}) collective-permute-start(bf16[1024,256]{1,0:T(8,128)(2,1)S(1)} %get-tuple-element.36.refs_0_), channel_id=1, source_target_pairs={{0,7},{1,0},{2,1},{3,2},{4,3},{5,4},{6,5},{7,6},{8,15},{9,8},{10,9... | collective-permute-start | bytes 1572872 | tf_op jit(solution)/shard_map/ppermute | solution.py:208
  58.9 23.1 %collective-permute-start.11 = (bf16[1024,256]{1,0:T(8,128)(2,1)S(1)}, bf16[1024,256]{1,0:T(8,128)(2,1)}, u32[]{:S(2)}, u32[]{:S(2)}) collective-permute-start(bf16[1024,256]{1,0:T(8,128)(2,1)S(1)} %get-tuple-element.37.refs_5_.refs_7_), channel_id=1, source_target_pairs={{0,1},{1,2},{2,3},{3,4},{4,5},{5,6},{6,7},{7,0},{8,9},{9,10},{10,1... | collective-permute-start | bytes 1572872 | tf_op jit(solution)/shard_map/ppermute | solution.py:208
  60.9 57.0 %all-to-all-start.1 = ((bf16[64,16,1024]{2,1,0:T(8,128)(2,1)}), bf16[64,16,1024]{2,1,0:T(8,128)(2,1)S(1)}, u32[]{:S(2)}, u32[]{:S(2)}) async-start(bf16[64,16,1024]{2,1,0:T(8,128)(2,1)} %bitcast.48), calls=%async_computation.1 | async-start | bytes 4194304 | tf_op jit(solution)/shard_map/all_to_all | solution.py:212
  68.2 19.1 %collective-permute-start.4 = (bf16[1024,256]{1,0:T(8,128)(2,1)}, bf16[1024,256]{1,0:T(8,128)(2,1)}, u32[]{:S(2)}, u32[]{:S(2)}) collective-permute-start(bf16[1024,256]{1,0:T(8,128)(2,1)} %collective-permute-done.3.refs_1_), channel_id=1, source_target_pairs={{0,1},{1,2},{2,3},{3,4},{4,5},{5,6},{6,7},{7,0},{8,9},{9,10},{10,1... | collective-permute-start | bytes 1572872 | tf_op jit(solution)/shard_map/ppermute | solution.py:208
  70.1 19.1 %collective-permute-start.7 = (bf16[1024,256]{1,0:T(8,128)(2,1)}, bf16[1024,256]{1,0:T(8,128)(2,1)}, u32[]{:S(2)}, u32[]{:S(2)}) collective-permute-start(bf16[1024,256]{1,0:T(8,128)(2,1)} %collective-permute-done.6.refs_7_.refs_9_), channel_id=1, source_target_pairs={{0,7},{1,0},{2,1},{3,2},{4,3},{5,4},{6,5},{7,6},{8,15},{9,8},{10,9... | collective-permute-start | bytes 1572872 | tf_op jit(solution)/shard_map/ppermute | solution.py:208
  76.6 22.6 %collective-permute-start.10 = (bf16[1024,256]{1,0:T(8,128)(2,1)}, bf16[1024,256]{1,0:T(8,128)(2,1)}, u32[]{:S(2)}, u32[]{:S(2)}) collective-permute-start(bf16[1024,256]{1,0:T(8,128)(2,1)} %collective-permute-done.9.refs_2_), channel_id=1, source_target_pairs={{0,7},{1,0},{2,1},{3,2},{4,3},{5,4},{6,5},{7,6},{8,15},{9,8},{10,9... | collective-permute-start | bytes 1572872 | tf_op jit(solution)/shard_map/ppermute | solution.py:208
  82.0 17.1 %collective-permute-start.12 = (bf16[1024,256]{1,0:T(8,128)(2,1)}, bf16[1024,256]{1,0:T(8,128)(2,1)}, u32[]{:S(2)}, u32[]{:S(2)}) collective-permute-start(bf16[1024,256]{1,0:T(8,128)(2,1)} %collective-permute-done.11.refs_6_.refs_8_), channel_id=1, source_target_pairs={{0,1},{1,2},{2,3},{3,4},{4,5},{5,6},{6,7},{7,0},{8,9},{9,10},{10,1... | collective-permute-start | bytes 1572872 | tf_op jit(solution)/shard_map/ppermute | solution.py:208
  87.3 19.2 %collective-permute-start.5 = (bf16[1024,256]{1,0:T(8,128)(2,1)}, bf16[1024,256]{1,0:T(8,128)(2,1)S(1)}, u32[]{:S(2)}, u32[]{:S(2)}) collective-permute-start(bf16[1024,256]{1,0:T(8,128)(2,1)} %collective-permute-done.4.refs_3_), channel_id=1, source_target_pairs={{0,1},{1,2},{2,3},{3,4},{4,5},{5,6},{6,7},{7,0},{8,9},{9,10},{10,1... | collective-permute-start | bytes 1572872 | tf_op jit(solution)/shard_map/ppermute | solution.py:208
  89.2 21.2 %collective-permute-start.8 = (bf16[1024,256]{1,0:T(8,128)(2,1)}, bf16[1024,256]{1,0:T(8,128)(2,1)S(1)}, u32[]{:S(2)}, u32[]{:S(2)}) collective-permute-start(bf16[1024,256]{1,0:T(8,128)(2,1)} %collective-permute-done.7.refs_9_.refs_11_), channel_id=1, source_target_pairs={{0,7},{1,0},{2,1},{3,2},{4,3},{5,4},{6,5},{7,6},{8,15},{9,8},{10,9... | collective-permute-start | bytes 1572872 | tf_op jit(solution)/shard_map/ppermute | solution.py:208
  106.5 3.9 %copy-start.7 = (bf16[1024,256]{1,0:T(8,128)(2,1)}, bf16[1024,256]{1,0:T(8,128)(2,1)S(1)}, u32[]{:S(2)}) copy-start(bf16[1024,256]{1,0:T(8,128)(2,1)S(1)} %collective-permute-done.5.refs_0_.refs_5_) | copy-start | bytes 1572868
  110.4 0.8 copy-start.8
  117.9 1.4 copy-start.3
  125.7 7.4 %copy-start = (bf16[1,176,2048]{2,1,0:T(8,128)(2,1)S(1)}, bf16[1,176,2048]{2,1,0:T(8,128)(2,1)}, u32[]{:S(2)}) copy-start(bf16[1,176,2048]{2,1,0:T(8,128)(2,1)} %param.11) | copy-start | bytes 2162692
  125.7 7.4 %copy-start.1 = (bf16[1,176,2048]{2,1,0:T(8,128)(2,1)S(1)}, bf16[1,176,2048]{2,1,0:T(8,128)(2,1)}, u32[]{:S(2)}) copy-start(bf16[1,176,2048]{2,1,0:T(8,128)(2,1)} %param.12) | copy-start | bytes 2162692
  125.7 7.4 %copy-start.2 = (bf16[352,1024]{1,0:T(8,128)(2,1)S(1)}, bf16[352,1024]{1,0:T(8,128)(2,1)}, u32[]{:S(2)}) copy-start(bf16[352,1024]{1,0:T(8,128)(2,1)} %get-tuple-element.44.refs_13_) | copy-start | bytes 2162692
  125.7 46.3 %all-to-all-start.3 = ((bf16[64,16,768]{2,1,0:T(8,128)(2,1)}), bf16[64,16,768]{2,1,0:T(8,128)(2,1)}, u32[]{:S(2)}, u32[]{:S(2)}) async-start(bf16[64,16,768]{2,1,0:T(8,128)(2,1)} %bitcast.50), calls=%async_computation.3 | async-start | bytes 3145728 | tf_op jit(solution)/shard_map/all_to_all | solution.py:212
  133.6 16.0 %collective-permute-start.15 = (bf16[1024,256]{1,0:T(8,128)(2,1)S(1)}, bf16[1024,256]{1,0:T(8,128)(2,1)S(1)}, u32[]{:S(2)}, u32[]{:S(2)}) collective-permute-start(bf16[1024,256]{1,0:T(8,128)(2,1)S(1)} %convolution_convert_fusion.1), channel_id=1, source_target_pairs={{0,7},{1,0},{2,1},{3,2},{4,3},{5,4},{6,5},{7,6},{8,15},{9,8},{10,9... | collective-permute-start | bytes 1572872 | tf_op jit(solution)/shard_map/ppermute | solution.py:208
  139.3 16.0 %collective-permute-start.13 = (bf16[1024,256]{1,0:T(8,128)(2,1)S(1)}, bf16[1024,256]{1,0:T(8,128)(2,1)S(1)}, u32[]{:S(2)}, u32[]{:S(2)}) collective-permute-start(bf16[1024,256]{1,0:T(8,128)(2,1)S(1)} %convolution_convert_fusion.3), channel_id=1, source_target_pairs={{0,1},{1,2},{2,3},{3,4},{4,5},{5,6},{6,7},{7,0},{8,9},{9,10},{10,1... | collective-permute-start | bytes 1572872 | tf_op jit(solution)/shard_map/ppermute | solution.py:208
  149.7 15.4 %collective-permute-start.16 = (bf16[1024,256]{1,0:T(8,128)(2,1)S(1)}, bf16[1024,256]{1,0:T(8,128)(2,1)S(1)}, u32[]{:S(2)}, u32[]{:S(2)}) collective-permute-start(bf16[1024,256]{1,0:T(8,128)(2,1)S(1)} %add_convert_fusion.1), channel_id=1, source_target_pairs={{0,7},{1,0},{2,1},{3,2},{4,3},{5,4},{6,5},{7,6},{8,15},{9,8},{10,9... | collective-permute-start | bytes 1572872 | tf_op jit(solution)/shard_map/ppermute | solution.py:208
  155.5 15.1 %collective-permute-start.14 = (bf16[1024,256]{1,0:T(8,128)(2,1)S(1)}, bf16[1024,256]{1,0:T(8,128)(2,1)S(1)}, u32[]{:S(2)}, u32[]{:S(2)}) collective-permute-start(bf16[1024,256]{1,0:T(8,128)(2,1)S(1)} %add_convert_fusion.2), channel_id=1, source_target_pairs={{0,1},{1,2},{2,3},{3,4},{4,5},{5,6},{6,7},{7,0},{8,9},{9,10},{10,1... | collective-permute-start | bytes 1572872 | tf_op jit(solution)/shard_map/ppermute | solution.py:208
  164.9 19.1 %copy-start.4 = (bf16[1024,128]{1,0:T(8,128)(2,1)S(1)}, bf16[1024,128]{1,0:T(8,128)(2,1)}, u32[]{:S(2)}) copy-start(bf16[1024,128]{1,0:T(8,128)(2,1)} %get-tuple-element.29) | copy-start | bytes 786436
  172.0 29.8 %all-to-all-start.2 = ((bf16[64,16,256]{2,1,0:T(8,128)(2,1)}), bf16[64,16,256]{2,1,0:T(8,128)(2,1)S(1)}, u32[]{:S(2)}, u32[]{:S(2)}) async-start(bf16[64,16,256]{2,1,0:T(8,128)(2,1)} %bitcast.10), calls=%async_computation.2 | async-start | bytes 1048576 | tf_op jit(solution)/shard_map/all_to_all | solution.py:212
  185.9 15.9 %collective-permute-start.19 = (bf16[128,256]{1,0:T(8,128)(2,1)S(1)}, bf16[128,256]{1,0:T(8,128)(2,1)S(1)}, u32[]{:S(2)}, u32[]{:S(2)}) collective-permute-start(bf16[128,256]{1,0:T(8,128)(2,1)S(1)} %get-tuple-element.57), channel_id=1, source_target_pairs={{0,5},{1,6},{2,7},{3,0},{4,1},{5,2},{6,3},{7,4},{8,13},{9,14},{10,... | collective-permute-start | bytes 196616 | tf_op jit(solution)/shard_map/ppermute | solution.py:208
  188.1 13.7 %collective-permute-start.18 = (bf16[128,256]{1,0:T(8,128)(2,1)S(1)}, bf16[128,256]{1,0:T(8,128)(2,1)S(1)}, u32[]{:S(2)}, u32[]{:S(2)}) collective-permute-start(bf16[128,256]{1,0:T(8,128)(2,1)S(1)} %get-tuple-element.58), channel_id=1, source_target_pairs={{0,3},{1,4},{2,5},{3,6},{4,7},{5,0},{6,1},{7,2},{8,11},{9,12},{10,... | collective-permute-start | bytes 196616 | tf_op jit(solution)/shard_map/ppermute | solution.py:208
  193.0 10.4 %collective-permute-start.17 = (bf16[128,256]{1,0:T(8,128)(2,1)S(1)}, bf16[128,256]{1,0:T(8,128)(2,1)S(1)}, u32[]{:S(2)}, u32[]{:S(2)}) collective-permute-start(bf16[128,256]{1,0:T(8,128)(2,1)S(1)} %get-tuple-element.56), channel_id=1, source_target_pairs={{0,4},{1,5},{2,6},{3,7},{4,0},{5,1},{6,2},{7,3},{8,12},{9,13},{10,... | collective-permute-start | bytes 196616 | tf_op jit(solution)/shard_map/ppermute | solution.py:208

commit v6 on v4

--- a/solution.py
+++ b/solution.py
@@ -8,7 +8,7 @@
 
 VMEM = pl.BlockSpec(memory_space=pltpu.VMEM)
 SMEM = pl.BlockSpec(memory_space=pltpu.SMEM)
-PARAMS = pltpu.CompilerParams(vmem_limit_bytes=56 * 1024 * 1024)
+PARAMS = pltpu.CompilerParams(vmem_limit_bytes=62 * 1024 * 1024)
 
 
 def nt(left, right):
@@ -111,18 +111,19 @@
         in_specs=[SMEM] + [VMEM] * (len(arrays) + 3),
         out_specs=[VMEM] * 3,
         compiler_params=PARAMS,
-        cost_estimate=pl.CostEstimate(flops=3400 * 10**7, bytes_accessed=1000, transcendentals=0),
+        cost_estimate=pl.CostEstimate(flops=32857 * 10**6, bytes_accessed=1000, transcendentals=0),
         name="first_products",
     )(me, *arrays, *weights)
 
 
-def activations(me, ring, width, features, cotangents, weights, sums):
+def activations(me, ring, width, features, cotangents, weights, sums, away):
     arrays, table = gathered(features + cotangents)
     rows = arrays[0].shape[0]
     units = weights[0].shape[0]
 
     def kernel(me_ref, *refs):
-        w_gate, w_up, w_down, a_ref, b_ref, dh_ref, grads_ref, hidden_ref = refs[len(arrays) :]
+        w_gate, w_up, w_down, a_ref, b_ref, dh_ref = refs[len(arrays) : len(arrays) + 6]
+        grads_ref, hidden_ref, away_ref = refs[len(arrays) + 6 :]
         a, b, dh = a_ref[...], b_ref[...], dh_ref[...]
         for k, (number, column, owner) in enumerate(table):
             block = refs[number][:, column : column + width]
@@ -138,15 +139,21 @@
         hidden_ref[...] = (swish * b).astype(jnp.bfloat16)
         grads_ref[:units, :] = (dh * b * s * (1.0 + a * (1.0 - s))).astype(jnp.bfloat16)
         grads_ref[units:, :] = (dh * swish).astype(jnp.bfloat16)
+        for k, owner in enumerate(away):
+            start = lax.rem(me_ref[0] + owner % ring, ring) * width
+            part = pl.ds(pl.multiple_of(start, width), width)
+            both = tn(grads_ref[:units, :], w_gate[:, part]) + tn(grads_ref[units:, :], w_up[:, part])
+            away_ref[:, k * width : (k + 1) * width] = both.astype(jnp.bfloat16)
 
     return pl.pallas_call(
         kernel,
         out_shape=(
             jax.ShapeDtypeStruct((2 * units, rows), jnp.bfloat16),
             jax.ShapeDtypeStruct((units, rows), jnp.bfloat16),
+            jax.ShapeDtypeStruct((rows, len(away) * width), jnp.bfloat16),
         ),
         in_specs=[SMEM] + [VMEM] * (len(arrays) + 6),
-        out_specs=(VMEM, VMEM),
+        out_specs=(VMEM, VMEM, VMEM),
         compiler_params=PARAMS,
         name="activations",
     )(me, *arrays, *weights, *sums)
@@ -236,7 +243,8 @@
     late_x = [(far, 0, half), (far, 2 * width, near), (x[-near], 0, -near)]
     late_g = [(far, width, half), (far, 3 * width, -near), (g[near], 0, near)]
     sums = first_products(me_ref, ring, width, early_x, early_g, weights)
-    grads, hidden = activations(me_ref, ring, width, late_x, late_g, weights, sums)
+    away = [half, near, -near]
+    grads, hidden, side = activations(me_ref, ring, width, late_x, late_g, weights, sums, away)
 
     paired = jnp.concatenate(weights[:2], axis=0)
 
@@ -250,10 +258,8 @@
     def added(*values):
         return sum(value.astype(jnp.float32) for value in values)
 
-    away = [half, near, -near]
     right, left = partial(near - 1), partial(1 - near)
-    side = jnp.concatenate([columns(d) for d in away], axis=1)
-    far_back = over_ep(tn(grads, side).astype(jnp.bfloat16))
+    far_back = over_ep(side)
     for d in range(near - 2, -1, -1):
         right, left = moved(right, 1), moved(left, -1)
         if d:

time: 206 us -> 207 us (level)
  matrix products: 8.48 us -> 5.14 us
    ppermute x20, waiting for transfers between devices: 31.7 us -> 41.5 us  [moved(): lax.ppermute(value, 'tp', [(i, (i + by) % ring) for i in range(ring)])]
    all_to_all x4, waiting for transfers between devices: 15 us -> 6.87 us  [over_ep(): lax.all_to_all(value.reshape(shape), 'ep', split_axis=0, concat_axis=0, t...]
    all_to_all x4, starting transfers between devices: 35 us -> 41.8 us  [over_ep(): lax.all_to_all(value.reshape(shape), 'ep', split_axis=0, concat_axis=0, t...]
    ppermute x20, starting transfers between devices: 80.7 us -> 76.1 us  [moved(): lax.ppermute(value, 'tp', [(i, (i + by) % ring) for i in range(ring)])]
    dot_general x8 -> x7, matrix products: 8.48 us -> 5.14 us  [tn(): lax.dot_general(left, right, (((0,), (0,)), ((), ())), preferred_element_...]
  transfers between devices with their start and end apart: 24 -> 24, of which waited for: 13 -> 13; matrix products, arithmetic and copies ran while one was open for 3% -> 4% of each run, Pallas kernels for 8% -> 8%
where the time goes in v6:
time: 207 us; the launch traced here: 205 us
  starting transfers between devices  118 us (57%)
  waiting for transfers between devices  48.4 us (23%)
  Pallas kernels  26.6 us (13%)
  matrix products  5.14 us (2%)
  other arithmetic  3.26 us (2%)
  local copies, waits for them, and re-layouts  2.41 us (1%)
    ppermute x20, starting transfers between devices, moved(): lax.ppermute(value, 'tp', [(i, (i + by) % ring) for i in range(ring)])  76.1 us
    all_to_all x4, starting transfers between devices, over_ep(): lax.all_to_all(value.reshape(shape), 'ep', split_axis=0, concat_axis=0, t...  41.8 us
    ppermute x20, waiting for transfers between devices, moved(): lax.ppermute(value, 'tp', [(i, (i + by) % ring) for i in range(ring)])  41.5 us
    pallas_call x1, Pallas kernels, activations(): pl.pallas_call(kernel, out_shape=(jax.ShapeDtypeStruct((2 * units, rows),...  7.24 us
    pallas_call x1, Pallas kernels, weight_grads(): pl.pallas_call(kernel, out_shape=[jax.ShapeDtypeStruct((units, ring * wid...  7.02 us
    all_to_all x4, waiting for transfers between devices, over_ep(): lax.all_to_all(value.reshape(shape), 'ep', split_axis=0, concat_axis=0, t...  6.87 us
    pallas_call x1, Pallas kernels, first_products(): pl.pallas_call(kernel, out_shape=[jax.ShapeDtypeStruct((units, rows), jnp...  6.67 us
    pallas_call x2, Pallas kernels, dispatch(): pl.pallas_call(kernel, out_shape=(jax.ShapeDtypeStruct((count, sum(widths...  5.68 us
  transfers between devices with their start and end apart: 24, of which 13 were waited for; matrix products, arithmetic and copies ran while one was open for 4% of the time, Pallas kernels for 8%

profile of v6, /device:TPU:1, one launch (start us, length us, event | category | flops | bytes accessed | tf_op | source)
XLA Modules:
  0.0 204.9 jit_solution(13626313601136553727)
XLA Ops:
  0.7 2.5 %dispatch.2 = (bf16[1024,512]{1,0:T(8,128)(2,1)}, bf16[1024,128]{1,0:T(8,128)(2,1)}) custom-call(s32[6,128]{1,0:T(8,128)} %bitcast.47, f32[6,128]{1,0:T(8,128)} %bitcast.49, bf16[128,256]{1,0:T(8,128)(2,1)} %refs_0_.1, bf16[128,256]{1,0:T(8,128)(2,1)} %refs_1_.1), custom_call_target="tpu_custom_call" | custom-call | tf_op jit(solution)/shard_map/dispatch/pallas_call | solution.py:64
  3.2 11.6 %all-to-all-start = ((bf16[64,16,512]{2,1,0:T(8,128)(2,1)}), bf16[64,16,512]{2,1,0:T(8,128)(2,1)S(1)}, u32[]{:S(2)}, u32[]{:S(2)}) async-start(bf16[64,16,512]{2,1,0:T(8,128)(2,1)} %bitcast.44), calls=%async_computation | async-start | bytes 2097152 | tf_op jit(solution)/shard_map/all_to_all | solution.py:208
  14.8 10.6 %collective-permute-start = (bf16[128,512]{1,0:T(8,128)(2,1)S(1)}, bf16[128,512]{1,0:T(8,128)(2,1)S(1)}, u32[]{:S(2)}, u32[]{:S(2)}) collective-permute-start(bf16[128,512]{1,0:T(8,128)(2,1)S(1)} %pad_maximum_fusion), channel_id=1, source_target_pairs={{0,4},{1,5},{2,6},{3,7},{4,0},{5,1},{6,2},{7,3},{8,12},{9,13},{10,... | collective-permute-start | bytes 393224 | tf_op jit(solution)/shard_map/ppermute | solution.py:204
  25.5 1.9 collective-permute-start.1
  27.4 5.2 %collective-permute-start.2 = (bf16[128,256]{1,0:T(8,128)(2,1)S(1)}, bf16[128,256]{1,0:T(8,128)(2,1)S(1)}, u32[]{:S(2)}, u32[]{:S(2)}) collective-permute-start(bf16[128,256]{1,0:T(8,128)(2,1)S(1)} %copy-done.9), channel_id=1, source_target_pairs={{0,3},{1,4},{2,5},{3,6},{4,7},{5,0},{6,1},{7,2},{8,11},{9,12},{10,... | collective-permute-start | bytes 196616 | tf_op jit(solution)/shard_map/ppermute | solution.py:204
  32.6 0.7 fusion.22
  33.3 1.8 collective-permute-done.1.refs_2_
  35.0 5.0 %collective-permute-done.2.refs_3_ = bf16[128,256]{1,0:T(8,128)(2,1)S(1)} collective-permute-done((bf16[128,256]{1,0:T(8,128)(2,1)S(1)}, bf16[128,256]{1,0:T(8,128)(2,1)S(1)}, u32[]{:S(2)}, u32[]{:S(2)}) %collective-permute-start.2) | collective-permute-done | bytes 65568 | tf_op jit(solution)/shard_map/ppermute | solution.py:204
  40.0 0.6 copy-done.11
  40.6 3.2 %dispatch.3 = (bf16[1024,1024]{1,0:T(8,128)(2,1)}, bf16[1024,128]{1,0:T(8,128)(2,1)}) custom-call(s32[6,128]{1,0:T(8,128)} %bitcast.48, f32[6,128]{1,0:T(8,128)} %bitcast.50, bf16[128,256]{1,0:T(8,128)(2,1)} %get-tuple-element.54.refs_0_, bf16[128,256]{1,0:T(8,128)(2,1)} %get-tuple-element.53.refs_1_, bf16[128,256]{1,0:T(8,128)(2,1)} %copy-done.10, ...), custom_call_target="tpu_custom_call" | custom-call | tf_op jit(solution)/shard_map/dispatch/pallas_call | solution.py:64
  43.9 3.0 %collective-permute-start.3 = (bf16[1024,256]{1,0:T(8,128)(2,1)S(1)}, bf16[1024,256]{1,0:T(8,128)(2,1)S(1)}, u32[]{:S(2)}, u32[]{:S(2)}) collective-permute-start(bf16[1024,256]{1,0:T(8,128)(2,1)S(1)} %get-tuple-element.33.refs_0_), channel_id=1, source_target_pairs={{0,1},{1,2},{2,3},{3,4},{4,5},{5,6},{6,7},{7,0},{8,9},{9,10},{10,1... | collective-permute-start | bytes 1572872 | tf_op jit(solution)/shard_map/ppermute | solution.py:204
  46.9 8.6 %collective-permute-start.6 = (bf16[1024,256]{1,0:T(8,128)(2,1)S(1)}, bf16[1024,256]{1,0:T(8,128)(2,1)S(1)}, u32[]{:S(2)}, u32[]{:S(2)}) collective-permute-start(bf16[1024,256]{1,0:T(8,128)(2,1)S(1)} %get-tuple-element.34.refs_5_.refs_7_), channel_id=1, source_target_pairs={{0,7},{1,0},{2,1},{3,2},{4,3},{5,4},{6,5},{7,6},{8,15},{9,8},{10,9... | collective-permute-start | bytes 1572872 | tf_op jit(solution)/shard_map/ppermute | solution.py:204
  55.5 6.9 %all-to-all-start.1 = ((bf16[64,16,1024]{2,1,0:T(8,128)(2,1)}), bf16[64,16,1024]{2,1,0:T(8,128)(2,1)}, u32[]{:S(2)}, u32[]{:S(2)}) async-start(bf16[64,16,1024]{2,1,0:T(8,128)(2,1)} %bitcast.41), calls=%async_computation.1 | async-start | bytes 4194304 | tf_op jit(solution)/shard_map/all_to_all | solution.py:208
  62.5 3.6 %collective-permute-start.9 = (bf16[1024,256]{1,0:T(8,128)(2,1)S(1)}, bf16[1024,256]{1,0:T(8,128)(2,1)}, u32[]{:S(2)}, u32[]{:S(2)}) collective-permute-start(bf16[1024,256]{1,0:T(8,128)(2,1)S(1)} %get-tuple-element.33.refs_0_), channel_id=1, source_target_pairs={{0,7},{1,0},{2,1},{3,2},{4,3},{5,4},{6,5},{7,6},{8,15},{9,8},{10,9... | collective-permute-start | bytes 1572872 | tf_op jit(solution)/shard_map/ppermute | solution.py:204
  66.1 1.9 collective-permute-start.11
  68.1 1.9 collective-permute-start.4
  70.0 4.6 %collective-permute-start.7 = (bf16[1024,256]{1,0:T(8,128)(2,1)S(1)}, bf16[1024,256]{1,0:T(8,128)(2,1)}, u32[]{:S(2)}, u32[]{:S(2)}) collective-permute-start(bf16[1024,256]{1,0:T(8,128)(2,1)S(1)} %collective-permute-done.6.refs_7_.refs_9_), channel_id=1, source_target_pairs={{0,7},{1,0},{2,1},{3,2},{4,3},{5,4},{6,5},{7,6},{8,15},{9,8},{10,9... | collective-permute-start | bytes 1572872 | tf_op jit(solution)/shard_map/ppermute | solution.py:204
  74.6 3.3 %collective-permute-done.9.refs_2_ = bf16[1024,256]{1,0:T(8,128)(2,1)} collective-permute-done((bf16[1024,256]{1,0:T(8,128)(2,1)S(1)}, bf16[1024,256]{1,0:T(8,128)(2,1)}, u32[]{:S(2)}, u32[]{:S(2)}) %collective-permute-start.9) | collective-permute-done | bytes 524320 | tf_op jit(solution)/shard_map/ppermute | solution.py:204
  77.9 5.4 %collective-permute-start.10 = (bf16[1024,256]{1,0:T(8,128)(2,1)}, bf16[1024,256]{1,0:T(8,128)(2,1)}, u32[]{:S(2)}, u32[]{:S(2)}) collective-permute-start(bf16[1024,256]{1,0:T(8,128)(2,1)} %collective-permute-done.9.refs_2_), channel_id=1, source_target_pairs={{0,7},{1,0},{2,1},{3,2},{4,3},{5,4},{6,5},{7,6},{8,15},{9,8},{10,9... | collective-permute-start | bytes 1572872 | tf_op jit(solution)/shard_map/ppermute | solution.py:204
  83.3 1.9 collective-permute-start.12
  85.3 7.9 %collective-permute-done.4.refs_3_ = bf16[1024,256]{1,0:T(8,128)(2,1)} collective-permute-done((bf16[1024,256]{1,0:T(8,128)(2,1)S(1)}, bf16[1024,256]{1,0:T(8,128)(2,1)}, u32[]{:S(2)}, u32[]{:S(2)}) %collective-permute-start.4) | collective-permute-done | bytes 524320 | tf_op jit(solution)/shard_map/ppermute | solution.py:204
  93.2 1.9 collective-permute-start.5
  95.2 4.6 %collective-permute-start.8 = (bf16[1024,256]{1,0:T(8,128)(2,1)}, bf16[1024,256]{1,0:T(8,128)(2,1)S(1)}, u32[]{:S(2)}, u32[]{:S(2)}) collective-permute-start(bf16[1024,256]{1,0:T(8,128)(2,1)} %collective-permute-done.7.refs_9_.refs_11_), channel_id=1, source_target_pairs={{0,7},{1,0},{2,1},{3,2},{4,3},{5,4},{6,5},{7,6},{8,15},{9,8},{10,9... | collective-permute-start | bytes 1572872 | tf_op jit(solution)/shard_map/ppermute | solution.py:204
  99.7 0.7 collective-permute-done.10.refs_4_
  100.5 4.0 %collective-permute-done.12.refs_8_.refs_10_ = bf16[1024,256]{1,0:T(8,128)(2,1)} collective-permute-done((bf16[1024,256]{1,0:T(8,128)(2,1)}, bf16[1024,256]{1,0:T(8,128)(2,1)}, u32[]{:S(2)}, u32[]{:S(2)}) %collective-permute-start.12) | collective-permute-done | bytes 524320 | tf_op jit(solution)/shard_map/ppermute | solution.py:204
  104.5 6.7 %first_products.1 = (f32[176,1024]{1,0:T(8,128)}, f32[176,1024]{1,0:T(8,128)}, f32[176,1024]{1,0:T(8,128)}) custom-call(s32[1]{0:T(128)} %bitcast.2.me_ref, bf16[1024,256]{1,0:T(8,128)(2,1)} %copy-done.7, bf16[1024,256]{1,0:T(8,128)(2,1)} %copy-done.12, bf16[1024,256]{1,0:T(8,128)(2,1)} %collective-permute-done.9.refs_2_, ...), custom_call_target="tpu_custom_call" | custom-call | flops 32856999936 | bytes 1000 | tf_op jit(solution)/shard_map/first_products/pallas_call | solution.py:108
  111.1 4.5 %collective-permute-done.5.refs_1_.refs_6_ = bf16[1024,256]{1,0:T(8,128)(2,1)S(1)} collective-permute-done((bf16[1024,256]{1,0:T(8,128)(2,1)}, bf16[1024,256]{1,0:T(8,128)(2,1)S(1)}, u32[]{:S(2)}, u32[]{:S(2)}) %collective-permute-start.5) | collective-permute-done | bytes 524320 | tf_op jit(solution)/shard_map/ppermute | solution.py:204
  115.6 0.8 copy-done.4
  116.6 7.2 %activations.1 = (bf16[352,1024]{1,0:T(8,128)(2,1)}, bf16[176,1024]{1,0:T(8,128)(2,1)}, bf16[1024,768]{1,0:T(8,128)(2,1)}) custom-call(s32[1]{0:T(128)} %bitcast.2.me_ref, bf16[1024,1024]{1,0:T(8,128)(2,1)} %bitcast.6.refs_0_.refs_5_, bf16[1024,256]{1,0:T(8,128)(2,1)} %copy-done.4, bf16[1024,256]{1,0:T(8,128)(2,1)} %copy-done.5, bf16[176,2048]{1,0:T(8,128)(2,1)} %bitcast.27, ...), custom_call_target="tpu_custom_call" | custom-call | tf_op jit(solution)/shard_map/activations/pallas_call | solution.py:148
  123.9 11.9 %all-to-all-start.3 = ((bf16[64,16,768]{2,1,0:T(8,128)(2,1)}), bf16[64,16,768]{2,1,0:T(8,128)(2,1)}, u32[]{:S(2)}, u32[]{:S(2)}) async-start(bf16[64,16,768]{2,1,0:T(8,128)(2,1)} %bitcast.43), calls=%async_computation.3 | async-start | bytes 3145728 | tf_op jit(solution)/shard_map/all_to_all | solution.py:208
  136.4 1.9 collective-permute-start.15
  138.8 3.4 %collective-permute-start.13 = (bf16[1024,256]{1,0:T(8,128)(2,1)S(1)}, bf16[1024,256]{1,0:T(8,128)(2,1)S(1)}, u32[]{:S(2)}, u32[]{:S(2)}) collective-permute-start(bf16[1024,256]{1,0:T(8,128)(2,1)S(1)} %convolution_convert_fusion.3), channel_id=1, source_target_pairs={{0,1},{1,2},{2,3},{3,4},{4,5},{5,6},{6,7},{7,0},{8,9},{9,10},{10,1... | collective-permute-start | bytes 1572872 | tf_op jit(solution)/shard_map/ppermute | solution.py:204
  142.6 0.5 convolution_convert_fusion.2
  143.1 8.2 %collective-permute-done.15 = bf16[1024,256]{1,0:T(8,128)(2,1)S(1)} collective-permute-done((bf16[1024,256]{1,0:T(8,128)(2,1)S(1)}, bf16[1024,256]{1,0:T(8,128)(2,1)S(1)}, u32[]{:S(2)}, u32[]{:S(2)}) %collective-permute-start.15) | collective-permute-done | bytes 524320 | tf_op jit(solution)/shard_map/ppermute | solution.py:204
  151.5 3.5 %collective-permute-start.16 = (bf16[1024,256]{1,0:T(8,128)(2,1)S(1)}, bf16[1024,256]{1,0:T(8,128)(2,1)}, u32[]{:S(2)}, u32[]{:S(2)}) collective-permute-start(bf16[1024,256]{1,0:T(8,128)(2,1)S(1)} %add_convert_fusion.1), channel_id=1, source_target_pairs={{0,7},{1,0},{2,1},{3,2},{4,3},{5,4},{6,5},{7,6},{8,15},{9,8},{10,9... | collective-permute-start | bytes 1572872 | tf_op jit(solution)/shard_map/ppermute | solution.py:204
  155.0 0.9 add_convert_fusion.2
  155.9 2.0 collective-permute-start.14
  158.4 7.0 %weight_grads.1 = (bf16[176,2048]{1,0:T(8,128)(2,1)}, bf16[176,2048]{1,0:T(8,128)(2,1)}, bf16[176,2048]{1,0:T(8,128)(2,1)}) custom-call(s32[1]{0:T(128)} %bitcast.2.me_ref, bf16[1024,256]{1,0:T(8,128)(2,1)} %copy-done.7, bf16[1024,256]{1,0:T(8,128)(2,1)} %copy-done.12, bf16[1024,256]{1,0:T(8,128)(2,1)} %collective-permute-done.9.refs_2_, ...), custom_call_target="tpu_custom_call" | custom-call | flops 5000000000 | bytes 1000 | tf_op jit(solution)/shard_map/weight_grads/pallas_call | solution.py:179
  165.6 5.7 %collective-permute-done.14 = bf16[1024,256]{1,0:T(8,128)(2,1)} collective-permute-done((bf16[1024,256]{1,0:T(8,128)(2,1)}, bf16[1024,256]{1,0:T(8,128)(2,1)}, u32[]{:S(2)}, u32[]{:S(2)}) %collective-permute-start.14) | collective-permute-done | bytes 524320 | tf_op jit(solution)/shard_map/ppermute | solution.py:204
  171.3 2.2 %add_convert_fusion = bf16[1024,256]{1,0:T(8,128)(2,1)} fusion(bf16[1024,256]{1,0:T(8,128)(2,1)} %collective-permute-done.16, bf16[1024,256]{1,0:T(8,128)(2,1)} %collective-permute-done.14, bf16[1024,256]{1,0:T(8,128)(2,1)S(1)} %convolution_convert_fusion.4), kind=kLoop, calls=%fused_computation.16 | loop fusion | flops 1572864 | bytes 2097152 | tf_op jit(solution)/shard_map/convert_element_type | solution.py:268
  173.5 1.2 all-to-all-done.3
  174.8 11.3 %all-to-all-start.2 = ((bf16[64,16,256]{2,1,0:T(8,128)(2,1)}), bf16[64,16,256]{2,1,0:T(8,128)(2,1)S(1)}, u32[]{:S(2)}, u32[]{:S(2)}) async-start(bf16[64,16,256]{2,1,0:T(8,128)(2,1)} %bitcast.10), calls=%async_computation.2 | async-start | bytes 1048576 | tf_op jit(solution)/shard_map/all_to_all | solution.py:208
  186.1 1.8 convolution_convert_fusion.5
  187.9 1.9 collective-permute-start.19
  189.8 5.2 %collective-permute-start.18 = (bf16[128,256]{1,0:T(8,128)(2,1)S(1)}, bf16[128,256]{1,0:T(8,128)(2,1)S(1)}, u32[]{:S(2)}, u32[]{:S(2)}) collective-permute-start(bf16[128,256]{1,0:T(8,128)(2,1)S(1)} %get-tuple-element.52), channel_id=1, source_target_pairs={{0,3},{1,4},{2,5},{3,6},{4,7},{5,0},{6,1},{7,2},{8,11},{9,12},{10,... | collective-permute-start | bytes 196616 | tf_op jit(solution)/shard_map/ppermute | solution.py:204
  195.0 3.1 %collective-permute-start.17 = (bf16[128,256]{1,0:T(8,128)(2,1)S(1)}, bf16[128,256]{1,0:T(8,128)(2,1)S(1)}, u32[]{:S(2)}, u32[]{:S(2)}) collective-permute-start(bf16[128,256]{1,0:T(8,128)(2,1)S(1)} %get-tuple-element.50), channel_id=1, source_target_pairs={{0,4},{1,5},{2,6},{3,7},{4,0},{5,1},{6,2},{7,3},{8,12},{9,13},{10,... | collective-permute-start | bytes 196616 | tf_op jit(solution)/shard_map/ppermute | solution.py:204
  198.1 5.6 %all-to-all-done.2 = bf16[64,16,256]{2,1,0:T(8,128)(2,1)S(1)} async-done(((bf16[64,16,256]{2,1,0:T(8,128)(2,1)}), bf16[64,16,256]{2,1,0:T(8,128)(2,1)S(1)}, u32[]{:S(2)}, u32[]{:S(2)}) %all-to-all-start.2) | async-done | bytes 524320 | tf_op jit(solution)/shard_map/all_to_all | solution.py:208
  204.0 0.9 add_convert_fusion.3
  (47 shorter events, 2.9 us)
Async XLA Ops:
  0.6 14.2 %copy-start.8 = (bf16[128,256]{1,0:T(8,128)(2,1)S(1)}, bf16[128,256]{1,0:T(8,128)(2,1)}, u32[]{:S(2)}) copy-start(bf16[128,256]{1,0:T(8,128)(2,1)} %refs_0_.1) | copy-start | bytes 196612
  0.6 14.2 %copy-start.9 = (bf16[128,256]{1,0:T(8,128)(2,1)S(1)}, bf16[128,256]{1,0:T(8,128)(2,1)}, u32[]{:S(2)}) copy-start(bf16[128,256]{1,0:T(8,128)(2,1)} %refs_1_.1) | copy-start | bytes 196612
  3.2 40.6 %all-to-all-start = ((bf16[64,16,512]{2,1,0:T(8,128)(2,1)}), bf16[64,16,512]{2,1,0:T(8,128)(2,1)S(1)}, u32[]{:S(2)}, u32[]{:S(2)}) async-start(bf16[64,16,512]{2,1,0:T(8,128)(2,1)} %bitcast.44), calls=%async_computation | async-start | bytes 2097152 | tf_op jit(solution)/shard_map/all_to_all | solution.py:208
  14.8 17.7 %collective-permute-start = (bf16[128,512]{1,0:T(8,128)(2,1)S(1)}, bf16[128,512]{1,0:T(8,128)(2,1)S(1)}, u32[]{:S(2)}, u32[]{:S(2)}) collective-permute-start(bf16[128,512]{1,0:T(8,128)(2,1)S(1)} %pad_maximum_fusion), channel_id=1, source_target_pairs={{0,4},{1,5},{2,6},{3,7},{4,0},{5,1},{6,2},{7,3},{8,12},{9,13},{10,... | collective-permute-start | bytes 393224 | tf_op jit(solution)/shard_map/ppermute | solution.py:204
  25.5 9.5 %collective-permute-start.1 = (bf16[128,256]{1,0:T(8,128)(2,1)S(1)}, bf16[128,256]{1,0:T(8,128)(2,1)S(1)}, u32[]{:S(2)}, u32[]{:S(2)}) collective-permute-start(bf16[128,256]{1,0:T(8,128)(2,1)S(1)} %copy-done.8), channel_id=1, source_target_pairs={{0,5},{1,6},{2,7},{3,0},{4,1},{5,2},{6,3},{7,4},{8,13},{9,14},{10,... | collective-permute-start | bytes 196616 | tf_op jit(solution)/shard_map/ppermute | solution.py:204
  27.4 12.6 %collective-permute-start.2 = (bf16[128,256]{1,0:T(8,128)(2,1)S(1)}, bf16[128,256]{1,0:T(8,128)(2,1)S(1)}, u32[]{:S(2)}, u32[]{:S(2)}) collective-permute-start(bf16[128,256]{1,0:T(8,128)(2,1)S(1)} %copy-done.9), channel_id=1, source_target_pairs={{0,3},{1,4},{2,5},{3,6},{4,7},{5,0},{6,1},{7,2},{8,11},{9,12},{10,... | collective-permute-start | bytes 196616 | tf_op jit(solution)/shard_map/ppermute | solution.py:204
  35.0 5.0 %copy-start.10 = (bf16[128,256]{1,0:T(8,128)(2,1)}, bf16[128,256]{1,0:T(8,128)(2,1)S(1)}, u32[]{:S(2)}) copy-start(bf16[128,256]{1,0:T(8,128)(2,1)S(1)} %collective-permute-done.1.refs_2_) | copy-start | bytes 196612
  40.0 0.6 copy-start.11
  43.9 18.6 %copy-start.7 = (bf16[1024,256]{1,0:T(8,128)(2,1)}, bf16[1024,256]{1,0:T(8,128)(2,1)S(1)}, u32[]{:S(2)}) copy-start(bf16[1024,256]{1,0:T(8,128)(2,1)S(1)} %get-tuple-element.33.refs_0_) | copy-start | bytes 1572868
  43.9 22.2 %copy-start.6 = (bf16[1024,256]{1,0:T(8,128)(2,1)}, bf16[1024,256]{1,0:T(8,128)(2,1)S(1)}, u32[]{:S(2)}) copy-start(bf16[1024,256]{1,0:T(8,128)(2,1)S(1)} %get-tuple-element.34.refs_5_.refs_7_) | copy-start | bytes 1572868
  43.9 24.2 %collective-permute-start.3 = (bf16[1024,256]{1,0:T(8,128)(2,1)S(1)}, bf16[1024,256]{1,0:T(8,128)(2,1)S(1)}, u32[]{:S(2)}, u32[]{:S(2)}) collective-permute-start(bf16[1024,256]{1,0:T(8,128)(2,1)S(1)} %get-tuple-element.33.refs_0_), channel_id=1, source_target_pairs={{0,1},{1,2},{2,3},{3,4},{4,5},{5,6},{6,7},{7,0},{8,9},{9,10},{10,1... | collective-permute-start | bytes 1572872 | tf_op jit(solution)/shard_map/ppermute | solution.py:204
  46.9 23.1 %collective-permute-start.6 = (bf16[1024,256]{1,0:T(8,128)(2,1)S(1)}, bf16[1024,256]{1,0:T(8,128)(2,1)S(1)}, u32[]{:S(2)}, u32[]{:S(2)}) collective-permute-start(bf16[1024,256]{1,0:T(8,128)(2,1)S(1)} %get-tuple-element.34.refs_5_.refs_7_), channel_id=1, source_target_pairs={{0,7},{1,0},{2,1},{3,2},{4,3},{5,4},{6,5},{7,6},{8,15},{9,8},{10,9... | collective-permute-start | bytes 1572872 | tf_op jit(solution)/shard_map/ppermute | solution.py:204
  55.5 60.1 %all-to-all-start.1 = ((bf16[64,16,1024]{2,1,0:T(8,128)(2,1)}), bf16[64,16,1024]{2,1,0:T(8,128)(2,1)}, u32[]{:S(2)}, u32[]{:S(2)}) async-start(bf16[64,16,1024]{2,1,0:T(8,128)(2,1)} %bitcast.41), calls=%async_computation.1 | async-start | bytes 4194304 | tf_op jit(solution)/shard_map/all_to_all | solution.py:208
  62.5 15.4 %collective-permute-start.9 = (bf16[1024,256]{1,0:T(8,128)(2,1)S(1)}, bf16[1024,256]{1,0:T(8,128)(2,1)}, u32[]{:S(2)}, u32[]{:S(2)}) collective-permute-start(bf16[1024,256]{1,0:T(8,128)(2,1)S(1)} %get-tuple-element.33.refs_0_), channel_id=1, source_target_pairs={{0,7},{1,0},{2,1},{3,2},{4,3},{5,4},{6,5},{7,6},{8,15},{9,8},{10,9... | collective-permute-start | bytes 1572872 | tf_op jit(solution)/shard_map/ppermute | solution.py:204
  66.1 17.2 %collective-permute-start.11 = (bf16[1024,256]{1,0:T(8,128)(2,1)S(1)}, bf16[1024,256]{1,0:T(8,128)(2,1)}, u32[]{:S(2)}, u32[]{:S(2)}) collective-permute-start(bf16[1024,256]{1,0:T(8,128)(2,1)S(1)} %get-tuple-element.34.refs_5_.refs_7_), channel_id=1, source_target_pairs={{0,1},{1,2},{2,3},{3,4},{4,5},{5,6},{6,7},{7,0},{8,9},{9,10},{10,1... | collective-permute-start | bytes 1572872 | tf_op jit(solution)/shard_map/ppermute | solution.py:204
  68.1 36.4 %copy-start.12 = (bf16[1024,256]{1,0:T(8,128)(2,1)}, bf16[1024,256]{1,0:T(8,128)(2,1)S(1)}, u32[]{:S(2)}) copy-start(bf16[1024,256]{1,0:T(8,128)(2,1)S(1)} %collective-permute-done.3.refs_1_) | copy-start | bytes 1572868
  68.1 25.1 %collective-permute-start.4 = (bf16[1024,256]{1,0:T(8,128)(2,1)S(1)}, bf16[1024,256]{1,0:T(8,128)(2,1)}, u32[]{:S(2)}, u32[]{:S(2)}) collective-permute-start(bf16[1024,256]{1,0:T(8,128)(2,1)S(1)} %collective-permute-done.3.refs_1_), channel_id=1, source_target_pairs={{0,1},{1,2},{2,3},{3,4},{4,5},{5,6},{6,7},{7,0},{8,9},{9,10},{10,1... | collective-permute-start | bytes 1572872 | tf_op jit(solution)/shard_map/ppermute | solution.py:204
  70.0 25.1 %copy-start.13 = (bf16[1024,256]{1,0:T(8,128)(2,1)}, bf16[1024,256]{1,0:T(8,128)(2,1)S(1)}, u32[]{:S(2)}) copy-start(bf16[1024,256]{1,0:T(8,128)(2,1)S(1)} %collective-permute-done.6.refs_7_.refs_9_) | copy-start | bytes 1572868
  70.0 25.1 %collective-permute-start.7 = (bf16[1024,256]{1,0:T(8,128)(2,1)S(1)}, bf16[1024,256]{1,0:T(8,128)(2,1)}, u32[]{:S(2)}, u32[]{:S(2)}) collective-permute-start(bf16[1024,256]{1,0:T(8,128)(2,1)S(1)} %collective-permute-done.6.refs_7_.refs_9_), channel_id=1, source_target_pairs={{0,7},{1,0},{2,1},{3,2},{4,3},{5,4},{6,5},{7,6},{8,15},{9,8},{10,9... | collective-permute-start | bytes 1572872 | tf_op jit(solution)/shard_map/ppermute | solution.py:204
  77.9 22.6 %collective-permute-start.10 = (bf16[1024,256]{1,0:T(8,128)(2,1)}, bf16[1024,256]{1,0:T(8,128)(2,1)}, u32[]{:S(2)}, u32[]{:S(2)}) collective-permute-start(bf16[1024,256]{1,0:T(8,128)(2,1)} %collective-permute-done.9.refs_2_), channel_id=1, source_target_pairs={{0,7},{1,0},{2,1},{3,2},{4,3},{5,4},{6,5},{7,6},{8,15},{9,8},{10,9... | collective-permute-start | bytes 1572872 | tf_op jit(solution)/shard_map/ppermute | solution.py:204
  83.3 21.1 %collective-permute-start.12 = (bf16[1024,256]{1,0:T(8,128)(2,1)}, bf16[1024,256]{1,0:T(8,128)(2,1)}, u32[]{:S(2)}, u32[]{:S(2)}) collective-permute-start(bf16[1024,256]{1,0:T(8,128)(2,1)} %collective-permute-done.11.refs_6_.refs_8_), channel_id=1, source_target_pairs={{0,1},{1,2},{2,3},{3,4},{4,5},{5,6},{6,7},{7,0},{8,9},{9,10},{10,1... | collective-permute-start | bytes 1572872 | tf_op jit(solution)/shard_map/ppermute | solution.py:204
  93.2 22.4 %collective-permute-start.5 = (bf16[1024,256]{1,0:T(8,128)(2,1)}, bf16[1024,256]{1,0:T(8,128)(2,1)S(1)}, u32[]{:S(2)}, u32[]{:S(2)}) collective-permute-start(bf16[1024,256]{1,0:T(8,128)(2,1)} %collective-permute-done.4.refs_3_), channel_id=1, source_target_pairs={{0,1},{1,2},{2,3},{3,4},{4,5},{5,6},{6,7},{7,0},{8,9},{9,10},{10,1... | collective-permute-start | bytes 1572872 | tf_op jit(solution)/shard_map/ppermute | solution.py:204
  95.2 20.4 %collective-permute-start.8 = (bf16[1024,256]{1,0:T(8,128)(2,1)}, bf16[1024,256]{1,0:T(8,128)(2,1)S(1)}, u32[]{:S(2)}, u32[]{:S(2)}) collective-permute-start(bf16[1024,256]{1,0:T(8,128)(2,1)} %collective-permute-done.7.refs_9_.refs_11_), channel_id=1, source_target_pairs={{0,7},{1,0},{2,1},{3,2},{4,3},{5,4},{6,5},{7,6},{8,15},{9,8},{10,9... | collective-permute-start | bytes 1572872 | tf_op jit(solution)/shard_map/ppermute | solution.py:204
  115.6 0.8 copy-start.4
  115.6 1.0 copy-start.5
  123.9 12.0 %copy-start = (bf16[1,176,2048]{2,1,0:T(8,128)(2,1)S(1)}, bf16[1,176,2048]{2,1,0:T(8,128)(2,1)}, u32[]{:S(2)}) copy-start(bf16[1,176,2048]{2,1,0:T(8,128)(2,1)} %param.11) | copy-start | bytes 2162692
  123.9 12.0 %copy-start.1 = (bf16[1,176,2048]{2,1,0:T(8,128)(2,1)S(1)}, bf16[1,176,2048]{2,1,0:T(8,128)(2,1)}, u32[]{:S(2)}) copy-start(bf16[1,176,2048]{2,1,0:T(8,128)(2,1)} %param.12) | copy-start | bytes 2162692
  123.9 12.0 %copy-start.2 = (bf16[352,1024]{1,0:T(8,128)(2,1)S(1)}, bf16[352,1024]{1,0:T(8,128)(2,1)}, u32[]{:S(2)}) copy-start(bf16[352,1024]{1,0:T(8,128)(2,1)} %get-tuple-element.38.refs_13_) | copy-start | bytes 2162692
  123.9 50.9 %all-to-all-start.3 = ((bf16[64,16,768]{2,1,0:T(8,128)(2,1)}), bf16[64,16,768]{2,1,0:T(8,128)(2,1)}, u32[]{:S(2)}, u32[]{:S(2)}) async-start(bf16[64,16,768]{2,1,0:T(8,128)(2,1)} %bitcast.43), calls=%async_computation.3 | async-start | bytes 3145728 | tf_op jit(solution)/shard_map/all_to_all | solution.py:208
  136.4 15.0 %collective-permute-start.15 = (bf16[1024,256]{1,0:T(8,128)(2,1)S(1)}, bf16[1024,256]{1,0:T(8,128)(2,1)S(1)}, u32[]{:S(2)}, u32[]{:S(2)}) collective-permute-start(bf16[1024,256]{1,0:T(8,128)(2,1)S(1)} %convolution_convert_fusion.1), channel_id=1, source_target_pairs={{0,7},{1,0},{2,1},{3,2},{4,3},{5,4},{6,5},{7,6},{8,15},{9,8},{10,9... | collective-permute-start | bytes 1572872 | tf_op jit(solution)/shard_map/ppermute | solution.py:204
  138.8 16.2 %collective-permute-start.13 = (bf16[1024,256]{1,0:T(8,128)(2,1)S(1)}, bf16[1024,256]{1,0:T(8,128)(2,1)S(1)}, u32[]{:S(2)}, u32[]{:S(2)}) collective-permute-start(bf16[1024,256]{1,0:T(8,128)(2,1)S(1)} %convolution_convert_fusion.3), channel_id=1, source_target_pairs={{0,1},{1,2},{2,3},{3,4},{4,5},{5,6},{6,7},{7,0},{8,9},{9,10},{10,1... | collective-permute-start | bytes 1572872 | tf_op jit(solution)/shard_map/ppermute | solution.py:204
  151.5 14.1 %collective-permute-start.16 = (bf16[1024,256]{1,0:T(8,128)(2,1)S(1)}, bf16[1024,256]{1,0:T(8,128)(2,1)}, u32[]{:S(2)}, u32[]{:S(2)}) collective-permute-start(bf16[1024,256]{1,0:T(8,128)(2,1)S(1)} %add_convert_fusion.1), channel_id=1, source_target_pairs={{0,7},{1,0},{2,1},{3,2},{4,3},{5,4},{6,5},{7,6},{8,15},{9,8},{10,9... | collective-permute-start | bytes 1572872 | tf_op jit(solution)/shard_map/ppermute | solution.py:204
  155.9 15.4 %collective-permute-start.14 = (bf16[1024,256]{1,0:T(8,128)(2,1)}, bf16[1024,256]{1,0:T(8,128)(2,1)}, u32[]{:S(2)}, u32[]{:S(2)}) collective-permute-start(bf16[1024,256]{1,0:T(8,128)(2,1)} %add_convert_fusion.2), channel_id=1, source_target_pairs={{0,1},{1,2},{2,3},{3,4},{4,5},{5,6},{6,7},{7,0},{8,9},{9,10},{10,1... | collective-permute-start | bytes 1572872 | tf_op jit(solution)/shard_map/ppermute | solution.py:204
  165.4 20.7 %copy-start.3 = (bf16[1024,128]{1,0:T(8,128)(2,1)S(1)}, bf16[1024,128]{1,0:T(8,128)(2,1)}, u32[]{:S(2)}) copy-start(bf16[1024,128]{1,0:T(8,128)(2,1)} %get-tuple-element.26) | copy-start | bytes 786436
  174.8 29.0 %all-to-all-start.2 = ((bf16[64,16,256]{2,1,0:T(8,128)(2,1)}), bf16[64,16,256]{2,1,0:T(8,128)(2,1)S(1)}, u32[]{:S(2)}, u32[]{:S(2)}) async-start(bf16[64,16,256]{2,1,0:T(8,128)(2,1)} %bitcast.10), calls=%async_computation.2 | async-start | bytes 1048576 | tf_op jit(solution)/shard_map/all_to_all | solution.py:208
  187.9 15.9 %collective-permute-start.19 = (bf16[128,256]{1,0:T(8,128)(2,1)S(1)}, bf16[128,256]{1,0:T(8,128)(2,1)S(1)}, u32[]{:S(2)}, u32[]{:S(2)}) collective-permute-start(bf16[128,256]{1,0:T(8,128)(2,1)S(1)} %get-tuple-element.51), channel_id=1, source_target_pairs={{0,5},{1,6},{2,7},{3,0},{4,1},{5,2},{6,3},{7,4},{8,13},{9,14},{10,... | collective-permute-start | bytes 196616 | tf_op jit(solution)/shard_map/ppermute | solution.py:204
  189.8 13.9 %collective-permute-start.18 = (bf16[128,256]{1,0:T(8,128)(2,1)S(1)}, bf16[128,256]{1,0:T(8,128)(2,1)S(1)}, u32[]{:S(2)}, u32[]{:S(2)}) collective-permute-start(bf16[128,256]{1,0:T(8,128)(2,1)S(1)} %get-tuple-element.52), channel_id=1, source_target_pairs={{0,3},{1,4},{2,5},{3,6},{4,7},{5,0},{6,1},{7,2},{8,11},{9,12},{10,... | collective-permute-start | bytes 196616 | tf_op jit(solution)/shard_map/ppermute | solution.py:204
  195.0 9.0 %collective-permute-start.17 = (bf16[128,256]{1,0:T(8,128)(2,1)S(1)}, bf16[128,256]{1,0:T(8,128)(2,1)S(1)}, u32[]{:S(2)}, u32[]{:S(2)}) collective-permute-start(bf16[128,256]{1,0:T(8,128)(2,1)S(1)} %get-tuple-element.50), channel_id=1, source_target_pairs={{0,4},{1,5},{2,6},{3,7},{4,0},{5,1},{6,2},{7,3},{8,12},{9,13},{10,... | collective-permute-start | bytes 196616 | tf_op jit(solution)/shard_map/ppermute | solution.py:204

commit v7 on v5

--- a/solution.py
+++ b/solution.py
@@ -8,7 +8,7 @@
 
 VMEM = pl.BlockSpec(memory_space=pltpu.VMEM)
 SMEM = pl.BlockSpec(memory_space=pltpu.SMEM)
-PARAMS = pltpu.CompilerParams(vmem_limit_bytes=56 * 1024 * 1024)
+PARAMS = pltpu.CompilerParams(vmem_limit_bytes=62 * 1024 * 1024)
 
 
 def nt(left, right):

time: 205 us -> 206 us (level)
  transfers between devices with their start and end apart: 24 -> 24, of which waited for: 14 -> 11; matrix products, arithmetic and copies ran while one was open for 3% -> 4% of each run, Pallas kernels for 10% -> 10%
where the time goes in v7:
time: 206 us; the launch traced here: 205 us
  starting transfers between devices  120 us (58%)
  waiting for transfers between devices  42.1 us (20%)
  Pallas kernels  30 us (15%)
  matrix products  5.15 us (2%)
  other arithmetic  3.29 us (2%)
  local copies, waits for them, and re-layouts  3.01 us (1%)
    ppermute x20, starting transfers between devices, moved(): lax.ppermute(value, 'tp', [(i, (i + by) % ring) for i in range(ring)])  81.4 us
    all_to_all x4, starting transfers between devices, over_ep(): lax.all_to_all(value.reshape(shape), 'ep', split_axis=0, concat_axis=0, t...  39.1 us
    ppermute x20, waiting for transfers between devices, moved(): lax.ppermute(value, 'tp', [(i, (i + by) % ring) for i in range(ring)])  35.4 us
    pallas_call x2, Pallas kernels, first_products(): pl.pallas_call(kernel, out_shape=[jax.ShapeDtypeStruct((units, rows), jnp...  10.9 us
    pallas_call x1, Pallas kernels, weight_grads(): pl.pallas_call(kernel, out_shape=[jax.ShapeDtypeStruct((units, ring * wid...  7.02 us
    all_to_all x4, waiting for transfers between devices, over_ep(): lax.all_to_all(value.reshape(shape), 'ep', split_axis=0, concat_axis=0, t...  6.73 us
    pallas_call x1, Pallas kernels, activations(): pl.pallas_call(kernel, out_shape=(jax.ShapeDtypeStruct((2 * units, rows),...  6.36 us
    pallas_call x2, Pallas kernels, dispatch(): pl.pallas_call(kernel, out_shape=(jax.ShapeDtypeStruct((count, sum(widths...  5.68 us
  transfers between devices with their start and end apart: 24, of which 11 were waited for; matrix products, arithmetic and copies ran while one was open for 4% of the time, Pallas kernels for 10%

profile of v7, /device:TPU:1, one launch (start us, length us, event | category | flops | bytes accessed | tf_op | source)
XLA Modules:
  0.0 205.1 jit_solution(15269111534767213042)
XLA Ops:
  0.7 2.5 %dispatch.2 = (bf16[1024,512]{1,0:T(8,128)(2,1)}, bf16[1024,128]{1,0:T(8,128)(2,1)}) custom-call(s32[6,128]{1,0:T(8,128)} %bitcast.50, f32[6,128]{1,0:T(8,128)} %bitcast.52, bf16[128,256]{1,0:T(8,128)(2,1)} %refs_0_.1, bf16[128,256]{1,0:T(8,128)(2,1)} %refs_1_.1), custom_call_target="tpu_custom_call" | custom-call | tf_op jit(solution)/shard_map/dispatch/pallas_call | solution.py:64
  3.2 11.6 %all-to-all-start = ((bf16[64,16,512]{2,1,0:T(8,128)(2,1)}), bf16[64,16,512]{2,1,0:T(8,128)(2,1)S(1)}, u32[]{:S(2)}, u32[]{:S(2)}) async-start(bf16[64,16,512]{2,1,0:T(8,128)(2,1)} %bitcast.49), calls=%async_computation | async-start | bytes 2097152 | tf_op jit(solution)/shard_map/all_to_all | solution.py:212
  14.8 10.6 %collective-permute-start = (bf16[128,512]{1,0:T(8,128)(2,1)S(1)}, bf16[128,512]{1,0:T(8,128)(2,1)S(1)}, u32[]{:S(2)}, u32[]{:S(2)}) collective-permute-start(bf16[128,512]{1,0:T(8,128)(2,1)S(1)} %pad_maximum_fusion), channel_id=1, source_target_pairs={{0,4},{1,5},{2,6},{3,7},{4,0},{5,1},{6,2},{7,3},{8,12},{9,13},{10,... | collective-permute-start | bytes 393224 | tf_op jit(solution)/shard_map/ppermute | solution.py:208
  25.5 1.9 collective-permute-start.1
  27.4 5.2 %collective-permute-start.2 = (bf16[128,256]{1,0:T(8,128)(2,1)S(1)}, bf16[128,256]{1,0:T(8,128)(2,1)S(1)}, u32[]{:S(2)}, u32[]{:S(2)}) collective-permute-start(bf16[128,256]{1,0:T(8,128)(2,1)S(1)} %copy-done.9), channel_id=1, source_target_pairs={{0,3},{1,4},{2,5},{3,6},{4,7},{5,0},{6,1},{7,2},{8,11},{9,12},{10,... | collective-permute-start | bytes 196616 | tf_op jit(solution)/shard_map/ppermute | solution.py:208
  32.6 0.7 fusion.22
  33.3 1.8 collective-permute-done.1.refs_2_
  35.0 5.0 %collective-permute-done.2.refs_3_ = bf16[128,256]{1,0:T(8,128)(2,1)S(1)} collective-permute-done((bf16[128,256]{1,0:T(8,128)(2,1)S(1)}, bf16[128,256]{1,0:T(8,128)(2,1)S(1)}, u32[]{:S(2)}, u32[]{:S(2)}) %collective-permute-start.2) | collective-permute-done | bytes 65568 | tf_op jit(solution)/shard_map/ppermute | solution.py:208
  40.6 3.2 %dispatch.3 = (bf16[1024,1024]{1,0:T(8,128)(2,1)}, bf16[1024,128]{1,0:T(8,128)(2,1)}) custom-call(s32[6,128]{1,0:T(8,128)} %bitcast.51, f32[6,128]{1,0:T(8,128)} %bitcast.53, bf16[128,256]{1,0:T(8,128)(2,1)} %get-tuple-element.60.refs_0_, bf16[128,256]{1,0:T(8,128)(2,1)} %get-tuple-element.59.refs_1_, bf16[128,256]{1,0:T(8,128)(2,1)} %copy-done.10, ...), custom_call_target="tpu_custom_call" | custom-call | tf_op jit(solution)/shard_map/dispatch/pallas_call | solution.py:64
  43.9 3.0 %collective-permute-start.3 = (bf16[1024,256]{1,0:T(8,128)(2,1)S(1)}, bf16[1024,256]{1,0:T(8,128)(2,1)S(1)}, u32[]{:S(2)}, u32[]{:S(2)}) collective-permute-start(bf16[1024,256]{1,0:T(8,128)(2,1)S(1)} %get-tuple-element.36.refs_0_), channel_id=1, source_target_pairs={{0,1},{1,2},{2,3},{3,4},{4,5},{5,6},{6,7},{7,0},{8,9},{9,10},{10,1... | collective-permute-start | bytes 1572872 | tf_op jit(solution)/shard_map/ppermute | solution.py:208
  46.9 8.6 %collective-permute-start.6 = (bf16[1024,256]{1,0:T(8,128)(2,1)S(1)}, bf16[1024,256]{1,0:T(8,128)(2,1)S(1)}, u32[]{:S(2)}, u32[]{:S(2)}) collective-permute-start(bf16[1024,256]{1,0:T(8,128)(2,1)S(1)} %get-tuple-element.37.refs_5_.refs_7_), channel_id=1, source_target_pairs={{0,7},{1,0},{2,1},{3,2},{4,3},{5,4},{6,5},{7,6},{8,15},{9,8},{10,9... | collective-permute-start | bytes 1572872 | tf_op jit(solution)/shard_map/ppermute | solution.py:208
  55.5 3.4 %collective-permute-start.9 = (bf16[1024,256]{1,0:T(8,128)(2,1)S(1)}, bf16[1024,256]{1,0:T(8,128)(2,1)}, u32[]{:S(2)}, u32[]{:S(2)}) collective-permute-start(bf16[1024,256]{1,0:T(8,128)(2,1)S(1)} %get-tuple-element.36.refs_0_), channel_id=1, source_target_pairs={{0,7},{1,0},{2,1},{3,2},{4,3},{5,4},{6,5},{7,6},{8,15},{9,8},{10,9... | collective-permute-start | bytes 1572872 | tf_op jit(solution)/shard_map/ppermute | solution.py:208
  58.9 1.9 collective-permute-start.11
  60.8 7.5 %all-to-all-start.1 = ((bf16[64,16,1024]{2,1,0:T(8,128)(2,1)}), bf16[64,16,1024]{2,1,0:T(8,128)(2,1)}, u32[]{:S(2)}, u32[]{:S(2)}) async-start(bf16[64,16,1024]{2,1,0:T(8,128)(2,1)} %bitcast.46), calls=%async_computation.1 | async-start | bytes 4194304 | tf_op jit(solution)/shard_map/all_to_all | solution.py:212
  68.4 1.9 collective-permute-start.4
  70.3 4.9 %collective-permute-start.7 = (bf16[1024,256]{1,0:T(8,128)(2,1)S(1)}, bf16[1024,256]{1,0:T(8,128)(2,1)}, u32[]{:S(2)}, u32[]{:S(2)}) collective-permute-start(bf16[1024,256]{1,0:T(8,128)(2,1)S(1)} %collective-permute-done.6.refs_7_.refs_9_), channel_id=1, source_target_pairs={{0,7},{1,0},{2,1},{3,2},{4,3},{5,4},{6,5},{7,6},{8,15},{9,8},{10,9... | collective-permute-start | bytes 1572872 | tf_op jit(solution)/shard_map/ppermute | solution.py:208
  75.2 1.4 collective-permute-done.9.refs_2_
  76.6 5.4 %collective-permute-start.10 = (bf16[1024,256]{1,0:T(8,128)(2,1)}, bf16[1024,256]{1,0:T(8,128)(2,1)}, u32[]{:S(2)}, u32[]{:S(2)}) collective-permute-start(bf16[1024,256]{1,0:T(8,128)(2,1)} %collective-permute-done.9.refs_2_), channel_id=1, source_target_pairs={{0,7},{1,0},{2,1},{3,2},{4,3},{5,4},{6,5},{7,6},{8,15},{9,8},{10,9... | collective-permute-start | bytes 1572872 | tf_op jit(solution)/shard_map/ppermute | solution.py:208
  82.0 1.9 collective-permute-start.12
  83.9 3.3 %collective-permute-done.4.refs_3_ = bf16[1024,256]{1,0:T(8,128)(2,1)} collective-permute-done((bf16[1024,256]{1,0:T(8,128)(2,1)S(1)}, bf16[1024,256]{1,0:T(8,128)(2,1)}, u32[]{:S(2)}, u32[]{:S(2)}) %collective-permute-start.4) | collective-permute-done | bytes 524320 | tf_op jit(solution)/shard_map/ppermute | solution.py:208
  87.2 1.9 collective-permute-start.5
  89.2 4.6 %collective-permute-start.8 = (bf16[1024,256]{1,0:T(8,128)(2,1)}, bf16[1024,256]{1,0:T(8,128)(2,1)S(1)}, u32[]{:S(2)}, u32[]{:S(2)}) collective-permute-start(bf16[1024,256]{1,0:T(8,128)(2,1)} %collective-permute-done.7.refs_9_.refs_11_), channel_id=1, source_target_pairs={{0,7},{1,0},{2,1},{3,2},{4,3},{5,4},{6,5},{7,6},{8,15},{9,8},{10,9... | collective-permute-start | bytes 1572872 | tf_op jit(solution)/shard_map/ppermute | solution.py:208
  93.8 5.4 %collective-permute-done.10.refs_4_ = bf16[1024,256]{1,0:T(8,128)(2,1)} collective-permute-done((bf16[1024,256]{1,0:T(8,128)(2,1)}, bf16[1024,256]{1,0:T(8,128)(2,1)}, u32[]{:S(2)}, u32[]{:S(2)}) %collective-permute-start.10) | collective-permute-done | bytes 524320 | tf_op jit(solution)/shard_map/ppermute | solution.py:208
  99.2 0.8 copy-done.14
  100.0 6.7 %first_products.2 = (f32[176,1024]{1,0:T(8,128)}, f32[176,1024]{1,0:T(8,128)}, f32[176,1024]{1,0:T(8,128)}) custom-call(s32[1]{0:T(128)} %bitcast.2.me_ref, bf16[1024,256]{1,0:T(8,128)(2,1)} %copy-done.5, bf16[1024,256]{1,0:T(8,128)(2,1)} %copy-done.12, bf16[1024,256]{1,0:T(8,128)(2,1)} %collective-permute-done.9.refs_2_, ...), custom_call_target="tpu_custom_call" | custom-call | flops 33999998976 | bytes 1000 | tf_op jit(solution)/shard_map/first_products/pallas_call | solution.py:112
  106.6 3.7 %collective-permute-done.8.refs_1_.refs_12_ = bf16[1024,256]{1,0:T(8,128)(2,1)S(1)} collective-permute-done((bf16[1024,256]{1,0:T(8,128)(2,1)}, bf16[1024,256]{1,0:T(8,128)(2,1)S(1)}, u32[]{:S(2)}, u32[]{:S(2)}) %collective-permute-start.8) | collective-permute-done | bytes 524320 | tf_op jit(solution)/shard_map/ppermute | solution.py:208
  110.4 0.8 copy-done.7
  111.2 4.3 %first_products.3 = (f32[176,1024]{1,0:T(8,128)}, f32[176,1024]{1,0:T(8,128)}, f32[176,1024]{1,0:T(8,128)}) custom-call(s32[1]{0:T(128)} %bitcast.2.me_ref, bf16[1024,256]{1,0:T(8,128)(2,1)} %copy-done.6, bf16[1024,256]{1,0:T(8,128)(2,1)} %copy-done.7, bf16[176,2048]{1,0:T(8,128)(2,1)} %bitcast.27, bf16[176,2048]{1,0:T(8,128)(2,1)} %bitcast.35, ...), custom_call_target="tpu_custom_call" | custom-call | flops 1000000000 | bytes 1000 | tf_op jit(solution)/shard_map/first_products/pallas_call | solution.py:112
  115.4 2.5 %all-to-all-done.1 = bf16[64,16,1024]{2,1,0:T(8,128)(2,1)} async-done(((bf16[64,16,1024]{2,1,0:T(8,128)(2,1)}), bf16[64,16,1024]{2,1,0:T(8,128)(2,1)}, u32[]{:S(2)}, u32[]{:S(2)}) %all-to-all-start.1) | async-done | bytes 2097184 | tf_op jit(solution)/shard_map/all_to_all | solution.py:212
  117.9 6.4 %activations.1 = (bf16[352,1024]{1,0:T(8,128)(2,1)}, bf16[176,1024]{1,0:T(8,128)(2,1)}, bf16[1024,768]{1,0:T(8,128)(2,1)}) custom-call(s32[1]{0:T(128)} %bitcast.2.me_ref, bf16[1024,1024]{1,0:T(8,128)(2,1)} %bitcast.6.refs_0_.refs_6_, bf16[176,2048]{1,0:T(8,128)(2,1)} %bitcast.28, bf16[176,2048]{1,0:T(8,128)(2,1)} %bitcast.36, bf16[176,2048]{1,0:T(8,128)(2,1)} %bitcast.45, ...), custom_call_target="tpu_custom_call" | custom-call | tf_op jit(solution)/shard_map/activations/pallas_call | solution.py:152
  124.3 7.3 %all-to-all-start.3 = ((bf16[64,16,768]{2,1,0:T(8,128)(2,1)}), bf16[64,16,768]{2,1,0:T(8,128)(2,1)}, u32[]{:S(2)}, u32[]{:S(2)}) async-start(bf16[64,16,768]{2,1,0:T(8,128)(2,1)} %bitcast.48), calls=%async_computation.3 | async-start | bytes 3145728 | tf_op jit(solution)/shard_map/all_to_all | solution.py:212
  132.2 5.1 %collective-permute-start.15 = (bf16[1024,256]{1,0:T(8,128)(2,1)S(1)}, bf16[1024,256]{1,0:T(8,128)(2,1)S(1)}, u32[]{:S(2)}, u32[]{:S(2)}) collective-permute-start(bf16[1024,256]{1,0:T(8,128)(2,1)S(1)} %convolution_convert_fusion.1), channel_id=1, source_target_pairs={{0,7},{1,0},{2,1},{3,2},{4,3},{5,4},{6,5},{7,6},{8,15},{9,8},{10,9... | collective-permute-start | bytes 1572872 | tf_op jit(solution)/shard_map/ppermute | solution.py:208
  137.8 2.1 %collective-permute-start.13 = (bf16[1024,256]{1,0:T(8,128)(2,1)S(1)}, bf16[1024,256]{1,0:T(8,128)(2,1)S(1)}, u32[]{:S(2)}, u32[]{:S(2)}) collective-permute-start(bf16[1024,256]{1,0:T(8,128)(2,1)S(1)} %convolution_convert_fusion.3), channel_id=1, source_target_pairs={{0,1},{1,2},{2,3},{3,4},{4,5},{5,6},{6,7},{7,0},{8,9},{9,10},{10,1... | collective-permute-start | bytes 1572872 | tf_op jit(solution)/shard_map/ppermute | solution.py:208
  140.9 7.2 %collective-permute-done.15 = bf16[1024,256]{1,0:T(8,128)(2,1)S(1)} collective-permute-done((bf16[1024,256]{1,0:T(8,128)(2,1)S(1)}, bf16[1024,256]{1,0:T(8,128)(2,1)S(1)}, u32[]{:S(2)}, u32[]{:S(2)}) %collective-permute-start.15) | collective-permute-done | bytes 524320 | tf_op jit(solution)/shard_map/ppermute | solution.py:208
  148.2 5.4 %collective-permute-start.16 = (bf16[1024,256]{1,0:T(8,128)(2,1)S(1)}, bf16[1024,256]{1,0:T(8,128)(2,1)}, u32[]{:S(2)}, u32[]{:S(2)}) collective-permute-start(bf16[1024,256]{1,0:T(8,128)(2,1)S(1)} %add_convert_fusion.1), channel_id=1, source_target_pairs={{0,7},{1,0},{2,1},{3,2},{4,3},{5,4},{6,5},{7,6},{8,15},{9,8},{10,9... | collective-permute-start | bytes 1572872 | tf_op jit(solution)/shard_map/ppermute | solution.py:208
  153.7 1.0 add_convert_fusion.2
  154.6 1.9 collective-permute-start.14
  157.0 7.0 %weight_grads.1 = (bf16[176,2048]{1,0:T(8,128)(2,1)}, bf16[176,2048]{1,0:T(8,128)(2,1)}, bf16[176,2048]{1,0:T(8,128)(2,1)}) custom-call(s32[1]{0:T(128)} %bitcast.2.me_ref, bf16[1024,256]{1,0:T(8,128)(2,1)} %copy-done.5, bf16[1024,256]{1,0:T(8,128)(2,1)} %copy-done.12, bf16[1024,256]{1,0:T(8,128)(2,1)} %collective-permute-done.9.refs_2_, ...), custom_call_target="tpu_custom_call" | custom-call | flops 5000000000 | bytes 1000 | tf_op jit(solution)/shard_map/weight_grads/pallas_call | solution.py:183
  164.1 5.8 %collective-permute-done.14 = bf16[1024,256]{1,0:T(8,128)(2,1)} collective-permute-done((bf16[1024,256]{1,0:T(8,128)(2,1)}, bf16[1024,256]{1,0:T(8,128)(2,1)}, u32[]{:S(2)}, u32[]{:S(2)}) %collective-permute-start.14) | collective-permute-done | bytes 524320 | tf_op jit(solution)/shard_map/ppermute | solution.py:208
  169.9 2.2 %add_convert_fusion = bf16[1024,256]{1,0:T(8,128)(2,1)} fusion(bf16[1024,256]{1,0:T(8,128)(2,1)} %collective-permute-done.16, bf16[1024,256]{1,0:T(8,128)(2,1)} %collective-permute-done.14, bf16[1024,256]{1,0:T(8,128)(2,1)S(1)} %convolution_convert_fusion.4), kind=kLoop, calls=%fused_computation.16 | loop fusion | flops 1572864 | bytes 2097152 | tf_op jit(solution)/shard_map/convert_element_type | solution.py:274
  172.1 12.6 %all-to-all-start.2 = ((bf16[64,16,256]{2,1,0:T(8,128)(2,1)}), bf16[64,16,256]{2,1,0:T(8,128)(2,1)S(1)}, u32[]{:S(2)}, u32[]{:S(2)}) async-start(bf16[64,16,256]{2,1,0:T(8,128)(2,1)} %bitcast.10), calls=%async_computation.2 | async-start | bytes 1048576 | tf_op jit(solution)/shard_map/all_to_all | solution.py:212
  184.7 1.8 convolution_convert_fusion.5
  186.5 2.2 %collective-permute-start.19 = (bf16[128,256]{1,0:T(8,128)(2,1)S(1)}, bf16[128,256]{1,0:T(8,128)(2,1)S(1)}, u32[]{:S(2)}, u32[]{:S(2)}) collective-permute-start(bf16[128,256]{1,0:T(8,128)(2,1)S(1)} %get-tuple-element.57), channel_id=1, source_target_pairs={{0,5},{1,6},{2,7},{3,0},{4,1},{5,2},{6,3},{7,4},{8,13},{9,14},{10,... | collective-permute-start | bytes 196616 | tf_op jit(solution)/shard_map/ppermute | solution.py:208
  188.7 4.9 %collective-permute-start.18 = (bf16[128,256]{1,0:T(8,128)(2,1)S(1)}, bf16[128,256]{1,0:T(8,128)(2,1)S(1)}, u32[]{:S(2)}, u32[]{:S(2)}) collective-permute-start(bf16[128,256]{1,0:T(8,128)(2,1)S(1)} %get-tuple-element.58), channel_id=1, source_target_pairs={{0,3},{1,4},{2,5},{3,6},{4,7},{5,0},{6,1},{7,2},{8,11},{9,12},{10,... | collective-permute-start | bytes 196616 | tf_op jit(solution)/shard_map/ppermute | solution.py:208
  193.6 4.5 %collective-permute-start.17 = (bf16[128,256]{1,0:T(8,128)(2,1)S(1)}, bf16[128,256]{1,0:T(8,128)(2,1)S(1)}, u32[]{:S(2)}, u32[]{:S(2)}) collective-permute-start(bf16[128,256]{1,0:T(8,128)(2,1)S(1)} %get-tuple-element.56), channel_id=1, source_target_pairs={{0,4},{1,5},{2,6},{3,7},{4,0},{5,1},{6,2},{7,3},{8,12},{9,13},{10,... | collective-permute-start | bytes 196616 | tf_op jit(solution)/shard_map/ppermute | solution.py:208
  198.2 4.2 %all-to-all-done.2 = bf16[64,16,256]{2,1,0:T(8,128)(2,1)S(1)} async-done(((bf16[64,16,256]{2,1,0:T(8,128)(2,1)}), bf16[64,16,256]{2,1,0:T(8,128)(2,1)S(1)}, u32[]{:S(2)}, u32[]{:S(2)}) %all-to-all-start.2) | async-done | bytes 524320 | tf_op jit(solution)/shard_map/all_to_all | solution.py:212
  202.4 1.7 collective-permute-done.17
  204.1 0.9 add_convert_fusion.3
  (50 shorter events, 3.4 us)
Async XLA Ops:
  0.6 14.2 %copy-start.8 = (bf16[128,256]{1,0:T(8,128)(2,1)S(1)}, bf16[128,256]{1,0:T(8,128)(2,1)}, u32[]{:S(2)}) copy-start(bf16[128,256]{1,0:T(8,128)(2,1)} %refs_0_.1) | copy-start | bytes 196612
  0.6 14.2 %copy-start.9 = (bf16[128,256]{1,0:T(8,128)(2,1)S(1)}, bf16[128,256]{1,0:T(8,128)(2,1)}, u32[]{:S(2)}) copy-start(bf16[128,256]{1,0:T(8,128)(2,1)} %refs_1_.1) | copy-start | bytes 196612
  3.2 40.6 %all-to-all-start = ((bf16[64,16,512]{2,1,0:T(8,128)(2,1)}), bf16[64,16,512]{2,1,0:T(8,128)(2,1)S(1)}, u32[]{:S(2)}, u32[]{:S(2)}) async-start(bf16[64,16,512]{2,1,0:T(8,128)(2,1)} %bitcast.49), calls=%async_computation | async-start | bytes 2097152 | tf_op jit(solution)/shard_map/all_to_all | solution.py:212
  14.8 17.7 %collective-permute-start = (bf16[128,512]{1,0:T(8,128)(2,1)S(1)}, bf16[128,512]{1,0:T(8,128)(2,1)S(1)}, u32[]{:S(2)}, u32[]{:S(2)}) collective-permute-start(bf16[128,512]{1,0:T(8,128)(2,1)S(1)} %pad_maximum_fusion), channel_id=1, source_target_pairs={{0,4},{1,5},{2,6},{3,7},{4,0},{5,1},{6,2},{7,3},{8,12},{9,13},{10,... | collective-permute-start | bytes 393224 | tf_op jit(solution)/shard_map/ppermute | solution.py:208
  25.5 9.5 %collective-permute-start.1 = (bf16[128,256]{1,0:T(8,128)(2,1)S(1)}, bf16[128,256]{1,0:T(8,128)(2,1)S(1)}, u32[]{:S(2)}, u32[]{:S(2)}) collective-permute-start(bf16[128,256]{1,0:T(8,128)(2,1)S(1)} %copy-done.8), channel_id=1, source_target_pairs={{0,5},{1,6},{2,7},{3,0},{4,1},{5,2},{6,3},{7,4},{8,13},{9,14},{10,... | collective-permute-start | bytes 196616 | tf_op jit(solution)/shard_map/ppermute | solution.py:208
  27.4 12.6 %collective-permute-start.2 = (bf16[128,256]{1,0:T(8,128)(2,1)S(1)}, bf16[128,256]{1,0:T(8,128)(2,1)S(1)}, u32[]{:S(2)}, u32[]{:S(2)}) collective-permute-start(bf16[128,256]{1,0:T(8,128)(2,1)S(1)} %copy-done.9), channel_id=1, source_target_pairs={{0,3},{1,4},{2,5},{3,6},{4,7},{5,0},{6,1},{7,2},{8,11},{9,12},{10,... | collective-permute-start | bytes 196616 | tf_op jit(solution)/shard_map/ppermute | solution.py:208
  35.0 5.0 %copy-start.10 = (bf16[128,256]{1,0:T(8,128)(2,1)}, bf16[128,256]{1,0:T(8,128)(2,1)S(1)}, u32[]{:S(2)}) copy-start(bf16[128,256]{1,0:T(8,128)(2,1)S(1)} %collective-permute-done.1.refs_2_) | copy-start | bytes 196612
  40.0 0.6 copy-start.11
  43.9 16.9 %copy-start.4 = (bf16[1024,256]{1,0:T(8,128)(2,1)}, bf16[1024,256]{1,0:T(8,128)(2,1)S(1)}, u32[]{:S(2)}) copy-start(bf16[1024,256]{1,0:T(8,128)(2,1)S(1)} %get-tuple-element.37.refs_5_.refs_7_) | copy-start | bytes 1572868
  43.9 16.9 %copy-start.5 = (bf16[1024,256]{1,0:T(8,128)(2,1)}, bf16[1024,256]{1,0:T(8,128)(2,1)S(1)}, u32[]{:S(2)}) copy-start(bf16[1024,256]{1,0:T(8,128)(2,1)S(1)} %get-tuple-element.36.refs_0_) | copy-start | bytes 1572868
  43.9 24.4 %collective-permute-start.3 = (bf16[1024,256]{1,0:T(8,128)(2,1)S(1)}, bf16[1024,256]{1,0:T(8,128)(2,1)S(1)}, u32[]{:S(2)}, u32[]{:S(2)}) collective-permute-start(bf16[1024,256]{1,0:T(8,128)(2,1)S(1)} %get-tuple-element.36.refs_0_), channel_id=1, source_target_pairs={{0,1},{1,2},{2,3},{3,4},{4,5},{5,6},{6,7},{7,0},{8,9},{9,10},{10,1... | collective-permute-start | bytes 1572872 | tf_op jit(solution)/shard_map/ppermute | solution.py:208
  46.9 23.4 %collective-permute-start.6 = (bf16[1024,256]{1,0:T(8,128)(2,1)S(1)}, bf16[1024,256]{1,0:T(8,128)(2,1)S(1)}, u32[]{:S(2)}, u32[]{:S(2)}) collective-permute-start(bf16[1024,256]{1,0:T(8,128)(2,1)S(1)} %get-tuple-element.37.refs_5_.refs_7_), channel_id=1, source_target_pairs={{0,7},{1,0},{2,1},{3,2},{4,3},{5,4},{6,5},{7,6},{8,15},{9,8},{10,9... | collective-permute-start | bytes 1572872 | tf_op jit(solution)/shard_map/ppermute | solution.py:208
  55.5 21.1 %collective-permute-start.9 = (bf16[1024,256]{1,0:T(8,128)(2,1)S(1)}, bf16[1024,256]{1,0:T(8,128)(2,1)}, u32[]{:S(2)}, u32[]{:S(2)}) collective-permute-start(bf16[1024,256]{1,0:T(8,128)(2,1)S(1)} %get-tuple-element.36.refs_0_), channel_id=1, source_target_pairs={{0,7},{1,0},{2,1},{3,2},{4,3},{5,4},{6,5},{7,6},{8,15},{9,8},{10,9... | collective-permute-start | bytes 1572872 | tf_op jit(solution)/shard_map/ppermute | solution.py:208
  58.9 23.1 %collective-permute-start.11 = (bf16[1024,256]{1,0:T(8,128)(2,1)S(1)}, bf16[1024,256]{1,0:T(8,128)(2,1)}, u32[]{:S(2)}, u32[]{:S(2)}) collective-permute-start(bf16[1024,256]{1,0:T(8,128)(2,1)S(1)} %get-tuple-element.37.refs_5_.refs_7_), channel_id=1, source_target_pairs={{0,1},{1,2},{2,3},{3,4},{4,5},{5,6},{6,7},{7,0},{8,9},{9,10},{10,1... | collective-permute-start | bytes 1572872 | tf_op jit(solution)/shard_map/ppermute | solution.py:208
  60.8 57.1 %all-to-all-start.1 = ((bf16[64,16,1024]{2,1,0:T(8,128)(2,1)}), bf16[64,16,1024]{2,1,0:T(8,128)(2,1)}, u32[]{:S(2)}, u32[]{:S(2)}) async-start(bf16[64,16,1024]{2,1,0:T(8,128)(2,1)} %bitcast.46), calls=%async_computation.1 | async-start | bytes 4194304 | tf_op jit(solution)/shard_map/all_to_all | solution.py:212
  68.3 20.8 %copy-start.12 = (bf16[1024,256]{1,0:T(8,128)(2,1)}, bf16[1024,256]{1,0:T(8,128)(2,1)S(1)}, u32[]{:S(2)}) copy-start(bf16[1024,256]{1,0:T(8,128)(2,1)S(1)} %collective-permute-done.3.refs_1_) | copy-start | bytes 1572868
  68.4 18.9 %collective-permute-start.4 = (bf16[1024,256]{1,0:T(8,128)(2,1)S(1)}, bf16[1024,256]{1,0:T(8,128)(2,1)}, u32[]{:S(2)}, u32[]{:S(2)}) collective-permute-start(bf16[1024,256]{1,0:T(8,128)(2,1)S(1)} %collective-permute-done.3.refs_1_), channel_id=1, source_target_pairs={{0,1},{1,2},{2,3},{3,4},{4,5},{5,6},{6,7},{7,0},{8,9},{9,10},{10,1... | collective-permute-start | bytes 1572872 | tf_op jit(solution)/shard_map/ppermute | solution.py:208
  70.3 18.9 %copy-start.13 = (bf16[1024,256]{1,0:T(8,128)(2,1)}, bf16[1024,256]{1,0:T(8,128)(2,1)S(1)}, u32[]{:S(2)}) copy-start(bf16[1024,256]{1,0:T(8,128)(2,1)S(1)} %collective-permute-done.6.refs_7_.refs_9_) | copy-start | bytes 1572868
  70.3 18.9 %collective-permute-start.7 = (bf16[1024,256]{1,0:T(8,128)(2,1)S(1)}, bf16[1024,256]{1,0:T(8,128)(2,1)}, u32[]{:S(2)}, u32[]{:S(2)}) collective-permute-start(bf16[1024,256]{1,0:T(8,128)(2,1)S(1)} %collective-permute-done.6.refs_7_.refs_9_), channel_id=1, source_target_pairs={{0,7},{1,0},{2,1},{3,2},{4,3},{5,4},{6,5},{7,6},{8,15},{9,8},{10,9... | collective-permute-start | bytes 1572872 | tf_op jit(solution)/shard_map/ppermute | solution.py:208
  76.6 22.6 %collective-permute-start.10 = (bf16[1024,256]{1,0:T(8,128)(2,1)}, bf16[1024,256]{1,0:T(8,128)(2,1)}, u32[]{:S(2)}, u32[]{:S(2)}) collective-permute-start(bf16[1024,256]{1,0:T(8,128)(2,1)} %collective-permute-done.9.refs_2_), channel_id=1, source_target_pairs={{0,7},{1,0},{2,1},{3,2},{4,3},{5,4},{6,5},{7,6},{8,15},{9,8},{10,9... | collective-permute-start | bytes 1572872 | tf_op jit(solution)/shard_map/ppermute | solution.py:208
  82.0 17.1 %collective-permute-start.12 = (bf16[1024,256]{1,0:T(8,128)(2,1)}, bf16[1024,256]{1,0:T(8,128)(2,1)S(1)}, u32[]{:S(2)}, u32[]{:S(2)}) collective-permute-start(bf16[1024,256]{1,0:T(8,128)(2,1)} %collective-permute-done.11.refs_6_.refs_8_), channel_id=1, source_target_pairs={{0,1},{1,2},{2,3},{3,4},{4,5},{5,6},{6,7},{7,0},{8,9},{9,10},{10,1... | collective-permute-start | bytes 1572872 | tf_op jit(solution)/shard_map/ppermute | solution.py:208
  87.2 19.4 %collective-permute-start.5 = (bf16[1024,256]{1,0:T(8,128)(2,1)}, bf16[1024,256]{1,0:T(8,128)(2,1)S(1)}, u32[]{:S(2)}, u32[]{:S(2)}) collective-permute-start(bf16[1024,256]{1,0:T(8,128)(2,1)} %collective-permute-done.4.refs_3_), channel_id=1, source_target_pairs={{0,1},{1,2},{2,3},{3,4},{4,5},{5,6},{6,7},{7,0},{8,9},{9,10},{10,1... | collective-permute-start | bytes 1572872 | tf_op jit(solution)/shard_map/ppermute | solution.py:208
  89.2 21.2 %collective-permute-start.8 = (bf16[1024,256]{1,0:T(8,128)(2,1)}, bf16[1024,256]{1,0:T(8,128)(2,1)S(1)}, u32[]{:S(2)}, u32[]{:S(2)}) collective-permute-start(bf16[1024,256]{1,0:T(8,128)(2,1)} %collective-permute-done.7.refs_9_.refs_11_), channel_id=1, source_target_pairs={{0,7},{1,0},{2,1},{3,2},{4,3},{5,4},{6,5},{7,6},{8,15},{9,8},{10,9... | collective-permute-start | bytes 1572872 | tf_op jit(solution)/shard_map/ppermute | solution.py:208
  99.2 0.8 copy-start.14
  106.6 3.8 %copy-start.6 = (bf16[1024,256]{1,0:T(8,128)(2,1)}, bf16[1024,256]{1,0:T(8,128)(2,1)S(1)}, u32[]{:S(2)}) copy-start(bf16[1024,256]{1,0:T(8,128)(2,1)S(1)} %collective-permute-done.5.refs_0_.refs_5_) | copy-start | bytes 1572868
  110.4 0.8 copy-start.7
  124.3 7.4 %copy-start = (bf16[1,176,2048]{2,1,0:T(8,128)(2,1)S(1)}, bf16[1,176,2048]{2,1,0:T(8,128)(2,1)}, u32[]{:S(2)}) copy-start(bf16[1,176,2048]{2,1,0:T(8,128)(2,1)} %param.11) | copy-start | bytes 2162692
  124.3 7.4 %copy-start.1 = (bf16[1,176,2048]{2,1,0:T(8,128)(2,1)S(1)}, bf16[1,176,2048]{2,1,0:T(8,128)(2,1)}, u32[]{:S(2)}) copy-start(bf16[1,176,2048]{2,1,0:T(8,128)(2,1)} %param.12) | copy-start | bytes 2162692
  124.3 7.4 %copy-start.2 = (bf16[352,1024]{1,0:T(8,128)(2,1)S(1)}, bf16[352,1024]{1,0:T(8,128)(2,1)}, u32[]{:S(2)}) copy-start(bf16[352,1024]{1,0:T(8,128)(2,1)} %get-tuple-element.44.refs_13_) | copy-start | bytes 2162692
  124.3 47.8 %all-to-all-start.3 = ((bf16[64,16,768]{2,1,0:T(8,128)(2,1)}), bf16[64,16,768]{2,1,0:T(8,128)(2,1)}, u32[]{:S(2)}, u32[]{:S(2)}) async-start(bf16[64,16,768]{2,1,0:T(8,128)(2,1)} %bitcast.48), calls=%async_computation.3 | async-start | bytes 3145728 | tf_op jit(solution)/shard_map/all_to_all | solution.py:212
  132.2 15.9 %collective-permute-start.15 = (bf16[1024,256]{1,0:T(8,128)(2,1)S(1)}, bf16[1024,256]{1,0:T(8,128)(2,1)S(1)}, u32[]{:S(2)}, u32[]{:S(2)}) collective-permute-start(bf16[1024,256]{1,0:T(8,128)(2,1)S(1)} %convolution_convert_fusion.1), channel_id=1, source_target_pairs={{0,7},{1,0},{2,1},{3,2},{4,3},{5,4},{6,5},{7,6},{8,15},{9,8},{10,9... | collective-permute-start | bytes 1572872 | tf_op jit(solution)/shard_map/ppermute | solution.py:208
  137.8 15.9 %collective-permute-start.13 = (bf16[1024,256]{1,0:T(8,128)(2,1)S(1)}, bf16[1024,256]{1,0:T(8,128)(2,1)S(1)}, u32[]{:S(2)}, u32[]{:S(2)}) collective-permute-start(bf16[1024,256]{1,0:T(8,128)(2,1)S(1)} %convolution_convert_fusion.3), channel_id=1, source_target_pairs={{0,1},{1,2},{2,3},{3,4},{4,5},{5,6},{6,7},{7,0},{8,9},{9,10},{10,1... | collective-permute-start | bytes 1572872 | tf_op jit(solution)/shard_map/ppermute | solution.py:208
  148.2 15.9 %collective-permute-start.16 = (bf16[1024,256]{1,0:T(8,128)(2,1)S(1)}, bf16[1024,256]{1,0:T(8,128)(2,1)}, u32[]{:S(2)}, u32[]{:S(2)}) collective-permute-start(bf16[1024,256]{1,0:T(8,128)(2,1)S(1)} %add_convert_fusion.1), channel_id=1, source_target_pairs={{0,7},{1,0},{2,1},{3,2},{4,3},{5,4},{6,5},{7,6},{8,15},{9,8},{10,9... | collective-permute-start | bytes 1572872 | tf_op jit(solution)/shard_map/ppermute | solution.py:208
  154.6 15.2 %collective-permute-start.14 = (bf16[1024,256]{1,0:T(8,128)(2,1)}, bf16[1024,256]{1,0:T(8,128)(2,1)}, u32[]{:S(2)}, u32[]{:S(2)}) collective-permute-start(bf16[1024,256]{1,0:T(8,128)(2,1)} %add_convert_fusion.2), channel_id=1, source_target_pairs={{0,1},{1,2},{2,3},{3,4},{4,5},{5,6},{6,7},{7,0},{8,9},{9,10},{10,1... | collective-permute-start | bytes 1572872 | tf_op jit(solution)/shard_map/ppermute | solution.py:208
  164.1 20.6 %copy-start.3 = (bf16[1024,128]{1,0:T(8,128)(2,1)S(1)}, bf16[1024,128]{1,0:T(8,128)(2,1)}, u32[]{:S(2)}) copy-start(bf16[1024,128]{1,0:T(8,128)(2,1)} %get-tuple-element.29) | copy-start | bytes 786436
  172.1 30.3 %all-to-all-start.2 = ((bf16[64,16,256]{2,1,0:T(8,128)(2,1)}), bf16[64,16,256]{2,1,0:T(8,128)(2,1)S(1)}, u32[]{:S(2)}, u32[]{:S(2)}) async-start(bf16[64,16,256]{2,1,0:T(8,128)(2,1)} %bitcast.10), calls=%async_computation.2 | async-start | bytes 1048576 | tf_op jit(solution)/shard_map/all_to_all | solution.py:212
  186.5 15.9 %collective-permute-start.19 = (bf16[128,256]{1,0:T(8,128)(2,1)S(1)}, bf16[128,256]{1,0:T(8,128)(2,1)S(1)}, u32[]{:S(2)}, u32[]{:S(2)}) collective-permute-start(bf16[128,256]{1,0:T(8,128)(2,1)S(1)} %get-tuple-element.57), channel_id=1, source_target_pairs={{0,5},{1,6},{2,7},{3,0},{4,1},{5,2},{6,3},{7,4},{8,13},{9,14},{10,... | collective-permute-start | bytes 196616 | tf_op jit(solution)/shard_map/ppermute | solution.py:208
  188.7 13.7 %collective-permute-start.18 = (bf16[128,256]{1,0:T(8,128)(2,1)S(1)}, bf16[128,256]{1,0:T(8,128)(2,1)S(1)}, u32[]{:S(2)}, u32[]{:S(2)}) collective-permute-start(bf16[128,256]{1,0:T(8,128)(2,1)S(1)} %get-tuple-element.58), channel_id=1, source_target_pairs={{0,3},{1,4},{2,5},{3,6},{4,7},{5,0},{6,1},{7,2},{8,11},{9,12},{10,... | collective-permute-start | bytes 196616 | tf_op jit(solution)/shard_map/ppermute | solution.py:208
  193.6 10.5 %collective-permute-start.17 = (bf16[128,256]{1,0:T(8,128)(2,1)S(1)}, bf16[128,256]{1,0:T(8,128)(2,1)S(1)}, u32[]{:S(2)}, u32[]{:S(2)}) collective-permute-start(bf16[128,256]{1,0:T(8,128)(2,1)S(1)} %get-tuple-element.56), channel_id=1, source_target_pairs={{0,4},{1,5},{2,6},{3,7},{4,0},{5,1},{6,2},{7,3},{8,12},{9,13},{10,... | collective-permute-start | bytes 196616 | tf_op jit(solution)/shard_map/ppermute | solution.py:208
